TPU v7x, 32 devices: a whole 2x2x4 slice. The times are simulated.
32 devices in a mesh: dp: 2 (over x), ctx: 4 (over y, core), tp: 4 (over z).
Axes of the slice: x: 2, y: 2, z: 4, core: 2. Of those that a mesh axis runs over, the one named last changes fastest.
Arguments:
- block_in: bfloat16 [2, 4096, 768], P('dp', 'ctx'), may hold values from -6 to 6
- out_grad: bfloat16 [2, 4096, 768], P('dp', 'ctx'), may hold values from -6 to 6
- parents: int32 [2, 16], P('dp'), may hold values from -1 to 7, as said below
- mixer_gain: float32 [768], replicated, may hold values from 0.5 to 1.5
- mixer_shift: float32 [768], replicated, may hold values from -1.75 to 1.75
- in_proj: bfloat16 [768, 3, 768], P('dp', None, 'tp'), may hold values from -0.21875 to 0.21875
- in_bias: float32 [3, 768], P(None, 'tp'), may hold values from -3 to 3
- short_weight: float32 [3, 3, 768], P(None, None, 'tp'), may hold values from -3.5 to 3.5
- short_bias: float32 [3, 768], P(None, 'tp'), may hold values from -1.75 to 1.75
- filter_one: float32 [33, 64], replicated, may hold values from -1 to 1
- filter_one_bias: float32 [64], replicated, may hold values from -6 to 6
- filter_two: float32 [64, 64], replicated, may hold values from -0.75 to 0.75
- filter_two_bias: float32 [64], replicated, may hold values from -6 to 6
- filter_freq: float32 [64], replicated, may hold values from 1.5 to 2
- filter_out: bfloat16 [64, 768], P('dp', 'tp'), may hold values from -0.1875 to 0.1875
- skip_gain: float32 [768], P('tp'), may hold values from -6 to 6
- out_proj: bfloat16 [768, 768], P('tp', 'dp'), may hold values from -0.21875 to 0.21875
- out_bias: float32 [768], replicated, may hold values from -1.75 to 1.75
- feed_gain: float32 [768], replicated, may hold values from 0.5 to 1.5
- feed_shift: float32 [768], replicated, may hold values from -1.75 to 1.75
- feed_up: bfloat16 [768, 3072], P('dp', 'tp'), may hold values from -0.21875 to 0.21875
- feed_up_bias: float32 [3072], P('tp'), may hold values from -1.75 to 1.75
- feed_down: bfloat16 [3072, 768], P('tp', 'dp'), may hold values from -0.109375 to 0.109375
- feed_down_bias: float32 [768], replicated, may hold values from -1.75 to 1.75
Outputs:
- block_out: float32 [2, 4096, 768], P('dp', 'ctx')
- grad_block_in: float32 [2, 4096, 768], P('dp', 'ctx')
- grad_mixer_gain: float32 [768], replicated
- grad_mixer_shift: float32 [768], replicated
- grad_in_proj: float32 [768, 3, 768], P('dp', None, 'tp')
- grad_in_bias: float32 [3, 768], P(None, 'tp')
- grad_short_weight: float32 [3, 3, 768], P(None, None, 'tp')
- grad_short_bias: float32 [3, 768], P(None, 'tp')
- grad_filter_one: float32 [33, 64], replicated
- grad_filter_one_bias: float32 [64], replicated
- grad_filter_two: float32 [64, 64], replicated
- grad_filter_two_bias: float32 [64], replicated
- grad_filter_freq: float32 [64], replicated
- grad_filter_out: float32 [64, 768], P('dp', 'tp')
- grad_skip_gain: float32 [768], P('tp')
- grad_out_proj: float32 [768, 768], P('tp', 'dp')
- grad_out_bias: float32 [768], replicated
- grad_feed_gain: float32 [768], replicated
- grad_feed_shift: float32 [768], replicated
- grad_feed_up: float32 [768, 3072], P('dp', 'tp')
- grad_feed_up_bias: float32 [3072], P('tp')
- grad_feed_down: float32 [3072, 768], P('tp', 'dp')
- grad_feed_down_bias: float32 [768], replicated
Inputs may be any that keep to these rules, and one draw needn't show every extreme that they name: `parents`: blocks 0 to 3 form the trunk, block i having parent i - 1 (block 0 is the root, parent -1). Each of the next 4 blocks has a parent among trunk blocks 1 to 3. Each of the last 8 blocks has a parent among those 4 branch blocks; the last block's parent is block 7.
All inputs are finite; a program needn't handle non-finite values.
Results may differ from a plain program's by a relative error of at most 0.009.
Values may be sent and summed in bfloat16 or wider, within the bound.
A program may use at most 128 MiB of HBM per device.

v0:
```python
import math

import jax
import jax.numpy as jnp
from jax import lax
from jax.sharding import PartitionSpec as P

SEG = 256
DEPTH = 6


EXACT = lax.Precision.HIGHEST
TRIPLE = lax.Precision.HIGH
EPSILON = 1e-05
SLOW_RATE = -math.log(0.01) / 1.5
FAST_RATE = -math.log(0.01) / 0.3
SHIFT_FLOOR = 0.05


def layer_norm(inputs, gain, shift):
    mean_value = jnp.mean(inputs, axis=-1, keepdims=True)
    centered = inputs - mean_value
    variance = jnp.mean(centered * centered, axis=-1, keepdims=True)
    return centered * lax.rsqrt(variance + EPSILON) * gain + shift


def gelu_exact(values):
    return jax.nn.gelu(values, approximate=False)


def implicit_filter(
    first_weight,
    first_bias,
    second_weight,
    second_bias,
    frequency,
    last_weight,
    length,
    channel_first,
    width_all,
):
    positions = jnp.arange(length, dtype=jnp.float32)
    time_pos = positions / (length - 1)
    bands = (first_weight.shape[0] - 1) // 2
    band_freq = jnp.linspace(0.0001, bands - 1, bands, dtype=jnp.float32)
    angles = 2.0 * math.pi / length * positions
    phases = angles[:, None] * band_freq[None, :]
    embedding = jnp.concatenate([time_pos[:, None], jnp.cos(phases), -jnp.sin(phases)], axis=1)
    hidden = jnp.sin(frequency * (jnp.dot(embedding, first_weight, precision=EXACT) + first_bias))
    hidden = jnp.sin(frequency * (jnp.dot(hidden, second_weight, precision=EXACT) + second_bias))
    raw_taps = jnp.dot(hidden, last_weight, precision=EXACT)
    channel_ids = (channel_first + jnp.arange(last_weight.shape[1])).astype(jnp.float32)
    decay_rate = SLOW_RATE + (FAST_RATE - SLOW_RATE) * channel_ids / (width_all - 1)
    envelope = jnp.exp(-time_pos[:, None] * decay_rate[None, :])
    return raw_taps * (envelope + SHIFT_FLOOR)


def tree_tables(parent_row):
    block_count = parent_row.shape[0]
    block_ids = jnp.arange(block_count, dtype=jnp.int32)
    parent_map = (parent_row[:, None] == block_ids[None, :]).astype(jnp.float32)
    identity = jnp.eye(block_count, dtype=jnp.float32)

    def extend(unused_step, current):
        return identity + jnp.dot(parent_map, current, precision=EXACT)

    ancestor = lax.fori_loop(0, block_count, extend, identity)
    depths = jnp.sum(ancestor, axis=1)
    return (parent_map, ancestor, depths[:, None] - depths[None, :])


def short_conv(parent_tail, projected, weight, shift):
    extended = jnp.concatenate([parent_tail, projected], axis=1)
    return (
        weight[:, 0] * extended[:, :-2]
        + weight[:, 1] * extended[:, 1:-1]
        + weight[:, 2] * extended[:, 2:]
        + shift
    )


def spectral_tables(block_len):
    spec_len = 2 * block_len
    freq_ids = jnp.arange(spec_len, dtype=jnp.int32)[:, None]
    place_ids = jnp.arange(block_len, dtype=jnp.int32)[None, :]
    unit_angle = 2.0 * math.pi / spec_len
    ahead_angle = (freq_ids * place_ids % spec_len).astype(jnp.float32) * unit_angle
    behind = (freq_ids * (place_ids + block_len) % spec_len).astype(jnp.float32) * unit_angle
    keep_mask = (place_ids > 0).astype(jnp.float32)
    forward_table = jnp.stack([jnp.cos(ahead_angle), -jnp.sin(ahead_angle)])
    lower_table = jnp.stack([jnp.cos(behind) * keep_mask, -jnp.sin(behind) * keep_mask])
    return (forward_table, lower_table)


def spec_mul(first_spec, second_spec):
    real_part = (
        first_spec[..., 0, :, :] * second_spec[..., 0, :, :]
        - first_spec[..., 1, :, :] * second_spec[..., 1, :, :]
    )
    imag_part = (
        first_spec[..., 0, :, :] * second_spec[..., 1, :, :]
        + first_spec[..., 1, :, :] * second_spec[..., 0, :, :]
    )
    return jnp.stack([real_part, imag_part], axis=-3)


def spec_conj_mul(first_spec, second_spec):
    real_part = (
        first_spec[..., 0, :, :] * second_spec[..., 0, :, :]
        + first_spec[..., 1, :, :] * second_spec[..., 1, :, :]
    )
    imag_part = (
        first_spec[..., 0, :, :] * second_spec[..., 1, :, :]
        - first_spec[..., 1, :, :] * second_spec[..., 0, :, :]
    )
    return jnp.stack([real_part, imag_part], axis=-3)


def keep_same(unchanged):
    return unchanged


def over_tp(partial_sum):
    return lax.psum(partial_sum, "tp")


def body(
    block_in,
    out_grad,
    parents,
    mixer_gain,
    mixer_shift,
    in_proj,
    in_bias,
    short_weight,
    short_bias,
    filter_one,
    filter_one_bias,
    filter_two,
    filter_two_bias,
    filter_freq,
    filter_out,
    skip_gain,
    out_proj,
    out_bias,
    feed_gain,
    feed_shift,
    feed_up,
    feed_up_bias,
    feed_down,
    feed_down_bias,
):
    inputs = block_in[0].astype(jnp.float32)
    total_rows, model_width = inputs.shape
    channels = skip_gain.shape[0]
    block_len = SEG
    blocks = total_rows // block_len
    spec_len = 2 * block_len
    tp_count = lax.axis_size("tp")
    tp_index = lax.axis_index("tp")
    first_index = lax.axis_index("ctx") * blocks
    in_all, out_all, up_all, down_all, last_all = (
        lax.all_gather(in_proj, "dp", axis=0, tiled=True),
        lax.all_gather(out_proj, "dp", axis=1, tiled=True),
        lax.all_gather(feed_up, "dp", axis=0, tiled=True),
        lax.all_gather(feed_down, "dp", axis=1, tiled=True),
        lax.all_gather(filter_out, "dp", axis=0, tiled=True),
    )
    in_flat = in_all.reshape(model_width, 3 * channels)
    parent_map, ancestor, depth_gap = tree_tables(parents[0])
    local_parent = lax.dynamic_slice_in_dim(parent_map, first_index, blocks, 0)
    dest_anc = lax.dynamic_slice_in_dim(ancestor, first_index, blocks, 0)
    dest_gap = lax.dynamic_slice_in_dim(depth_gap, first_index, blocks, 0)
    source_anc = lax.dynamic_slice_in_dim(ancestor, first_index, blocks, 1)
    source_gap = lax.dynamic_slice_in_dim(depth_gap, first_index, blocks, 1)
    mixer_normed, mixer_back = jax.vjp(layer_norm, inputs, mixer_gain, mixer_shift)
    mixer_low = mixer_normed.astype(jnp.bfloat16)
    projected = (
        jnp.dot(mixer_low, in_flat, preferred_element_type=jnp.float32).reshape(
            total_rows, 3, channels
        )
        + in_bias
    ).reshape(blocks, block_len, 3, channels)
    tail_rows = lax.all_gather(projected[:, block_len - 2 :], "ctx", axis=0, tiled=True)
    parent_tail = jnp.einsum("sb,bkgc->skgc", local_parent, tail_rows, precision=EXACT)
    mixed_in, short_back = jax.vjp(short_conv, parent_tail, projected, short_weight, short_bias)
    gate_zero = mixed_in[:, :, 0]
    gate_one = mixed_in[:, :, 1]
    values = mixed_in[:, :, 2]
    carried = (values * gate_one).astype(jnp.bfloat16)
    carried_wide = carried.astype(jnp.float32)
    forward_table, lower_table = spectral_tables(block_len)

    def make_taps(first_weight, first_bias, second_weight, second_bias, frequency, last_weight):
        return implicit_filter(
            first_weight,
            first_bias,
            second_weight,
            second_bias,
            frequency,
            last_weight,
            DEPTH * block_len,
            tp_index * channels,
            channels * tp_count,
        )

    filter_taps, taps_back = jax.vjp(
        make_taps,
        filter_one,
        filter_one_bias,
        filter_two,
        filter_two_bias,
        filter_freq,
        last_all.astype(jnp.float32),
    )
    padded_taps = jnp.concatenate(
        [jnp.zeros((block_len, channels), jnp.float32), filter_taps], axis=0
    ).reshape(DEPTH + 1, block_len, channels)
    spectra = jnp.einsum(
        "rfj,djc->drfc", lower_table, padded_taps[:-1], precision=EXACT
    ) + jnp.einsum("rfj,djc->drfc", forward_table, padded_taps[1:], precision=EXACT)
    incoming = lax.all_gather(carried, "ctx", axis=0, tiled=True)

    def accumulate(current):
        source_spec = jnp.einsum(
            "rfn,anc->arfc", forward_table, incoming.astype(jnp.float32), precision=TRIPLE
        )
        for distance in range(DEPTH):
            selector = dest_anc * (dest_gap == distance)
            combined = jnp.einsum("sa,arfc->srfc", selector, source_spec, precision=EXACT)
            current = current + spec_mul(spectra[distance], combined)
        return current

    spec_out = lax.cond(
        jnp.sum(dest_anc) > 0,
        accumulate,
        keep_same,
        jnp.zeros((blocks, 2, spec_len, channels), jnp.float32),
    )
    long_out = jnp.einsum("rfn,srfc->snc", forward_table, spec_out, precision=EXACT) / spec_len
    convolved = long_out + skip_gain * carried_wide
    gated = (convolved * gate_zero).reshape(total_rows, channels).astype(jnp.bfloat16)
    mix_part = jnp.dot(gated, out_all, preferred_element_type=jnp.float32)
    residual = inputs + over_tp(mix_part) + out_bias
    feed_normed, feed_back = jax.vjp(layer_norm, residual, feed_gain, feed_shift)
    feed_low = feed_normed.astype(jnp.bfloat16)
    pre_act = jnp.dot(feed_low, up_all, preferred_element_type=jnp.float32) + feed_up_bias
    hidden_act, gelu_back = jax.vjp(gelu_exact, pre_act)
    hidden_low = hidden_act.astype(jnp.bfloat16)
    down_part = jnp.dot(hidden_low, down_all, preferred_element_type=jnp.float32)
    result = residual + over_tp(down_part) + feed_down_bias
    grad_low = out_grad[0]
    grad_down_bias = jnp.sum(grad_low.astype(jnp.float32), axis=0)
    grad_down = jnp.einsum("rh,rd->hd", hidden_low, grad_low, preferred_element_type=jnp.float32)
    grad_hidden = jnp.einsum("rd,hd->rh", grad_low, down_all, preferred_element_type=jnp.float32)
    grad_pre = gelu_back(grad_hidden)[0].astype(jnp.bfloat16)
    grad_up_bias = jnp.sum(grad_pre.astype(jnp.float32), axis=0)
    grad_up = jnp.einsum("rd,rh->dh", feed_low, grad_pre, preferred_element_type=jnp.float32)
    norm_part = jnp.einsum("rh,dh->rd", grad_pre, up_all, preferred_element_type=jnp.float32)
    leader = (tp_index == 0).astype(jnp.float32)
    grad_resid_norm, grad_feed_gain, grad_feed_shift = feed_back(over_tp(norm_part))
    grad_residual = grad_low.astype(jnp.float32) + grad_resid_norm
    grad_mix = grad_residual.astype(jnp.bfloat16)
    grad_out_bias = jnp.sum(grad_mix.astype(jnp.float32), axis=0)
    grad_out_proj = jnp.einsum("rc,rd->cd", gated, grad_mix, preferred_element_type=jnp.float32)
    grad_gated = jnp.einsum(
        "rd,cd->rc", grad_mix, out_all, preferred_element_type=jnp.float32
    ).reshape(blocks, block_len, channels)
    grad_conv = grad_gated * gate_zero
    grad_zero = grad_gated * convolved
    grad_skip = jnp.sum(grad_conv * carried_wide, axis=(0, 1))
    grad_long = grad_conv.astype(jnp.bfloat16)
    own_spec = jnp.einsum("rfn,anc->arfc", forward_table, carried_wide, precision=TRIPLE)
    start_state = (
        jnp.zeros((blocks, 2, spec_len, channels), jnp.float32),
        jnp.zeros((DEPTH, 2, spec_len, channels), jnp.float32),
    )
    add_incoming = lax.all_gather(grad_long, "ctx", axis=0, tiled=True)

    def accumulate(current):
        grad_source, grad_spectra = current
        target_spec = (
            jnp.einsum(
                "rfn,snc->srfc", forward_table, add_incoming.astype(jnp.float32), precision=TRIPLE
            )
            / spec_len
        )
        for distance in range(DEPTH):
            selector = source_anc * (source_gap == distance)
            collected = jnp.einsum("sa,srfc->arfc", selector, target_spec, precision=EXACT)
            grad_source = grad_source + spec_conj_mul(spectra[distance], collected)
            grad_spectra = grad_spectra.at[distance].add(
                jnp.sum(spec_conj_mul(own_spec, collected), axis=0)
            )
        return (grad_source, grad_spectra)

    grad_source, grad_spectra = lax.cond(
        jnp.sum(source_anc) > 0, accumulate, keep_same, start_state
    )
    grad_carried = (
        jnp.einsum("rfn,arfc->anc", forward_table, grad_source, precision=EXACT)
        + skip_gain * grad_conv
    )
    grad_mixed = jnp.stack([grad_zero, grad_carried * values, grad_carried * gate_one], axis=2)
    grad_tail, grad_proj, grad_short_weight, grad_short_bias = short_back(grad_mixed)
    to_parent = jnp.einsum("sb,skgc->bkgc", local_parent, grad_tail, precision=EXACT)
    from_child = lax.psum_scatter(to_parent, "ctx", scatter_dimension=0, tiled=True)
    grad_proj = grad_proj.at[:, block_len - 2 :].add(from_child)
    grad_proj_low = grad_proj.reshape(total_rows, 3 * channels).astype(jnp.bfloat16)
    grad_in_bias = jnp.sum(grad_proj_low.astype(jnp.float32), axis=0).reshape(3, channels)
    grad_in_proj = jnp.einsum(
        "rd,rk->dk", mixer_low, grad_proj_low, preferred_element_type=jnp.float32
    ).reshape(model_width, 3, channels)
    proj_part = jnp.einsum("rk,dk->rd", grad_proj_low, in_flat, preferred_element_type=jnp.float32)
    grad_input_norm, grad_mixer_gain, grad_mixer_shift = mixer_back(over_tp(proj_part))
    grad_inputs = grad_residual + grad_input_norm
    upper_part = jnp.einsum("rfj,drfc->djc", forward_table, grad_spectra, precision=EXACT)
    lower_part = jnp.einsum("rfj,drfc->djc", lower_table, grad_spectra, precision=EXACT)
    grad_taps = upper_part + jnp.concatenate(
        [lower_part[1:], jnp.zeros((1, block_len, channels), jnp.float32)], axis=0
    )
    grad_first, grad_first_bias, grad_second, grad_second_bias, grad_freq, grad_last = taps_back(
        grad_taps.reshape(DEPTH * block_len, channels)
    )
    matrix_grads = (grad_in_proj, grad_out_proj, grad_up, grad_down, grad_last)
    summed_grads = lax.psum(
        (matrix_grads[0], matrix_grads[1], matrix_grads[2], matrix_grads[3], matrix_grads[4]), "ctx"
    )
    owned = (
        lax.psum_scatter(summed_grads[0], "dp", scatter_dimension=0, tiled=True),
        lax.psum_scatter(summed_grads[1], "dp", scatter_dimension=1, tiled=True),
        lax.psum_scatter(summed_grads[2], "dp", scatter_dimension=0, tiled=True),
        lax.psum_scatter(summed_grads[3], "dp", scatter_dimension=1, tiled=True),
        lax.psum_scatter(summed_grads[4], "dp", scatter_dimension=0, tiled=True),
    )

    def widen(piece_grad, axis_num):
        full_shape = list(piece_grad.shape)
        full_shape[axis_num] = piece_grad.shape[axis_num] * tp_count
        return lax.dynamic_update_slice_in_dim(
            jnp.zeros(full_shape, jnp.float32),
            piece_grad,
            tp_index * piece_grad.shape[axis_num],
            axis_num,
        )

    def narrow(whole_grad, axis_num):
        width_here = whole_grad.shape[axis_num] // tp_count
        return lax.dynamic_slice_in_dim(whole_grad, tp_index * width_here, width_here, axis_num)

    vector_grads = lax.psum(
        (
            leader * grad_mixer_gain,
            leader * grad_mixer_shift,
            leader * grad_feed_gain,
            leader * grad_feed_shift,
            leader * grad_out_bias,
            leader * grad_down_bias,
            widen(grad_in_bias, 1),
            widen(grad_short_weight, 2),
            widen(grad_short_bias, 1),
            widen(grad_skip, 0),
            widen(grad_up_bias, 0),
            grad_first,
            grad_first_bias,
            grad_second,
            grad_second_bias,
            grad_freq,
        ),
        ("dp", "ctx", "tp"),
    )
    return (
        result[None],
        grad_inputs[None],
        vector_grads[0],
        vector_grads[1],
        owned[0],
        narrow(vector_grads[6], 1),
        narrow(vector_grads[7], 2),
        narrow(vector_grads[8], 1),
        vector_grads[11],
        vector_grads[12],
        vector_grads[13],
        vector_grads[14],
        vector_grads[15],
        owned[4],
        narrow(vector_grads[9], 0),
        owned[1],
        vector_grads[4],
        vector_grads[2],
        vector_grads[3],
        owned[2],
        narrow(vector_grads[10], 0),
        owned[3],
        vector_grads[5],
    )


def solution(mesh):
    in_specs = (
        P("dp", "ctx", None),
        P("dp", "ctx", None),
        P("dp", None),
        P(),
        P(),
        P("dp", None, "tp"),
        P(None, "tp"),
        P(None, None, "tp"),
        P(None, "tp"),
        P(),
        P(),
        P(),
        P(),
        P(),
        P("dp", "tp"),
        P("tp"),
        P("tp", "dp"),
        P(),
        P(),
        P(),
        P("dp", "tp"),
        P("tp"),
        P("tp", "dp"),
        P(),
    )
    out_specs = (
        P("dp", "ctx", None),
        P("dp", "ctx", None),
        P(),
        P(),
        P("dp", None, "tp"),
        P(None, "tp"),
        P(None, None, "tp"),
        P(None, "tp"),
        P(),
        P(),
        P(),
        P(),
        P(),
        P("dp", "tp"),
        P("tp"),
        P("tp", "dp"),
        P(),
        P(),
        P(),
        P("dp", "tp"),
        P("tp"),
        P("tp", "dp"),
        P(),
    )
    return jax.shard_map(body, mesh=mesh, in_specs=in_specs, out_specs=out_specs, check_vma=False)
```

profile of v0, /device:TPU:0, one launch (start us, length us, event | category | flops | bytes accessed | tf_op | source)
XLA Modules:
  0.0 1171.8 jit_solution(9063578912354617219)
XLA Ops:
  12.6 13.8 %all_gather.25 = bf16[768,3,192]{0,2,1:T(8,128)(2,1)S(1)} all-gather(bf16[384,3,192]{0,2,1:T(8,128)(2,1)S(1)} %copy-done.79), channel_id=1, replica_groups=mesh['dp'=2,'ctx'=4,'tp'=4] {'dp'}, dimensions={0}, use_global_device_ids=true | all-gather | bytes 1327104 | tf_op jit(solution)/shard_map/all_gather | solution.py:163
  30.1 3.8 reshape.805
  37.6 5.3 all_gather.26
  44.8 5.0 add_add_fusion.2
  55.8 4.9 all_gather.24
  76.4 6.2 all_gather.28
  88.1 4.4 fusion.164
  92.6 6.1 add_bitcast_fusion
  98.7 93.9 %conditional.2 = (f32[4,2,512,192]{2,3,1,0:T(8,128)}) conditional(s32[]{:T(128)} %convert_element_type.161, () %tuple.59, (f32[6,2,512,192]{2,3,1,0:T(8,128)}, f32[16,16]{0,1:T(8,128)S(1)}, s32[]{:T(128)}, f32[4,16]{1,0:T(4,128)S(1)}, bf16[16,256,192]{1,2,0:T(8,128)(2,1)}, /*index=5*/f32[2,512,256]{2,1,0:T(8,128)}) %tuple.60), branch_computations={%region_6.7_spmd, %region_7.8_spmd} | conditional | flops 5760614400 | bytes 219179264 | solution.py:234
  98.9 4.2 slice_bitcast_fusion.1
  103.1 3.5 convolution_bitcast_fusion
  106.7 11.8 %fusion.12 = f32[4,2,512,192]{2,0,3,1:T(4,128)S(1)} fusion(f32[16,2,512,192]{2,3,1,0:T(8,128)S(1)} %convolution_bitcast_fusion, f32[4,16]{1,0:T(4,128)S(1)} %get-tuple-element.167, f32[16,16]{1,0:T(8,128)S(1)} %copy.135, s32[]{:T(128)} %get-tuple-element.166), kind=kOutput, calls=%fused_computation.10 | convolution fusion | flops 150995072 | bytes 15732740 | tf_op jit(solution)/shard_map/cond/branch_1_fun/sa,arfc->srfc/dot_general | solution.py:230
  118.4 12.0 %fusion.10 = f32[4,2,512,192]{2,0,3,1:T(4,128)S(1)} fusion(f32[16,2,512,192]{2,3,1,0:T(8,128)S(1)} %convolution_bitcast_fusion, f32[4,16]{1,0:T(4,128)S(1)} %get-tuple-element.167, f32[16,16]{1,0:T(8,128)S(1)} %copy.135, s32[]{:T(128)} %get-tuple-element.166), kind=kOutput, calls=%fused_computation.8 | convolution fusion | flops 150995072 | bytes 15732740 | tf_op jit(solution)/shard_map/cond/branch_1_fun/sa,arfc->srfc/dot_general | solution.py:230
  130.4 12.2 %fusion.8 = f32[4,2,512,192]{2,0,3,1:T(4,128)S(1)} fusion(f32[16,2,512,192]{2,3,1,0:T(8,128)S(1)} %convolution_bitcast_fusion, f32[4,16]{1,0:T(4,128)S(1)} %get-tuple-element.167, f32[16,16]{1,0:T(8,128)S(1)} %copy.135, s32[]{:T(128)} %get-tuple-element.166), kind=kOutput, calls=%fused_computation.6 | convolution fusion | flops 150995072 | bytes 15732740 | tf_op jit(solution)/shard_map/cond/branch_1_fun/sa,arfc->srfc/dot_general | solution.py:230
  145.5 11.9 %fusion.6 = f32[4,2,512,192]{2,0,3,1:T(4,128)S(1)} fusion(f32[16,2,512,192]{2,3,1,0:T(8,128)S(1)} %convolution_bitcast_fusion, f32[4,16]{1,0:T(4,128)S(1)} %get-tuple-element.167, f32[16,16]{1,0:T(8,128)S(1)} %copy.135, s32[]{:T(128)} %get-tuple-element.166), kind=kOutput, calls=%fused_computation.4 | convolution fusion | flops 150995072 | bytes 15732740 | tf_op jit(solution)/shard_map/cond/branch_1_fun/sa,arfc->srfc/dot_general | solution.py:230
  157.4 12.0 %fusion.4 = f32[4,2,512,192]{2,0,3,1:T(4,128)S(1)} fusion(f32[16,2,512,192]{2,3,1,0:T(8,128)S(1)} %convolution_bitcast_fusion, f32[4,16]{1,0:T(4,128)S(1)} %get-tuple-element.167, f32[16,16]{1,0:T(8,128)S(1)} %copy.135, s32[]{:T(128)} %get-tuple-element.166), kind=kOutput, calls=%fused_computation.2 | convolution fusion | flops 150995072 | bytes 15732740 | tf_op jit(solution)/shard_map/cond/branch_1_fun/sa,arfc->srfc/dot_general | solution.py:230
  169.4 12.0 %fusion.14 = f32[4,2,512,192]{2,0,3,1:T(4,128)S(1)} fusion(f32[16,2,512,192]{2,3,1,0:T(8,128)S(1)} %convolution_bitcast_fusion, f32[4,16]{1,0:T(4,128)S(1)} %get-tuple-element.167, f32[16,16]{1,0:T(8,128)S(1)} %copy.135, s32[]{:T(128)} %get-tuple-element.166), kind=kOutput, calls=%fused_computation.12 | convolution fusion | flops 150995072 | bytes 15732740 | tf_op jit(solution)/shard_map/cond/branch_1_fun/sa,arfc->srfc/dot_general | solution.py:230
  192.6 4.6 fusion.161
  202.4 121.5 %all-reduce.20.cloned.1.call-done = f32[1024,768]{1,0:T(8,128)} async-done(((f32[1024,768]{1,0:T(8,128)}), f32[1024,768]{1,0:T(8,128)}) %all-reduce.20.cloned.1.call-update) | async-done | bytes 3145744 | tf_op jit(solution)/shard_map/psum | solution.py:124
  327.6 11.3 multiply_convert_fusion
  338.9 5.9 convert_reduce_fusion.2
  354.2 115.2 %all-reduce.22.cloned.1.call-done = f32[1024,768]{1,0:T(8,128)} async-done(((f32[1024,768]{1,0:T(8,128)}), f32[1024,768]{1,0:T(8,128)}) %all-reduce.22.cloned.1.call-update) | async-done | bytes 3145744 | tf_op jit(solution)/shard_map/psum | solution.py:124
  485.9 13.5 %all-gather.11.cloned.1.call-done = bf16[16,256,192]{1,2,0:T(8,128)(2,1)} async-done(((bf16[4,256,192]{1,2,0:T(8,128)(2,1)}), bf16[16,256,192]{1,2,0:T(8,128)(2,1)}) %all-gather.11.cloned.1.call-update) | async-done | bytes 1572880 | tf_op jit(solution)/shard_map/all_gather | solution.py:278
  499.4 135.4 %conditional.3 = (f32[6,2,512,192]{2,3,1,0:T(8,128)}, f32[4,2,512,192]{2,3,1,0:T(8,128)S(1)}) conditional(s32[]{:T(128)} %convert_element_type.177, () %tuple.61, (f32[6,2,512,192]{2,3,1,0:T(8,128)}, f32[16,16]{0,1:T(8,128)S(1)}, s32[]{:T(128)}, f32[16,4]{1,0:T(8,128)S(1)}, bf16[16,256,192]{1,2,0:T(8,128)(2,1)}, ...), branch_computations={%region_16.17_spmd, %region_17.24_spmd} | conditional | flops 5786959872 | bytes 337929152 | solution.py:297
  499.6 3.9 copy.141
  503.6 4.0 slice_bitcast_fusion.13
  507.6 3.6 multiply_bitcast_fusion
  511.2 12.0 %fusion.70 = f32[4,2,512,192]{2,0,3,1:T(4,128)S(1)} fusion(f32[16,2,512,192]{2,3,1,0:T(8,128)S(1)} %multiply_bitcast_fusion, f32[16,4]{0,1:T(4,128)S(1)} %copy.140, f32[16,16]{0,1:T(8,128)S(1)} %get-tuple-element.171, s32[]{:T(128)} %get-tuple-element.172), kind=kOutput, calls=%fused_computation.96 | convolution fusion | flops 150995072 | bytes 15732740 | tf_op jit(solution)/shard_map/cond/branch_1_fun/sa,srfc->arfc/dot_general | solution.py:290
  527.9 12.2 %fusion.68 = f32[4,2,512,192]{2,0,3,1:T(4,128)S(1)} fusion(f32[16,2,512,192]{2,3,1,0:T(8,128)S(1)} %multiply_bitcast_fusion, f32[16,4]{0,1:T(4,128)S(1)} %copy.140, f32[16,16]{0,1:T(8,128)S(1)} %get-tuple-element.171, s32[]{:T(128)} %get-tuple-element.172), kind=kOutput, calls=%fused_computation.94 | convolution fusion | flops 150995072 | bytes 15732740 | tf_op jit(solution)/shard_map/cond/branch_1_fun/sa,srfc->arfc/dot_general | solution.py:290
  544.9 11.9 %fusion.66 = f32[4,2,512,192]{2,0,3,1:T(4,128)S(1)} fusion(f32[16,2,512,192]{2,3,1,0:T(8,128)S(1)} %multiply_bitcast_fusion, f32[16,4]{0,1:T(4,128)S(1)} %copy.140, f32[16,16]{0,1:T(8,128)S(1)} %get-tuple-element.171, s32[]{:T(128)} %get-tuple-element.172), kind=kOutput, calls=%fused_computation.92 | convolution fusion | flops 150995072 | bytes 15732740 | tf_op jit(solution)/shard_map/cond/branch_1_fun/sa,srfc->arfc/dot_general | solution.py:290
  562.6 11.9 %fusion.64 = f32[4,2,512,192]{2,0,3,1:T(4,128)S(1)} fusion(f32[16,2,512,192]{2,3,1,0:T(8,128)S(1)} %multiply_bitcast_fusion, f32[16,4]{0,1:T(4,128)S(1)} %copy.140, f32[16,16]{0,1:T(8,128)S(1)} %get-tuple-element.171, s32[]{:T(128)} %get-tuple-element.172), kind=kOutput, calls=%fused_computation.90 | convolution fusion | flops 150995072 | bytes 15732740 | tf_op jit(solution)/shard_map/cond/branch_1_fun/sa,srfc->arfc/dot_general | solution.py:290
  580.4 12.0 %fusion.62 = f32[4,2,512,192]{2,0,3,1:T(4,128)S(1)} fusion(f32[16,2,512,192]{2,3,1,0:T(8,128)S(1)} %multiply_bitcast_fusion, f32[16,4]{0,1:T(4,128)S(1)} %copy.140, f32[16,16]{0,1:T(8,128)S(1)} %get-tuple-element.171, s32[]{:T(128)} %get-tuple-element.172), kind=kOutput, calls=%fused_computation.88 | convolution fusion | flops 150995072 | bytes 15732740 | tf_op jit(solution)/shard_map/cond/branch_1_fun/sa,srfc->arfc/dot_general | solution.py:290
  592.4 12.2 %fusion.72 = f32[4,2,512,192]{2,0,3,1:T(4,128)S(1)} fusion(f32[16,2,512,192]{2,3,1,0:T(8,128)S(1)} %multiply_bitcast_fusion, f32[16,4]{0,1:T(4,128)S(1)} %copy.140, f32[16,16]{0,1:T(8,128)S(1)} %get-tuple-element.171, s32[]{:T(128)} %get-tuple-element.172), kind=kOutput, calls=%fused_computation.98 | convolution fusion | flops 150995072 | bytes 15732740 | tf_op jit(solution)/shard_map/cond/branch_1_fun/sa,srfc->arfc/dot_general | solution.py:290
  610.3 4.6 fusion.77
  636.5 5.8 bitcast_multiply_fusion.5
  651.1 4.5 fusion.249
  658.1 24.2 %all-reduce.24.cloned.1.call-done = f32[16,2,3,192]{3,1,2,0:T(2,128)} async-done(((f32[16,2,3,192]{3,1,2,0:T(2,128)}), f32[16,2,3,192]{3,1,2,0:T(2,128)}) %all-reduce.24.cloned.1.call-update) | async-done | bytes 73744
  684.9 6.8 scatter-add.24
  700.1 4.6 fusion.247
  704.8 5.0 fusion.151
  709.9 4.4 fusion.232
  727.2 5.8 convolution_bitcast_fusion.2
  733.2 6.0 fusion.158
  762.9 157.4 %all-reduce.28.cloned.1.call-done = (f32[1024,768]{1,0:T(8,128)}, f32[1024,768]{1,0:T(8,128)}) async-done(((f32[1024,768]{1,0:T(8,128)}, f32[1024,768]{1,0:T(8,128)}), (f32[1024,768]{1,0:T(8,128)}, f32[1024,768]{1,0:T(8,128)})) %all-reduce.28.cloned.1.call-update) | async-done | bytes 6291472 | tf_op jit(solution)/shard_map/psum | solution.py:124
  930.7 13.1 %psum.201 = f32[32,192]{1,0:T(8,128)} all-reduce(f32[32,192]{1,0:T(8,128)} %reduce-scatter.8.cloned.1.call-done), channel_id=1, replica_groups=mesh['dp'=2,'ctx'=4,'tp'=4] {'ctx'}, use_global_device_ids=true, to_apply=%region_51.52 | all-reduce | flops 6144 | bytes 49152 | tf_op jit(solution)/shard_map/psum | solution.py:326
  943.8 4.0 add_bitcast_fusion.2
  947.7 115.6 %all-reduce.26.cloned.1.call-done = (f32[768]{0:T(1024)}, f32[768]{0:T(1024)}, f32[3,768]{1,0:T(4,128)}, f32[3,3,768]{2,1,0:T(4,128)}, f32[3,768]{1,0:T(4,128)},...) async-done(((f32[768]{0:T(1024)}, f32[768]{0:T(1024)}, ...) | async-done | bytes 105488 | tf_op jit(solution)/shard_map/psum | solution.py:351
  1070.2 74.7 %all-reduce.30.cloned.1.call-done = (f32[384,3,192]{0,2,1:T(8,128)}, f32[192,384]{1,0:T(8,128)}, f32[384,768]{1,0:T(8,128)}, f32[768,384]{1,0:T(8,128)}) async-done(((f32[384,3,192]{0,2,1:T(8,128)}, f32[192,384]{1,0:T(8,128)}, f32[384,768]{1,0:T(8,128)}, f32[768,384]{1,0:T(8,128)}), (f32[384,3,192]{0,2,1:T(8,128)}, f32[192,384]{1,0:T(8,128)}, f32[384,768]{1,0:T(8,128)}, ...) | async-done | bytes 3538960 | tf_op jit(solution)/shard_map/psum | solution.py:326
  (497 shorter events, 233.0 us)
Async XLA Ops:
  8.0 55.2 %copy-start = (f32[64,64]{1,0:T(8,128)S(1)}, f32[64,64]{1,0:T(8,128)}, u32[]{:S(2)}) copy-start(f32[64,64]{1,0:T(8,128)} %param.55) | copy-start | bytes 49156
  8.0 19.3 %copy-start.3 = (bf16[1,1024,768]{2,1,0:T(8,128)(2,1)S(1)}, bf16[1,1024,768]{2,1,0:T(8,128)(2,1)}, u32[]{:S(2)}) copy-start(bf16[1,1024,768]{2,1,0:T(8,128)(2,1)} %param.44) | copy-start | bytes 4718596
  8.1 19.2 %copy-start.93 = (f32[768]{0:T(1024)S(1)}, f32[768]{0:T(1024)}, u32[]{:S(2)}) copy-start(f32[768]{0:T(1024)} %param.47) | copy-start | bytes 9220
  8.1 19.2 %copy-start.128 = (f32[768]{0:T(1024)S(1)}, f32[768]{0:T(1024)}, u32[]{:S(2)}) copy-start(f32[768]{0:T(1024)} %param.48) | copy-start | bytes 9220
  8.1 19.2 %copy-start.125 = (f32[3,192]{1,0:T(4,128)S(1)}, f32[3,192]{1,0:T(4,128)}, u32[]{:S(2)}) copy-start(f32[3,192]{1,0:T(4,128)} %param.50) | copy-start | bytes 6916
  8.1 90.6 %all-gather.5.cloned.1.call-start = ((), (), s32[]{:S(2)}) async-start(), calls=%async_computation.5 | async-start | bytes 1966080 | tf_op jit(solution)/shard_map/all_gather | solution.py:222
  10.0 16.4 %copy-start.86 = (f32[1024]{0:T(1024)}, f32[1024]{0:T(1024)S(1)}, u32[]{:S(2)}) copy-start(f32[1024]{0:T(1024)S(1)} %broadcast_multiply_fusion.10) | copy-start | bytes 12292
  12.0 14.4 %copy-start.95 = (f32[1024]{0:T(1024)}, f32[1024]{0:T(1024)S(1)}, u32[]{:S(2)}) copy-start(f32[1024]{0:T(1024)S(1)} %fusion.216) | copy-start | bytes 12292
  12.6 32.2 %copy-start.97 = (f32[3,1,192]{2,0,1:T(4,128)}, f32[3,1,192]{2,0,1:T(4,128)S(1)}, u32[]{:S(2)}) copy-start(f32[3,1,192]{2,0,1:T(4,128)S(1)} %copy.236) | copy-start | bytes 6916
  44.8 17.1 %copy-start.107 = (f32[33,64]{1,0:T(8,128)S(1)}, f32[33,64]{1,0:T(8,128)}, u32[]{:S(2)}) copy-start(f32[33,64]{1,0:T(8,128)} %param.53) | copy-start | bytes 25348
  44.8 17.1 %copy-start.122 = (f32[64]{0:T(128)S(1)}, f32[64]{0:T(128)}, u32[]{:S(2)}) copy-start(f32[64]{0:T(128)} %param.54) | copy-start | bytes 772
  49.9 147.3 %copy-start.5 = (f32[4,256,3,192]{1,3,0,2:T(8,128)}, f32[4,256,3,192]{1,3,0,2:T(8,128)S(1)}, u32[]{:S(2)}) copy-start(f32[4,256,3,192]{1,3,0,2:T(8,128)S(1)} %add_add_fusion.2) | copy-start | bytes 7077892
  49.9 13.3 %copy-start.105 = (f32[64]{0:T(128)S(1)}, f32[64]{0:T(128)}, u32[]{:S(2)}) copy-start(f32[64]{0:T(128)} %param.57) | copy-start | bytes 772
  49.9 13.3 %copy-start.121 = (f32[64]{0:T(128)S(1)}, f32[64]{0:T(128)}, u32[]{:S(2)}) copy-start(f32[64]{0:T(128)} %param.56) | copy-start | bytes 772
  50.8 273.1 %all-reduce.20.cloned.1.call-start = ((), (), s32[]{:S(2)}) async-start(), calls=%async_computation.6 | async-start | bytes 6291456 | tf_op jit(solution)/shard_map/psum | solution.py:124
  50.9 20.5 %copy-start.88 = (f32[1536,1]{0,1:T(1,128)}, f32[1536,1]{0,1:T(1,128)S(1)}, u32[]{:S(2)}) copy-start(f32[1536,1]{0,1:T(1,128)S(1)} %iota_multiply_fusion.1) | copy-start | bytes 18436
  50.9 17.9 %copy-start.84 = (f32[1536]{0:T(1024)}, f32[1536]{0:T(1024)S(1)}, u32[]{:S(2)}) copy-start(f32[1536]{0:T(1024)S(1)} %multiply_negate_fusion.1) | copy-start | bytes 18436
  51.0 17.9 %copy-start.111 = (f32[192]{0:T(256)}, f32[192]{0:T(256)S(1)}, u32[]{:S(2)}) copy-start(f32[192]{0:T(256)S(1)} %multiply_add_fusion.20) | copy-start | bytes 2308
  60.8 13.1 %copy-start.80 = (bf16[64,192]{1,0:T(8,128)(2,1)}, bf16[64,192]{1,0:T(8,128)(2,1)S(1)}, u32[]{:S(2)}) copy-start(bf16[64,192]{1,0:T(8,128)(2,1)S(1)} %all_gather.24) | copy-start | bytes 73732
  76.4 11.7 copy-start.32
  84.7 107.8 %copy-start.9 = (f32[1,512,256]{2,1,0:T(8,128)}, f32[1,512,256]{2,1,0:T(8,128)S(1)}, u32[]{:S(2)}) copy-start(f32[1,512,256]{2,1,0:T(8,128)S(1)} %get-tuple-element.414) | copy-start | bytes 1572868
  84.7 107.8 %copy-start.12 = (f32[1,512,256]{2,1,0:T(8,128)}, f32[1,512,256]{2,1,0:T(8,128)S(1)}, u32[]{:S(2)}) copy-start(f32[1,512,256]{2,1,0:T(8,128)S(1)} %get-tuple-element.415) | copy-start | bytes 1572868
  98.7 93.9 %copy-start.118 = (f32[192]{0:T(256)S(1)}, f32[192]{0:T(256)}, u32[]{:S(2)}) copy-start(f32[192]{0:T(256)} %param.59) | copy-start | bytes 2308
  198.9 125.0 %copy-start.114 = (f32[768]{0:T(1024)S(1)}, f32[768]{0:T(1024)}, u32[]{:S(2)}) copy-start(f32[768]{0:T(1024)} %param.61) | copy-start | bytes 9220
  201.2 126.2 %all-gather.7.cloned.1.call-start = ((), (), s32[]{:S(2)}) async-start(), calls=%async_computation.7 | async-start | bytes 1769472 | tf_op jit(solution)/shard_map/all_gather | solution.py:165
  201.8 137.1 %all-gather.9.cloned.1.call-start = ((), (), s32[]{:S(2)}) async-start(), calls=%async_computation.8 | async-start | bytes 1769472 | tf_op jit(solution)/shard_map/all_gather | solution.py:166
  202.4 267.0 %all-reduce.22.cloned.1.call-start = ((), (), s32[]{:S(2)}) async-start(), calls=%async_computation.9 | async-start | bytes 6291456 | tf_op jit(solution)/shard_map/psum | solution.py:124
  326.8 145.7 %copy-start.1 = (f32[1024,768]{1,0:T(8,128)}, f32[1024,768]{1,0:T(8,128)S(1)}, u32[]{:S(2)}) copy-start(f32[1024,768]{1,0:T(8,128)S(1)} %get-tuple-element.308) | copy-start | bytes 9437188
  349.2 150.2 %all-gather.11.cloned.1.call-start = ((), (), s32[]{:S(2)}) async-start(), calls=%async_computation.10 | async-start | bytes 1966080 | tf_op jit(solution)/shard_map/all_gather | solution.py:278
  480.6 201.7 %all-reduce.24.cloned.1.call-start = ((), (), s32[]{:S(2)}) async-start(), calls=%async_computation.16 | async-start | bytes 196608
  650.8 269.5 %all-reduce.28.cloned.1.call-start = ((), (), s32[]{:S(2)}) async-start(), calls=%async_computation.18 | async-start | bytes 12582912 | tf_op jit(solution)/shard_map/psum | solution.py:124
  697.0 233.2 %reduce-scatter.10.cloned.1.call-start = ((), (), s32[]{:S(2)}) async-start(), calls=%async_computation.13 | async-start | bytes 884736 | tf_op jit(solution)/shard_map/reduce_scatter | solution.py:331
  700.1 230.1 %reduce-scatter.12.cloned.1.call-start = ((), (), s32[]{:S(2)}) async-start(), calls=%async_computation.14 | async-start | bytes 3538944 | tf_op jit(solution)/shard_map/reduce_scatter | solution.py:332
  704.8 225.4 %reduce-scatter.14.cloned.1.call-start = ((), (), s32[]{:S(2)}) async-start(), calls=%async_computation.15 | async-start | bytes 3538944 | tf_op jit(solution)/shard_map/reduce_scatter | solution.py:333
  709.8 220.4 %reduce-scatter.6.cloned.1.call-start = ((), (), s32[]{:S(2)}) async-start(), calls=%async_computation.11 | async-start | bytes 2654208 | tf_op jit(solution)/shard_map/reduce_scatter | solution.py:330
  714.3 216.3 %reduce-scatter.8.cloned.1.call-start = ((), (), s32[]{:S(2)}) async-start(), calls=%async_computation.12 | async-start | bytes 98304 | tf_op jit(solution)/shard_map/reduce_scatter | solution.py:334
  715.2 12.0 %copy-start.91 = (f32[3072]{0:T(1024)}, f32[3072]{0:T(1024)S(1)}, u32[]{:S(2)}) copy-start(f32[3072]{0:T(1024)S(1)} %dynamic_update_slice.19) | copy-start | bytes 36868
  720.3 12.7 %copy-start.110 = (f32[768]{0:T(1024)}, f32[768]{0:T(1024)S(1)}, u32[]{:S(2)}) copy-start(f32[768]{0:T(1024)S(1)} %dynamic_update_slice.18) | copy-start | bytes 9220
  759.6 164.2 %copy-start.102 = (f32[1024]{0:T(1024)S(1)}, f32[1024]{0:T(1024)}, u32[]{:S(2)}) copy-start(f32[1024]{0:T(1024)} %copy-done.101) | copy-start | bytes 12292
  759.6 303.8 %all-reduce.26.cloned.1.call-start = ((), (), s32[]{:S(2)}) async-start(), calls=%async_computation.17 | async-start | bytes 314368 | tf_op jit(solution)/shard_map/psum | solution.py:351
  760.6 165.4 %copy-start.92 = (f32[3,768]{1,0:T(4,128)}, f32[3,768]{1,0:T(4,128)S(1)}, u32[]{:S(2)}) copy-start(f32[3,768]{1,0:T(4,128)S(1)} %dynamic_update_slice.17) | copy-start | bytes 27652
  760.9 165.1 %copy-start.83 = (f32[3,3,768]{2,1,0:T(4,128)}, f32[3,3,768]{2,1,0:T(4,128)S(1)}, u32[]{:S(2)}) copy-start(f32[3,3,768]{2,1,0:T(4,128)S(1)} %dynamic_update_slice.16) | copy-start | bytes 82948
  762.9 163.2 %copy-start.90 = (f32[3,768]{1,0:T(4,128)}, f32[3,768]{1,0:T(4,128)S(1)}, u32[]{:S(2)}) copy-start(f32[3,768]{1,0:T(4,128)S(1)} %dynamic_update_slice.15) | copy-start | bytes 27652
  929.4 14.4 %copy-start.115 = (f32[768]{0:T(1024)S(1)}, f32[768]{0:T(1024)}, u32[]{:S(2)}) copy-start(f32[768]{0:T(1024)} %param.67) | copy-start | bytes 9220
  930.1 214.8 %all-reduce.30.cloned.1.call-start = ((), (), s32[]{:S(2)}) async-start(), calls=%async_computation.19 | async-start | bytes 7077888 | tf_op jit(solution)/shard_map/psum | solution.py:326
  1144.8 16.5 %copy-start.71 = (f32[384,768]{1,0:T(8,128)S(1)}, f32[384,768]{1,0:T(8,128)}, u32[]{:S(2)}) copy-start(f32[384,768]{1,0:T(8,128)} %get-tuple-element.474) | copy-start | bytes 3538948
  1144.8 17.5 %copy-start.70 = (f32[768,384]{1,0:T(8,128)S(1)}, f32[768,384]{1,0:T(8,128)}, u32[]{:S(2)}) copy-start(f32[768,384]{1,0:T(8,128)} %get-tuple-element.476) | copy-start | bytes 3538948
  1149.7 13.7 %copy-start.116 = (f32[768]{0:T(1024)S(1)}, f32[768]{0:T(1024)}, u32[]{:S(2)}) copy-start(f32[768]{0:T(1024)} %get-tuple-element.477) | copy-start | bytes 9220
  (100 other events, 391.5 us)
Sparse Core Ops, SparseCore 0:
  50.9 21.2 all-gather.4
  201.3 122.5 all-reduce.19
  349.3 120.0 all-reduce.21
  480.7 18.6 all-gather.10
  651.0 31.2 all-reduce.23
  697.1 223.1 all-reduce.27
Sparse Core Ops, SparseCore 1:
  203.2 24.1 all-gather.6
  228.8 22.6 all-gather.8
  700.1 15.2 reduce-scatter.9
  717.6 34.6 reduce-scatter.11
  754.6 34.7 reduce-scatter.13
  791.7 28.1 reduce-scatter.5
  822.5 9.9 reduce-scatter.7
  930.1 133.2 all-reduce.25
  1068.1 76.6 all-reduce.29
where the time goes:
time: 1180 us; the launch traced here: 1170 us
  waiting for transfers between devices  624 us (53%)
  matrix products  258 us (22%)
  local copies, waits for them, and re-layouts  113 us (10%)
  other arithmetic  111 us (9%)
  blocking collectives  43.4 us (4%)
  between operations  19.6 us (2%)
    psum x3, waiting for transfers between devices, over_tp(): return lax.psum(partial_sum, 'tp')  394 us
    psum x1, waiting for transfers between devices, body(): lax.psum((leader * grad_mixer_gain, leader * grad_mixer_shift, leader * g...  116 us
    psum x1, waiting for transfers between devices, body(): lax.psum((matrix_grads[0], matrix_grads[1], matrix_grads[2], matrix_grads...  74.7 us
    dot_general x6, matrix products, accumulate(): jnp.einsum('sa,srfc->arfc', selector, target_spec, precision=EXACT)  72.2 us
    dot_general x6, matrix products, accumulate(): jnp.einsum('sa,arfc->srfc', selector, source_spec, precision=EXACT)  71.9 us
    unnamed x247, local copies, waits for them, and re-layouts  38.4 us
    unnamed x16, waiting for transfers between devices  25.8 us
  transfers between devices with their start and end apart: 15, of which 7 were waited for; matrix products, arithmetic and copies ran while one was open for 13% of the time, Pallas kernels for 0%

commit v1 on v0

v1 whole, which is shorter than its diff:
```python
import functools
import math

import jax
import jax.numpy as jnp
import numpy as np
from jax import lax
from jax.experimental import pallas as pl
from jax.experimental.pallas import tpu as pltpu
from jax.sharding import PartitionSpec as P

SEG = 256
DEPTH = 6
HEADS = 8
EXACT = lax.Precision.HIGHEST
EPSILON = 1e-05
SLOW_RATE = -math.log(0.01) / 1.5
FAST_RATE = -math.log(0.01) / 0.3
SHIFT_FLOOR = 0.05
F32 = jnp.float32
BF16 = jnp.bfloat16
MESH = pl.DeviceIdType.MESH
VM = pl.BlockSpec(memory_space=pltpu.VMEM)
SM = pl.BlockSpec(memory_space=pltpu.SMEM)
LIMIT = 60 << 20


def sds(shape, dtype):
    return jax.ShapeDtypeStruct(shape, dtype)


def call(kernel, out_shape, in_specs, scratch=(), collective=None, flops=0, traffic=0):
    many = isinstance(out_shape, (tuple, list))
    return pl.pallas_call(
        kernel,
        out_shape=out_shape,
        in_specs=in_specs,
        out_specs=tuple(VM for _ in out_shape) if many else VM,
        scratch_shapes=list(scratch),
        compiler_params=pltpu.CompilerParams(
            vmem_limit_bytes=LIMIT,
            collective_id=collective,
            has_side_effects=collective is not None,
        ),
        cost_estimate=pl.CostEstimate(flops=flops, bytes_accessed=traffic, transcendentals=0),
    )


def spectral_constants(block_len):
    freq = np.arange(block_len)[:, None]
    place = np.arange(block_len)[None, :]
    angle = ((2 * freq + 1) * place % (4 * block_len)) * (2.0 * math.pi / (4 * block_len))
    table = np.concatenate([np.cos(angle), -np.sin(angle)], axis=0).astype(np.float32)
    high = table.astype(jnp.bfloat16)
    low = (table - high.astype(np.float32)).astype(jnp.bfloat16)
    sign = np.where(np.arange(block_len) % 2 == 0, 1.0, -1.0).astype(np.float32)[:, None]
    return high, low, np.ascontiguousarray(high.T), np.ascontiguousarray(low.T), sign


def implicit_filter(w1, b1, w2, b2, frequency, last_weight, length, channel_first, width_all):
    positions = jnp.arange(length, dtype=F32)
    time_pos = positions / (length - 1)
    bands = (w1.shape[0] - 1) // 2
    band_freq = jnp.linspace(0.0001, bands - 1, bands, dtype=F32)
    angles = 2.0 * math.pi / length * positions
    phases = angles[:, None] * band_freq[None, :]
    embedding = jnp.concatenate([time_pos[:, None], jnp.cos(phases), -jnp.sin(phases)], axis=1)
    hidden = jnp.sin(frequency * (jnp.dot(embedding, w1, precision=EXACT) + b1))
    hidden = jnp.sin(frequency * (jnp.dot(hidden, w2, precision=EXACT) + b2))
    raw_taps = jnp.dot(hidden, last_weight, precision=EXACT)
    channel_ids = (channel_first + jnp.arange(last_weight.shape[1])).astype(F32)
    decay_rate = SLOW_RATE + (FAST_RATE - SLOW_RATE) * channel_ids / (width_all - 1)
    envelope = jnp.exp(-time_pos[:, None] * decay_rate[None, :])
    return raw_taps * (envelope + SHIFT_FLOOR)


def normalize(values):
    mean_value = jnp.mean(values, axis=-1, keepdims=True)
    centered = values - mean_value
    variance = jnp.mean(centered * centered, axis=-1, keepdims=True)
    scale = lax.rsqrt(variance + EPSILON)
    return centered * scale, scale


def split(values):
    high = values.astype(BF16)
    return high, (values - high.astype(F32)).astype(BF16)


def mm(lhs, rhs):
    return jnp.dot(lhs, rhs, preferred_element_type=F32)


def mm_nt(lhs, rhs):
    return lax.dot_general(lhs, rhs, (((1,), (1,)), ((), ())), preferred_element_type=F32)


def mm_tn(lhs, rhs):
    return lax.dot_general(lhs, rhs, (((0,), (0,)), ((), ())), preferred_element_type=F32)


def mm_split(high, low, values):
    v_high, v_low = split(values)
    return mm(high, v_high) + (mm(low, v_high) + mm(high, v_low))


def mix_in_kernel(
    x_ref, xt_ref, pick_ref, w_ref, bias_ref, gain_ref, shift_ref, sw_ref, sb_ref,
    low_ref, proj_ref, head_ref, mixed_ref, carried_ref, ext_ref,
):
    gain, shift = gain_ref[...], shift_ref[...]
    tails = normalize(xt_ref[...].astype(F32))[0] * gain + shift
    tails = tails.astype(BF16)
    tail_proj = [mm(tails, w_ref[g]) + bias_ref[g : g + 1] for g in range(3)]
    blocks = x_ref.shape[0] // SEG

    def one(s, unused):
        rows = pl.ds(pl.multiple_of(s * SEG, SEG), SEG)
        low = (normalize(x_ref[rows].astype(F32))[0] * gain + shift).astype(BF16)
        low_ref[rows] = low
        out = []
        for g in range(3):
            projected = mm(low, w_ref[g]) + bias_ref[g : g + 1]
            proj_ref[g, rows] = projected
            head = jnp.dot(pick_ref[s], tail_proj[g], precision=EXACT, preferred_element_type=F32)
            head_ref[g, s] = head
            ext_ref[g, 0:HEADS] = head
            ext_ref[g, HEADS : HEADS + SEG] = projected
            mixed = (
                sw_ref[3 * g : 3 * g + 1] * ext_ref[g, HEADS - 2 : HEADS - 2 + SEG]
                + sw_ref[3 * g + 1 : 3 * g + 2] * ext_ref[g, HEADS - 1 : HEADS - 1 + SEG]
                + sw_ref[3 * g + 2 : 3 * g + 3] * projected
                + sb_ref[g : g + 1]
            )
            mixed_ref[g, rows] = mixed
            out.append(mixed)
        carried_ref[rows] = (out[2] * out[1]).astype(BF16)
        return unused

    lax.fori_loop(0, blocks, one, 0)


FT = 64


def conv_fwd_kernel(
    idx_ref, own_ref, trunk_ref, branch_ref, taps_ref, gate_ref, skip_ref,
    fh_ref, fl_ref, th_ref, tl_ref, sign_ref,
    conv_ref, gated_ref, spec_ref, filt_ref, acc_ref,
):
    blocks = own_ref.shape[0]
    fh, fl, th, tl = fh_ref[...], fl_ref[...], th_ref[...], tl_ref[...]

    def source(j, unused):
        for base, ref in ((0, own_ref), (4, trunk_ref), (8, branch_ref)):
            part = ref[j]
            out = mm(fh, part) + mm(fl, part)
            spec_ref[base + j, 0] = out[:SEG]
            spec_ref[base + j, 1] = out[SEG:]
        return unused

    lax.fori_loop(0, blocks, source, 0)
    sign = sign_ref[...]
    last = None
    for j in range(DEPTH):
        part = taps_ref[j * SEG : (j + 1) * SEG]
        out = mm_split(fh, fl, part)
        re, im = out[:SEG], out[SEG:]
        if last is None:
            filt_ref[j, 0] = re
            filt_ref[j, 1] = im
        else:
            filt_ref[j, 0] = re - sign * last[1]
            filt_ref[j, 1] = im + sign * (last[0] - last[2])
        last = (re, im, part[0:1])
    filt_ref[DEPTH] = jnp.zeros(filt_ref.shape[1:], F32)

    def dest(s, unused):
        pairs = [(0, s), (idx_ref[s, 4], 8 + idx_ref[s, 5])] + [(idx_ref[s, a], 4 + a) for a in range(4)]
        for t in range(SEG // FT):
            rows = slice(t * FT, (t + 1) * FT)
            re = im = None
            for h, x in pairs:
                hr, hi = filt_ref[h, 0, rows], filt_ref[h, 1, rows]
                xr, xi = spec_ref[x, 0, rows], spec_ref[x, 1, rows]
                pr, pi = hr * xr - hi * xi, hr * xi + hi * xr
                re, im = (pr, pi) if re is None else (re + pr, im + pi)
            acc_ref[rows] = re
            acc_ref[SEG + t * FT : SEG + (t + 1) * FT] = im
        long_out = mm_split(th, tl, acc_ref[...]) * (1.0 / SEG)
        place = pl.ds(pl.multiple_of(s * SEG, SEG), SEG)
        convolved = long_out + skip_ref[...] * own_ref[s].astype(F32)
        conv_ref[place] = convolved
        gated_ref[place] = (convolved * gate_ref[place]).astype(BF16)
        return unused

    lax.fori_loop(0, blocks, dest, 0)


def conv_bwd_kernel(
    idx_ref, back_ref, leaf_ref, dlong_ref, dall_ref, dconv_ref, spec_ref, filt_ref, skip_ref,
    fh_ref, fl_ref, th_ref, tl_ref, sign_ref,
    dcar_ref, dtaps_ref, yspec_ref, dfilt_ref, acc_ref, sum_ref,
):
    blocks = dlong_ref.shape[0]
    fh, fl, th, tl = fh_ref[...], fl_ref[...], th_ref[...], tl_ref[...]
    scale = 1.0 / SEG

    def transform(j, unused):
        for base, ref, off in ((0, dlong_ref, 0), (4, dall_ref, 0), (8, dall_ref, 4)):
            part = ref[off + j]
            out = (mm(fh, part) + mm(fl, part)) * scale
            yspec_ref[base + j, 0] = out[:SEG]
            yspec_ref[base + j, 1] = out[SEG:]
        total = leaf_ref[j, 0] * dall_ref[8].astype(F32)
        for leaf in range(1, 8):
            total = total + leaf_ref[j, leaf] * dall_ref[8 + leaf].astype(F32)
        out = mm_split(fh, fl, total) * scale
        yspec_ref[12 + j, 0] = out[:SEG]
        yspec_ref[12 + j, 1] = out[SEG:]
        return unused

    lax.fori_loop(0, blocks, transform, 0)

    def source(s, unused):
        pairs = [(0, s)] + [(back_ref[s, k], 4 + k) for k in range(12)]
        for t in range(SEG // FT):
            rows = slice(t * FT, (t + 1) * FT)
            re = im = None
            for h, y in pairs:
                hr, hi = filt_ref[h, 0, rows], filt_ref[h, 1, rows]
                yr, yi = yspec_ref[y, 0, rows], yspec_ref[y, 1, rows]
                pr, pi = hr * yr + hi * yi, hr * yi - hi * yr
                re, im = (pr, pi) if re is None else (re + pr, im + pi)
            acc_ref[rows] = re
            acc_ref[SEG + t * FT : SEG + (t + 1) * FT] = im
        place = pl.ds(pl.multiple_of(s * SEG, SEG), SEG)
        dcar_ref[place] = mm_split(th, tl, acc_ref[...]) + skip_ref[...] * dconv_ref[place]
        return unused

    lax.fori_loop(0, blocks, source, 0)
    dfilt_ref[...] = jnp.zeros(dfilt_ref.shape, F32)

    def filters(s, unused):
        pairs = [(0, s), (idx_ref[s, 4], 8 + idx_ref[s, 5])] + [(idx_ref[s, a], 4 + a) for a in range(4)]
        for t in range(SEG // FT):
            rows = slice(t * FT, (t + 1) * FT)
            yr, yi = yspec_ref[s, 0, rows], yspec_ref[s, 1, rows]
            for h, x in pairs:
                xr, xi = spec_ref[x, 0, rows], spec_ref[x, 1, rows]
                dfilt_ref[h, 0, rows] += xr * yr + xi * yi
                dfilt_ref[h, 1, rows] += xr * yi - xi * yr
        return unused

    lax.fori_loop(0, blocks, filters, 0)
    sign = sign_ref[...]
    first_row = lax.broadcasted_iota(jnp.int32, (SEG, 1), 0) == 0
    for j in range(DEPTH):
        re, im = dfilt_ref[j, 0], dfilt_ref[j, 1]
        fix = None
        if j + 1 < DEPTH:
            nr, ni = dfilt_ref[j + 1, 0], dfilt_ref[j + 1, 1]
            re = re + sign * ni
            im = im - sign * nr
            fix = jnp.sum(sign * ni, axis=0, keepdims=True)
        acc_ref[0:SEG] = re
        acc_ref[SEG : 2 * SEG] = im
        taps = mm_split(th, tl, acc_ref[...])
        if fix is not None:
            taps = jnp.where(first_row, taps - fix, taps)
        dtaps_ref[j * SEG : (j + 1) * SEG] = taps


def feed_kernel(
    gated_ref, out_ref, x_ref, g_ref, ob_ref, gain_ref, shift_ref, up_ref, ub_ref, down_ref,
    resid_ref, dpart_ref, npart_ref, gdown_ref, gup_ref, gdb_ref, gub_ref,
):
    groups = gated_ref.shape[0]
    gdown_ref[...] = jnp.zeros(gdown_ref.shape, F32)
    gup_ref[...] = jnp.zeros(gup_ref.shape, F32)
    gdb_ref[...] = jnp.zeros(gdb_ref.shape, F32)
    gub_ref[...] = jnp.zeros(gub_ref.shape, F32)

    def one(s, unused):
        rows = pl.ds(pl.multiple_of(s * SEG, SEG), SEG)
        residual = x_ref[rows].astype(F32)
        mixed = mm(gated_ref[0, rows], out_ref[0])
        for z in range(1, groups):
            mixed = mixed + mm(gated_ref[z, rows], out_ref[z])
        residual = residual + mixed + ob_ref[...]
        resid_ref[rows] = residual
        low = (normalize(residual)[0] * gain_ref[...] + shift_ref[...]).astype(BF16)
        pre = mm(low, up_ref[...]) + ub_ref[...]
        cdf = 0.5 * (1.0 + lax.erf(pre * math.sqrt(0.5)))
        hidden = (pre * cdf).astype(BF16)
        slope = cdf + pre * (jnp.exp(-0.5 * pre * pre) * (1.0 / math.sqrt(2.0 * math.pi)))
        dpart_ref[rows] = mm(hidden, down_ref[...]).astype(BF16)
        grad = g_ref[rows]
        d_pre = (mm_nt(grad, down_ref[...]) * slope).astype(BF16)
        npart_ref[rows] = mm_nt(d_pre, up_ref[...]).astype(BF16)
        gdown_ref[...] += mm_tn(hidden, grad)
        gup_ref[...] += mm_tn(low, d_pre)
        gdb_ref[...] += jnp.sum(grad.astype(F32), axis=0, keepdims=True)
        gub_ref[...] += jnp.sum(d_pre.astype(F32), axis=0, keepdims=True)
        return unused

    lax.fori_loop(0, x_ref.shape[0] // SEG, one, 0)


def feed_back_kernel(
    resid_ref, dn_ref, g_ref, gain_ref, out_ref, gated_ref, mixed_ref, conv_ref, carried_ref,
    dres_ref, dconv_ref, dlong_ref, dzero_ref, gout_ref, gob_ref, ggain_ref, gshift_ref, gskip_ref,
):
    for ref in (gout_ref, gob_ref, ggain_ref, gshift_ref, gskip_ref):
        ref[...] = jnp.zeros(ref.shape, F32)

    def one(s, unused):
        rows = pl.ds(pl.multiple_of(s * SEG, SEG), SEG)
        xhat, scale = normalize(resid_ref[rows])
        dn = dn_ref[rows].astype(F32)
        e = dn * gain_ref[...]
        d_res = g_ref[rows].astype(F32) + scale * (
            e - jnp.mean(e, axis=-1, keepdims=True) - xhat * jnp.mean(e * xhat, axis=-1, keepdims=True)
        )
        dres_ref[rows] = d_res
        ggain_ref[...] += jnp.sum(dn * xhat, axis=0, keepdims=True)
        gshift_ref[...] += jnp.sum(dn, axis=0, keepdims=True)
        d_mix = d_res.astype(BF16)
        gob_ref[...] += jnp.sum(d_mix.astype(F32), axis=0, keepdims=True)
        gout_ref[...] += mm_tn(gated_ref[rows], d_mix)
        d_gated = mm_nt(d_mix, out_ref[...])
        d_conv = d_gated * mixed_ref[rows]
        dconv_ref[rows] = d_conv
        dlong_ref[rows] = d_conv.astype(BF16)
        dzero_ref[rows] = d_gated * conv_ref[rows]
        gskip_ref[...] += jnp.sum(d_conv * carried_ref[rows].astype(F32), axis=0, keepdims=True)
        return unused

    lax.fori_loop(0, g_ref.shape[0] // SEG, one, 0)


def mix_back_kernel(
    dzero_ref, dcar_ref, mixed_ref, proj_ref, head_ref, heads_ref, pick_ref, sw_ref, low_ref, w_ref,
    part_ref, gin_ref, gib_ref, gsw_ref, gsb_ref, ext_ref, dm_ref,
):
    for ref in (gin_ref, gib_ref, gsw_ref, gsb_ref):
        ref[...] = jnp.zeros(ref.shape, F32)

    def one(s, unused):
        rows = pl.ds(pl.multiple_of(s * SEG, SEG), SEG)
        part = None
        for g in range(3):
            if g == 0:
                dm = dzero_ref[rows]
            else:
                dm = dcar_ref[rows] * mixed_ref[3 - g, rows]
            ext_ref[0:HEADS] = head_ref[g, s]
            ext_ref[HEADS : HEADS + SEG] = proj_ref[g, rows]
            for k in range(3):
                piece = ext_ref[HEADS - 2 + k : HEADS - 2 + k + SEG]
                gsw_ref[3 * g + k : 3 * g + k + 1] += jnp.sum(piece * dm, axis=0, keepdims=True)
            gsb_ref[g : g + 1] += jnp.sum(dm, axis=0, keepdims=True)
            child = jnp.dot(pick_ref[s], heads_ref[g], precision=EXACT, preferred_element_type=F32)
            dm_ref[0:SEG] = dm
            dm_ref[SEG : SEG + HEADS] = child
            dp = (
                sw_ref[3 * g + 2 : 3 * g + 3] * dm
                + sw_ref[3 * g + 1 : 3 * g + 2] * dm_ref[1 : 1 + SEG]
                + sw_ref[3 * g : 3 * g + 1] * dm_ref[2 : 2 + SEG]
            ).astype(BF16)
            gib_ref[g : g + 1] += jnp.sum(dp.astype(F32), axis=0, keepdims=True)
            gin_ref[g] += mm_tn(low_ref[rows], dp)
            term = mm_nt(dp, w_ref[g])
            part = term if part is None else part + term
        part_ref[rows] = part.astype(BF16)
        return unused

    lax.fori_loop(0, low_ref.shape[0] // SEG, one, 0)


def norm_back_kernel(x_ref, dn_ref, dres_ref, gain_ref, gin_ref, ggain_ref, gshift_ref):
    ggain_ref[...] = jnp.zeros(ggain_ref.shape, F32)
    gshift_ref[...] = jnp.zeros(gshift_ref.shape, F32)

    def one(s, unused):
        rows = pl.ds(pl.multiple_of(s * SEG, SEG), SEG)
        xhat, scale = normalize(x_ref[rows].astype(F32))
        dn = dn_ref[rows].astype(F32)
        e = dn * gain_ref[...]
        gin_ref[rows] = dres_ref[rows] + scale * (
            e - jnp.mean(e, axis=-1, keepdims=True) - xhat * jnp.mean(e * xhat, axis=-1, keepdims=True)
        )
        ggain_ref[...] += jnp.sum(dn * xhat, axis=0, keepdims=True)
        gshift_ref[...] += jnp.sum(dn, axis=0, keepdims=True)
        return unused

    lax.fori_loop(0, x_ref.shape[0] // SEG, one, 0)


def spot(**changes):
    base = {name: lax.axis_index(name) for name in ("dp", "ctx", "tp")}
    base.update(changes)
    return (base["dp"], base["ctx"], base["tp"])


def remote(src, dst, send, recv, where):
    return pltpu.make_async_remote_copy(
        src_ref=src, dst_ref=dst, send_sem=send, recv_sem=recv, device_id=where, device_id_type=MESH
    )


def greet(partners):
    barrier = pltpu.get_barrier_semaphore()
    for where in partners:
        pl.semaphore_signal(barrier, inc=1, device_id=where, device_id_type=MESH)
    pl.semaphore_wait(barrier, len(partners))


CHUNK = 64


def chain_sum_kernel(part_ref, out_ref, end_ref, mid_ref, send_ref, acc_ref, s_end, r_end, s_mid, r_mid, s_out, r_out, s_cross, r_cross, s_fwd):
    tp = lax.axis_index("tp")
    inner = jnp.logical_and(tp > 0, tp < 3)
    pairs = part_ref.shape[0] // (2 * CHUNK)
    side = jnp.where(tp < 2, 0, 1)
    mate = spot(tp=jnp.where(inner, jnp.where(side == 0, 0, 3), jnp.where(side == 0, 1, 2)))
    cross = spot(tp=3 - tp)
    barrier = pltpu.get_barrier_semaphore()
    pl.semaphore_signal(barrier, inc=1, device_id=mate, device_id_type=MESH)
    pl.semaphore_signal(barrier, inc=1, device_id=cross, device_id_type=MESH)
    pl.semaphore_wait(barrier, 2)

    def rows(c):
        return pl.ds(pl.multiple_of(c * CHUNK, CHUNK), CHUNK)

    def to_mid(c):
        return remote(part_ref.at[rows(c)], end_ref.at[rows(c)], s_end.at[c], r_end.at[c], mate)

    def to_cross(c):
        return remote(send_ref.at[rows(c)], mid_ref.at[rows(c)], s_mid.at[c], r_mid.at[c], cross)

    def final_end(c):
        return remote(out_ref.at[rows(c)], out_ref.at[rows(c)], s_out.at[c], r_out.at[c], mate)

    def final_cross(c):
        return remote(out_ref.at[rows(c)], out_ref.at[rows(c)], s_cross.at[c], r_cross.at[c], cross)

    @pl.when(jnp.logical_not(inner))
    def _():
        for c in range(2 * pairs):
            to_mid(c).start()
        for c in range(2 * pairs):
            final_end(c).wait_recv()
        for c in range(2 * pairs):
            to_mid(c).wait_send()

    lag = 2

    @pl.when(inner)
    def _():
        for k in range(pairs + 2 * lag):
            if k < pairs:
                mine, other = 2 * k + side, 2 * k + 1 - side
                to_mid(2 * k).wait_recv()
                to_mid(2 * k + 1).wait_recv()
                send_ref[rows(other)] = (
                    part_ref[rows(other)].astype(F32) + end_ref[rows(other)].astype(F32)
                ).astype(BF16)
                to_cross(other).start()
            j = k - lag
            if 0 <= j < pairs:
                mine = 2 * j + side
                to_cross(mine).wait_recv()
                out_ref[rows(mine)] = (
                    part_ref[rows(mine)].astype(F32)
                    + end_ref[rows(mine)].astype(F32)
                    + mid_ref[rows(mine)].astype(F32)
                ).astype(BF16)
                final_cross(mine).start()
                final_end(mine).start()
            j = k - 2 * lag
            if 0 <= j < pairs:
                other = 2 * j + 1 - side
                final_cross(other).wait_recv()
                final_end(other).start()
        for j in range(pairs):
            mine, other = 2 * j + side, 2 * j + 1 - side
            to_cross(other).wait_send()
            final_cross(mine).wait_send()
            final_end(mine).wait_send()
            final_end(other).wait_send()


def chain_sum(part, collective):
    rows, width = part.shape
    count = rows // CHUNK
    return call(
        chain_sum_kernel,
        sds((rows, width), BF16),
        [VM],
        [
            pltpu.VMEM((rows, width), BF16),
            pltpu.VMEM((rows, width), BF16),
            pltpu.VMEM((rows, width), BF16),
            pltpu.VMEM((8, 128), F32),
        ]
        + [pltpu.SemaphoreType.DMA((count,)) for _ in range(8)]
        + [pltpu.SemaphoreType.DMA((1,))],
        collective,
        traffic=rows * width * 8,
    )(part)


def line_gather_kernel(x_ref, out_ref, local_sem, send_sem, recv_sem):
    tp = lax.axis_index("tp")
    count = out_ref.shape[0]
    greet([spot(tp=lax.rem(tp + i, count)) for i in range(1, count)])
    copies = [
        remote(x_ref, out_ref.at[tp], send_sem.at[i], recv_sem.at[tp], spot(tp=lax.rem(tp + i, count)))
        for i in range(1, count)
    ]
    for copy in copies:
        copy.start()
    own = pltpu.make_async_copy(x_ref, out_ref.at[tp], local_sem)
    own.start()
    for i in range(1, count):
        source = lax.rem(tp + i, count)
        remote(x_ref, out_ref.at[source], send_sem.at[0], recv_sem.at[source], spot()).wait_recv()
    for copy in copies:
        copy.wait_send()
    own.wait()


def line_gather(x, count, collective):
    return call(
        line_gather_kernel,
        sds((count,) + x.shape, x.dtype),
        [VM],
        [pltpu.SemaphoreType.DMA, pltpu.SemaphoreType.DMA((count,)), pltpu.SemaphoreType.DMA((count,))],
        collective,
        traffic=x.size * 2 * count,
    )(x)


def pieces_of(half):
    return max(p for p in (1, 2, 3, 4) if half % (16 * p) == 0)


def matrix_sum_kernel(g_ref, out_ref, core_ref, keep_ref, part_ref, y_ref, y_own, s_core, r_core, s_dp, r_dp, s_y, r_y, s_back, r_back):
    dp, ctx = lax.axis_index("dp"), lax.axis_index("ctx")
    owners = g_ref.shape[0]
    half = g_ref.shape[1] // 2
    pieces = pieces_of(half)
    rows = half // pieces
    low = lax.rem(ctx, 2)
    mate = spot(ctx=ctx + 1 - 2 * low)
    across = spot(ctx=lax.rem(ctx + 2, 4))
    peers = [spot(dp=lax.rem(dp + i, owners)) for i in range(1, owners)]
    greet([mate, across] + peers)
    mine, other = low * half, (1 - low) * half

    def at(base, p):
        return pl.ds(pl.multiple_of(base + p * rows, 16), rows)

    def core_copy(o, p):
        return remote(g_ref.at[o, at(other, p)], core_ref.at[o, at(0, p)], s_core.at[o, p], r_core.at[o, p], mate)

    def dp_copy(i, p):
        o = lax.rem(dp + i, owners)
        return remote(keep_ref.at[o, at(0, p)], part_ref.at[dp, at(0, p)], s_dp.at[o, p], r_dp.at[dp, p], peers[i - 1])

    def y_copy(p):
        return remote(y_own.at[at(0, p)], y_ref.at[at(0, p)], s_y.at[p], r_y.at[p], across)

    def back_copy(p):
        return remote(out_ref.at[at(mine, p)], out_ref.at[at(mine, p)], s_back.at[p], r_back.at[p], mate)

    for p in range(pieces):
        for o in range(owners):
            core_copy(o, p).start()
    for p in range(pieces):
        for o in range(owners):
            core_copy(o, p).wait_recv()
            keep_ref[o, at(0, p)] = (
                g_ref[o, at(mine, p)].astype(F32) + core_ref[o, at(0, p)].astype(F32)
            ).astype(BF16)
        for i in range(1, owners):
            dp_copy(i, p).start()
    for p in range(pieces):
        total = keep_ref[dp, at(0, p)].astype(F32)
        for i in range(1, owners):
            source = lax.rem(dp + i, owners)
            remote(keep_ref.at[0, at(0, p)], part_ref.at[source, at(0, p)], s_dp.at[0, p], r_dp.at[source, p], mate).wait_recv()
            total = total + part_ref[source, at(0, p)].astype(F32)
        y_own[at(0, p)] = total.astype(BF16)
        y_copy(p).start()
    for p in range(pieces):
        y_copy(p).wait_recv()
        out_ref[at(mine, p)] = y_own[at(0, p)].astype(F32) + y_ref[at(0, p)].astype(F32)
        back_copy(p).start()
    for p in range(pieces):
        for o in range(owners):
            core_copy(o, p).wait_send()
        for i in range(1, owners):
            dp_copy(i, p).wait_send()
        y_copy(p).wait_send()
        back_copy(p).wait_send()
        remote(out_ref.at[at(other, p)], out_ref.at[at(other, p)], s_back.at[p], r_back.at[p], mate).wait_recv()


def matrix_sum(grads, collective):
    owners, rows, width = grads.shape
    half = rows // 2
    pieces = pieces_of(half)
    return call(
        matrix_sum_kernel,
        sds((rows, width), F32),
        [VM],
        [
            pltpu.VMEM((owners, half, width), BF16),
            pltpu.VMEM((owners, half, width), BF16),
            pltpu.VMEM((owners, half, width), BF16),
            pltpu.VMEM((half, width), BF16),
            pltpu.VMEM((half, width), BF16),
            pltpu.SemaphoreType.DMA((owners, pieces)),
            pltpu.SemaphoreType.DMA((owners, pieces)),
            pltpu.SemaphoreType.DMA((owners, pieces)),
            pltpu.SemaphoreType.DMA((owners, pieces)),
            pltpu.SemaphoreType.DMA((pieces,)),
            pltpu.SemaphoreType.DMA((pieces,)),
            pltpu.SemaphoreType.DMA((pieces,)),
            pltpu.SemaphoreType.DMA((pieces,)),
        ],
        collective,
        traffic=grads.size * 8,
    )(grads)


def tree_tables(parent_row):
    block_count = parent_row.shape[0]
    ids = jnp.arange(block_count, dtype=jnp.int32)
    parent_map = (parent_row[:, None] == ids[None, :]).astype(jnp.int32)
    ancestor = jnp.eye(block_count, dtype=jnp.int32)
    for _ in range(DEPTH - 1):
        ancestor = jnp.eye(block_count, dtype=jnp.int32) + jnp.sum(
            parent_map[:, :, None] * ancestor[None, :, :], axis=1
        )
    depths = jnp.sum(ancestor, axis=1)
    gap = depths[:, None] - depths[None, :]
    return parent_map, ancestor, gap


def body(
    block_in, out_grad, parents, mixer_gain, mixer_shift, in_proj, in_bias, short_weight, short_bias,
    filter_one, filter_one_bias, filter_two, filter_two_bias, filter_freq, filter_out, skip_gain,
    out_proj, out_bias, feed_gain, feed_shift, feed_up, feed_up_bias, feed_down, feed_down_bias,
):
    x = block_in[0]
    g = out_grad[0]
    total_rows, width = x.shape
    channels = skip_gain.shape[0]
    blocks = total_rows // SEG
    hidden = feed_up.shape[1]
    tp_count = lax.axis_size("tp")
    tp_index = lax.axis_index("tp")
    owners = lax.axis_size("dp")
    first = lax.axis_index("ctx") * blocks
    all_blocks = parents.shape[1]

    in_all = jnp.transpose(lax.all_gather(in_proj, "dp", axis=0, tiled=True), (1, 0, 2))
    tails = lax.all_gather(x.reshape(blocks, SEG, width)[:, SEG - 2 :], "ctx", axis=0, tiled=True)
    tails = tails.reshape(2 * all_blocks, width)
    out_own = lax.all_gather(out_proj, "dp", axis=1, tiled=True)
    out_all = lax.all_gather(out_own, "tp", axis=0)
    up_all = lax.all_gather(feed_up, "dp", axis=0, tiled=True)
    down_all = lax.all_gather(feed_down, "dp", axis=1, tiled=True)
    last_all = lax.all_gather(filter_out, "dp", axis=0, tiled=True)

    parent_map, ancestor, gap = tree_tables(parents[0])
    none = DEPTH

    def local(table, axis=0):
        return lax.dynamic_slice_in_dim(table, first, blocks, axis)

    hop = jnp.where(ancestor > 0, gap, none)
    own_ids = first + jnp.arange(blocks)
    to_trunk = jnp.where(own_ids[:, None] == jnp.arange(4)[None, :], none, local(hop)[:, :4])
    own_parent = local(parent_map)
    is_leaf = own_ids >= 8
    branch_of = jnp.sum(own_parent[:, 4:8] * jnp.arange(4), axis=1)
    fwd_idx = jnp.concatenate(
        [to_trunk, jnp.where(is_leaf, 1, none)[:, None], branch_of[:, None], jnp.zeros((blocks, 2), jnp.int32)],
        axis=1,
    ).astype(jnp.int32)
    down_hop = local(hop, 1)
    not_self = jnp.arange(8)[:, None] != own_ids[None, :]
    near = jnp.where(not_self, down_hop[:8], none).T
    branch_reach = down_hop[4:8].T
    far = jnp.where(branch_reach < none, branch_reach + 1, none)
    back_idx = jnp.concatenate([near, far], axis=1).astype(jnp.int32)
    leaf_sel = parent_map[8:16, 4:8].T.astype(F32)

    row_id = jnp.arange(HEADS)
    tail_id = jnp.arange(2 * all_blocks)
    own_par = local(parents[0])
    pick = (
        (tail_id[None, None, :] == (2 * own_par[:, None] + row_id[None, :] - (HEADS - 2))[:, :, None])
        & (row_id[None, :, None] >= HEADS - 2)
        & (own_par[:, None, None] >= 0)
    ).astype(F32)
    child_of = parents[0][tail_id // 2]
    pick_child = (
        (child_of[None, None, :] == own_ids[:, None, None])
        & ((tail_id % 2)[None, None, :] == row_id[None, :, None])
    ).astype(F32)

    def make_taps(w1, b1, w2, b2, frequency, last_weight):
        return implicit_filter(
            w1, b1, w2, b2, frequency, last_weight, DEPTH * SEG, tp_index * channels, channels * tp_count
        )

    filter_taps, taps_back = jax.vjp(
        make_taps, filter_one, filter_one_bias, filter_two, filter_two_bias, filter_freq, last_all.astype(F32)
    )

    row = lambda v: v.reshape(1, -1)
    sw = short_weight.reshape(9, channels)
    low, proj, head, mixed, carried = call(
        mix_in_kernel,
        (
            sds((total_rows, width), BF16),
            sds((3, total_rows, channels), F32),
            sds((3, blocks, HEADS, channels), F32),
            sds((3, total_rows, channels), F32),
            sds((total_rows, channels), BF16),
        ),
        [VM] * 9,
        [pltpu.VMEM((3, HEADS + SEG, channels), F32)],
    )(x, tails, pick, in_all, in_bias, row(mixer_gain), row(mixer_shift), sw, short_bias)

    carried_b = carried.reshape(blocks, SEG, channels)
    incoming = lax.all_gather(carried_b, "ctx", axis=0, tiled=True)
    fh, fl, th, tl, sign = (jnp.asarray(t) for t in spectral_constants(SEG))
    skip = row(skip_gain)
    conv, gated, spec, filt = call(
        conv_fwd_kernel,
        (
            sds((total_rows, channels), F32),
            sds((total_rows, channels), BF16),
            sds((12, 2, SEG, channels), F32),
            sds((DEPTH + 1, 2, SEG, channels), F32),
        ),
        [SM] + [VM] * 11,
        [pltpu.VMEM((2 * SEG, channels), F32)],
    )(fwd_idx, carried_b, incoming[:4], incoming[4:8], filter_taps, mixed[0], skip, fh, fl, th, tl, sign)

    gated_all = line_gather(gated, tp_count, 1)
    residual, down_part, norm_part, grad_down, grad_up, grad_down_bias, grad_up_bias = call(
        feed_kernel,
        (
            sds((total_rows, width), F32),
            sds((total_rows, width), BF16),
            sds((total_rows, width), BF16),
            sds((hidden, width), F32),
            sds((width, hidden), F32),
            sds((1, width), F32),
            sds((1, hidden), F32),
        ),
        [VM] * 10,
    )(
        gated_all, out_all, x, g, row(out_bias), row(feed_gain), row(feed_shift), up_all, row(feed_up_bias), down_all
    )
    norm_sum = chain_sum(norm_part, 2)
    d_res, d_conv, d_long, d_zero, grad_out, grad_out_bias, grad_feed_gain, grad_feed_shift, grad_skip = call(
        feed_back_kernel,
        (
            sds((total_rows, width), F32),
            sds((total_rows, channels), F32),
            sds((total_rows, channels), BF16),
            sds((total_rows, channels), F32),
            sds((channels, width), F32),
            sds((1, width), F32),
            sds((1, width), F32),
            sds((1, width), F32),
            sds((1, channels), F32),
        ),
        [VM] * 9,
    )(residual, norm_sum, g, row(feed_gain), out_own, gated, mixed[0], conv, carried)

    d_long_b = d_long.reshape(blocks, SEG, channels)
    d_all = lax.all_gather(d_long_b, "ctx", axis=0, tiled=True)
    d_car, d_taps = call(
        conv_bwd_kernel,
        (sds((total_rows, channels), F32), sds((DEPTH * SEG, channels), F32)),
        [SM, SM, SM] + [VM] * 11,
        [
            pltpu.VMEM((16, 2, SEG, channels), F32),
            pltpu.VMEM((DEPTH + 1, 2, SEG, channels), F32),
            pltpu.VMEM((2 * SEG, channels), F32),
            pltpu.VMEM((8, 128), F32),
        ],
    )(fwd_idx, back_idx, leaf_sel, d_long_b, d_all, d_conv, spec, filt, skip, fh, fl, th, tl, sign)

    def top(v):
        return v.reshape(blocks, SEG, channels)[:, :2]

    heads = jnp.stack([top(d_zero), top(d_car) * top(mixed[2]), top(d_car) * top(mixed[1])], axis=1)
    heads = lax.all_gather(heads, "ctx", axis=0, tiled=True)
    heads = jnp.transpose(heads, (1, 0, 2, 3)).reshape(3, 2 * all_blocks, channels)
    proj_part, grad_in, grad_in_bias, grad_sw, grad_sb = call(
        mix_back_kernel,
        (
            sds((total_rows, width), BF16),
            sds((3, width, channels), F32),
            sds((3, channels), F32),
            sds((9, channels), F32),
            sds((3, channels), F32),
        ),
        [VM] * 10,
        [pltpu.VMEM((HEADS + SEG, channels), F32), pltpu.VMEM((HEADS + SEG, channels), F32)],
    )(d_zero, d_car, mixed, proj, head, heads, pick_child, sw, low, in_all)
    proj_sum = chain_sum(proj_part, 3)
    grad_x, grad_mixer_gain, grad_mixer_shift = call(
        norm_back_kernel,
        (sds((total_rows, width), F32), sds((1, width), F32), sds((1, width), F32)),
        [VM] * 4,
    )(x, proj_sum, d_res, row(mixer_gain))
    result = residual + chain_sum(down_part, 4).astype(F32) + feed_down_bias

    def share_rows(v):
        return v.reshape(owners, -1, 2 * width // 4)

    def share_cols(v):
        return jnp.transpose(v.reshape(v.shape[0], owners, -1), (1, 0, 2)).reshape(owners, -1, 2 * width // 4)

    packed = jnp.concatenate(
        [
            share_rows(jnp.transpose(grad_in, (1, 0, 2))).astype(BF16),
            share_cols(grad_out).astype(BF16),
            share_rows(grad_up).astype(BF16),
            share_cols(grad_down).astype(BF16),
        ],
        axis=1,
    )
    summed = matrix_sum(packed, 5)
    sizes = [width * 3 * channels, channels * width, width * hidden, hidden * width]
    marks = np.cumsum([0] + [s // owners // (2 * width // 4) for s in sizes])
    parts = [summed[marks[i] : marks[i + 1]] for i in range(4)]
    own_in = parts[0].reshape(width // owners, 3, channels)
    own_out = parts[1].reshape(channels, width // owners)
    own_up = parts[2].reshape(width // owners, hidden)
    own_down = parts[3].reshape(hidden, width // owners)

    g1, g1b, g2, g2b, gfreq, glast = taps_back(d_taps)
    glast = lax.psum_scatter(lax.psum(glast, "ctx"), "dp", scatter_dimension=0, tiled=True)
    share = 1.0 / tp_count
    vec = lax.psum(
        (grad_in_bias, grad_sw, grad_sb, grad_skip, grad_up_bias, grad_mixer_gain, grad_mixer_shift,
         grad_feed_gain, grad_feed_shift, grad_out_bias, grad_down_bias),
        ("dp", "ctx"),
    )
    g1, g1b, g2, g2b, gfreq = lax.psum((g1, g1b, g2, g2b, gfreq), ("dp", "ctx", "tp"))
    flat = lambda v: v.reshape(-1)
    return (
        result[None], grad_x[None], flat(vec[5]), flat(vec[6]), own_in, vec[0], vec[1].reshape(3, 3, channels),
        vec[2], g1, g1b, g2, g2b, gfreq, glast, flat(vec[3]), own_out, flat(vec[9]), flat(vec[7]), flat(vec[8]),
        own_up, flat(vec[4]), own_down, flat(vec[10]),
    )


def solution(mesh):
    in_specs = (
        P("dp", "ctx", None), P("dp", "ctx", None), P("dp", None), P(), P(), P("dp", None, "tp"), P(None, "tp"),
        P(None, None, "tp"), P(None, "tp"), P(), P(), P(), P(), P(), P("dp", "tp"), P("tp"), P("tp", "dp"), P(),
        P(), P(), P("dp", "tp"), P("tp"), P("tp", "dp"), P(),
    )
    out_specs = (
        P("dp", "ctx", None), P("dp", "ctx", None), P(), P(), P("dp", None, "tp"), P(None, "tp"),
        P(None, None, "tp"), P(None, "tp"), P(), P(), P(), P(), P(), P("dp", "tp"), P("tp"), P("tp", "dp"), P(),
        P(), P(), P("dp", "tp"), P("tp"), P("tp", "dp"), P(),
    )
    return jax.shard_map(body, mesh=mesh, in_specs=in_specs, out_specs=out_specs, check_vma=False)
```

time: 1180 us -> 594 us (0.50)
  waiting for transfers between devices: 624 us -> 22.3 us
  Pallas kernels: 0 us -> 354 us
  matrix products: 258 us -> 17.8 us
  other arithmetic: 111 us -> 21.1 us
  blocking collectives: 43.4 us -> 113 us
  local copies, waits for them, and re-layouts: 113 us -> 45.1 us
    psum x5 -> x0, waiting for transfers between devices: 584 us -> none  [the longest x3 394 us: over_tp(): return lax.psum(partial_sum, 'tp')]
    pallas_call x0 -> x12, Pallas kernels: none -> 354 us  [the longest x3 178 us: chain_sum(): call(chain_sum_kernel, sds((rows, width), BF16), [VM], [pltpu.VMEM((rows,...]
    dot_general x56 -> x5, matrix products: 250 us -> 7.18 us  [the longest x3 6.13 us: implicit_filter(): hidden = jnp.sin(frequency * (jnp.dot(hidden, w2, precision=EXACT) + b2))]
    psum x1 -> x3, blocking collectives: 13.1 us -> 74.2 us  [the longest x1 38.3 us: body(): lax.psum((g1, g1b, g2, g2b, gfreq), ('dp', 'ctx', 'tp'))]
    reduce_sum x21 -> x6, other arithmetic: 45 us -> 0.66 us  [the longest x5 0.57 us: tree_tables(): jnp.sum(parent_map[:, :, None] * ancestor[None, :, :], axis=1)]
    unnamed x247 -> x84, local copies, waits for them, and re-layouts: 38.4 us -> 7.02 us
    add x12 -> x6, other arithmetic: 27.6 us -> 0.05 us  [the longest x4 0.04 us: tree_tables(): jnp.eye(block_count, dtype=jnp.int32)]
    unnamed x16 -> x6, waiting for transfers between devices: 25.8 us -> 1.44 us
  transfers between devices with their start and end apart: 15 -> 6, of which waited for: 7 -> 1; matrix products, arithmetic and copies ran while one was open for 13% -> 9% of each run, Pallas kernels for 0% -> 39%
where the time goes in v1:
time: 594 us; the launch traced here: 590 us
  Pallas kernels  354 us (60%)
  blocking collectives  113 us (19%)
  local copies, waits for them, and re-layouts  45.1 us (8%)
  waiting for transfers between devices  22.3 us (4%)
  other arithmetic  21.1 us (4%)
  matrix products  17.8 us (3%)
  between operations  15.1 us (3%)
    pallas_call x3, Pallas kernels, chain_sum(): call(chain_sum_kernel, sds((rows, width), BF16), [VM], [pltpu.VMEM((rows,...  178 us
    pallas_call x1, Pallas kernels, line_gather(): call(line_gather_kernel, sds((count,) + x.shape, x.dtype), [VM], [pltpu.S...  44.4 us
    psum x1, blocking collectives, body(): lax.psum((g1, g1b, g2, g2b, gfreq), ('dp', 'ctx', 'tp'))  38.3 us
    pallas_call x1, Pallas kernels, matrix_sum(): call(matrix_sum_kernel, sds((rows, width), F32), [VM], [pltpu.VMEM((owner...  36.3 us
    psum x1, blocking collectives, body(): lax.psum((grad_in_bias, grad_sw, grad_sb, grad_skip, grad_up_bias, grad_m...  23.4 us
    pallas_call x1, Pallas kernels, body(): call(conv_bwd_kernel, (sds((total_rows, channels), F32), sds((DEPTH * SEG...  22.2 us
    all_gather x1, waiting for transfers between devices, body(): out_all = lax.all_gather(out_own, 'tp', axis=0)  20.8 us
    pallas_call x1, Pallas kernels, body(): call(feed_kernel, (sds((total_rows, width), F32), sds((total_rows, width)...  18.3 us
  transfers between devices with their start and end apart: 6, of which 1 were waited for; matrix products, arithmetic and copies ran while one was open for 9% of the time, Pallas kernels for 39%

profile of v1, /device:TPU:0, one launch (start us, length us, event | category | flops | bytes accessed | tf_op | source)
XLA Modules:
  0.0 589.5 jit_solution(17670194112073044038)
XLA Ops:
  8.8 1.3 reshape.416.gain_ref
  10.1 1.3 reshape.417.shift_ref
  12.1 1.3 reshape.418.sw_ref
  13.5 6.2 %all_gather.33 = bf16[16,2,768]{2,1,0:T(2,128)(2,1)S(1)} all-gather(bf16[4,2,768]{2,1,0:T(2,128)(2,1)S(1)} %slice.80), channel_id=1, replica_groups=mesh['dp'=2,'ctx'=4,'tp'=4] {'ctx'}, dimensions={0}, use_global_device_ids=true | all-gather | bytes 61440 | tf_op jit(solution)/shard_map/all_gather | solution.py:672
  20.3 1.2 copy.110
  21.6 16.5 %all_gather.34 = bf16[768,3,192]{2,0,1:T(8,128)(2,1)} all-gather(bf16[384,3,192]{2,0,1:T(8,128)(2,1)S(1)} %copy.110), channel_id=1, replica_groups=mesh['dp'=2,'ctx'=4,'tp'=4] {'dp'}, dimensions={0}, use_global_device_ids=true | all-gather | bytes 1327104 | tf_op jit(solution)/shard_map/all_gather | solution.py:671
  38.8 9.5 %shard_map.452 = (bf16[1024,768]{1,0:T(8,128)(2,1)}, f32[3,1024,192]{2,1,0:T(8,128)}, f32[3,4,8,192]{3,2,1,0:T(8,128)}, f32[3,1024,192]{2,1,0:T(8,128)}, bf16[1024,192]{1,0:T(8,128)(2,1)}) custom-call(bf16[1024,768]{1,0:T(8,128)(2,1)} %bitcast.58, bf16[32,768]{1,0:T(8,128)(2,1)} %reshape.415.xt_ref, f32[4,8,32]{2,1,0:T(8,128)} %fusion.24.pick_ref, ...), custom_call_target="tpu_custom_call" | custom-call | tf_op jit(solution)/shard_map/pallas_call | solution.py:729
  48.3 2.0 copy.111
  52.0 6.3 %all_gather.37.out_ref = bf16[192,768]{1,0:T(8,128)(2,1)} all-gather(bf16[192,384]{1,0:T(8,128)(2,1)S(1)} %copy-done.15), channel_id=1, replica_groups=mesh['dp'=2,'ctx'=4,'tp'=4] {'dp'}, dimensions={1}, use_global_device_ids=true | all-gather | bytes 442368 | tf_op jit(solution)/shard_map/all_gather | solution.py:674
  60.4 4.9 all_gather.36
  70.6 1.8 convolution_add_fusion
  73.2 3.5 convolution_multiply_fusion.taps_ref
  76.8 1.7 fusion.40
  78.5 1.2 fusion.41
  81.7 15.1 %shard_map.453 = (f32[1024,192]{1,0:T(8,128)}, bf16[1024,192]{1,0:T(8,128)(2,1)}, f32[12,2,256,192]{3,2,1,0:T(8,128)}, f32[7,2,256,192]{3,2,1,0:T(8,128)}) custom-call(s32[4,8]{1,0:T(4,128)} %copy.115.idx_ref, bf16[4,256,192]{2,1,0:T(8,128)(2,1)} %bitcast.68, bf16[4,256,192]{2,1,0:T(8,128)(2,1)} %copy.125.trunk_ref, bf16[4,256,192]{2,1,0:T(8,128)(2,1)} %copy.126.branch_ref, ...), custom_call_target="tpu_custom_call" | custom-call | tf_op jit(solution)/shard_map/pallas_call | solution.py:746
  96.8 44.4 %shard_map.454.gated_ref = bf16[4,1024,192]{2,1,0:T(8,128)(2,1)} custom-call(bf16[1024,192]{1,0:T(8,128)(2,1)} %get-tuple-element.60.x_ref.gated_ref), custom_call_target="tpu_custom_call" | custom-call | bytes 1572864 | tf_op jit(solution)/shard_map/pallas_call | solution.py:536
  141.4 20.8 %all-gather.15.cloned.1.call-done = bf16[768,768]{1,0:T(8,128)(2,1)} async-done(((bf16[192,768]{1,0:T(8,128)(2,1)}), bf16[768,768]{1,0:T(8,128)(2,1)}) %all-gather.15.cloned.1.call-update) | async-done | bytes 1179664 | tf_op jit(solution)/shard_map/all_gather | solution.py:675
  162.2 18.3 %shard_map.455 = (f32[1024,768]{1,0:T(8,128)}, bf16[1024,768]{1,0:T(8,128)(2,1)}, bf16[1024,768]{1,0:T(8,128)(2,1)}, f32[768,768]{1,0:T(8,128)}, f32[768,768]{1,...) custom-call(bf16[4,1024,192]{2,1,0:T(8,128)(2,1)} %shard_map.454.gated_ref, bf16[4,192,768]{2,1,0:T(8,128)(2,1)} %bitcast.71, ...), custom_call_target="tpu_custom_call" | custom-call | tf_op jit(solution)/shard_map/pallas_call | solution.py:759
  180.5 62.0 %shard_map.457.dn_ref = bf16[1024,768]{1,0:T(8,128)(2,1)} custom-call(bf16[1024,768]{1,0:T(8,128)(2,1)} %get-tuple-element.63.part_ref), custom_call_target="tpu_custom_call" | custom-call | bytes 6291456 | tf_op jit(solution)/shard_map/pallas_call | solution.py:498
  242.5 10.4 %shard_map.458 = (f32[1024,768]{1,0:T(8,128)}, f32[1024,192]{1,0:T(8,128)}, bf16[1024,192]{1,0:T(8,128)(2,1)}, f32[1024,192]{1,0:T(8,128)}, f32[192,768]{1,0:T(8...) custom-call(f32[1024,768]{1,0:T(8,128)} %get-tuple-element.61.resid_ref, ...), custom_call_target="tpu_custom_call" | custom-call | tf_op jit(solution)/shard_map/pallas_call | solution.py:775
  252.9 2.0 copy.116
  257.9 56.2 %shard_map.456 = bf16[1024,768]{1,0:T(8,128)(2,1)} custom-call(bf16[1024,768]{1,0:T(8,128)(2,1)} %get-tuple-element.62.part_ref), custom_call_target="tpu_custom_call" | custom-call | bytes 6291456 | tf_op jit(solution)/shard_map/pallas_call | solution.py:498
  314.2 1.8 convert_element_type.112
  316.0 1.2 convert_element_type.113
  317.2 1.8 convert_element_type.114
  319.0 1.5 copy.121
  320.5 2.5 copy.122
  325.0 3.4 add_bitcast_fusion
  328.4 3.7 copy.118.dall_ref
  332.1 22.2 %shard_map.459 = (f32[1024,192]{1,0:T(8,128)}, f32[1536,192]{1,0:T(8,128)}) custom-call(s32[4,8]{1,0:T(4,128)} %copy.115.idx_ref, s32[4,12]{1,0:T(4,128)} %pad_add_fusion.back_ref, f32[4,8]{1,0:T(4,128)} %fusion.30.leaf_ref, bf16[4,256,192]{2,1,0:T(8,128)(2,1)} %bitcast.70, bf16[16,256,192]{2,1,0:T(8,128)(2,1)} %copy.118.dall_ref, ...), custom_call_target="tpu_custom_call" | custom-call | tf_op jit(solution)/shard_map/pallas_call | solution.py:793
  354.4 4.7 fusion.1
  359.0 2.4 convolution_multiply_fusion.2
  361.4 2.5 multiply_reduce_fusion.1
  363.9 1.8 fusion.12
  366.6 5.3 all_gather.43
  372.6 13.3 %shard_map.460 = (bf16[1024,768]{1,0:T(8,128)(2,1)}, f32[3,768,192]{2,1,0:T(8,128)}, f32[3,192]{1,0:T(4,128)}, f32[9,192]{1,0:T(8,128)}, f32[3,192]{1,0:T(4,128)}) custom-call(f32[1024,192]{1,0:T(8,128)} %get-tuple-element.65.dzero_ref, f32[1024,192]{1,0:T(8,128)} %get-tuple-element.70.dcar_ref, f32[3,1024,192]{2,1,0:T(8,128)} %get-tuple-element.59.mixed_ref, ...), custom_call_target="tpu_custom_call" | custom-call | tf_op jit(solution)/shard_map/pallas_call | solution.py:811
  386.0 1.8 convert_bitcast_fusion
  388.8 2.2 convert_element_type.108
  391.0 3.2 pad_maximum_fusion.g_ref
  394.1 36.3 %shard_map.463 = f32[2304,384]{1,0:T(8,128)} custom-call(bf16[2,2304,384]{2,1,0:T(8,128)(2,1)} %pad_maximum_fusion.g_ref), custom_call_target="tpu_custom_call" | custom-call | bytes 14155776 | tf_op jit(solution)/shard_map/pallas_call | solution.py:616
  430.4 3.4 fusion.39
  435.1 59.6 %shard_map.461.dn_ref = bf16[1024,768]{1,0:T(8,128)(2,1)} custom-call(bf16[1024,768]{1,0:T(8,128)(2,1)} %get-tuple-element.74.part_ref), custom_call_target="tpu_custom_call" | custom-call | bytes 6291456 | tf_op jit(solution)/shard_map/pallas_call | solution.py:498
  494.8 7.0 %shard_map.462 = (f32[1024,768]{1,0:T(8,128)}, f32[1,768]{1,0:T(1,128)}, f32[1,768]{1,0:T(1,128)}) custom-call(bf16[1024,768]{1,0:T(8,128)(2,1)} %bitcast.60, bf16[1024,768]{1,0:T(8,128)(2,1)} %shard_map.461.dn_ref, f32[1024,768]{1,0:T(8,128)} %get-tuple-element.75.dres_ref, f32[1,768]{1,0:T(1,128)} %reshape.416.gain_ref), custom_call_target="tpu_custom_call" | custom-call | tf_op jit(solution)/shard_map/pallas_call | solution.py:824
  504.0 1.5 copy.123
  505.6 2.6 reshape.437
  508.2 23.4 %all-reduce.1 = (f32[768]{0:T(1024)}, f32[768]{0:T(1024)}, f32[3,192]{1,0:T(4,128)}, f32[3,3,192]{2,1,0:T(4,128)}, f32[3,192]{1,0:T(4,128)}, /*index=5*/f32[192]...) all-reduce(f32[768]{0:T(1024)S(1)} %reduce, ...), channel_id=1, replica_groups=mesh['dp'=2,'ctx'=4,'tp'=4] {'dp','ctx'}, use_global_device_ids=true, to_apply=%region_7.8 | all-reduce | flops 8448 | bytes 67584 | tf_op jit(solution)/shard_map/psum | solution.py:858
  531.6 38.3 %all-reduce = (f32[33,64]{1,0:T(8,128)}, f32[64]{0:T(128)}, f32[64,64]{1,0:T(8,128)}, f32[64]{0:T(128)}, f32[64]{0:T(128)}) all-reduce(f32[33,64]{1,0:T(8,128)S(1)} %fusion.10, f32[64]{0:T(128)S(1)} %copy-done.34, f32[64,64]{1,0:T(8,128)S(1)} %fusion.12, ...), channel_id=1, replica_groups=mesh['dp'=2,'ctx'=4,'tp'=4] {'dp','ctx','tp'}, use_global_device_ids=true, to_apply=%region_12.13 | all-reduce | flops 6400 | bytes 51200 | tf_op jit(solution)/shard_map/psum | solution.py:863
  569.9 12.5 %psum.136 = f32[32,192]{1,0:T(8,128)} all-reduce(f32[32,192]{1,0:T(8,128)} %reduce-scatter.2.cloned.1.call-done), channel_id=1, replica_groups=mesh['dp'=2,'ctx'=4,'tp'=4] {'ctx'}, use_global_device_ids=true, to_apply=%region_21.22 | all-reduce | flops 6144 | bytes 49152 | tf_op jit(solution)/shard_map/psum | solution.py:856
  (182 shorter events, 26.4 us)
Async XLA Ops:
  7.2 63.5 %copy-start = (f32[64,64]{1,0:T(8,128)S(1)}, f32[64,64]{1,0:T(8,128)}, u32[]{:S(2)}) copy-start(f32[64,64]{1,0:T(8,128)} %param.40) | copy-start | bytes 49156
  7.2 71.3 %all-gather.7.cloned.1.call-start = ((), (), s32[]{:S(2)}) async-start(), calls=%async_computation.1 | async-start | bytes 1966080 | tf_op jit(solution)/shard_map/all_gather | solution.py:743
  48.3 3.7 copy-start.15
  48.3 10.3 %copy-start.1 = (s32[1,16]{1,0:T(1,128)S(1)}, s32[1,16]{1,0:T(1,128)}, u32[]{:S(2)}) copy-start(s32[1,16]{1,0:T(1,128)} %param.31) | copy-start | bytes 196
  50.3 10.0 %copy-start.18 = (bf16[32,192]{1,0:T(8,128)(2,1)S(1)}, bf16[32,192]{1,0:T(8,128)(2,1)}, u32[]{:S(2)}) copy-start(bf16[32,192]{1,0:T(8,128)(2,1)} %param.43) | copy-start | bytes 36868
  50.3 15.0 %copy-start.24 = (f32[768]{0:T(1024)S(1)}, f32[768]{0:T(1024)}, u32[]{:S(2)}) copy-start(f32[768]{0:T(1024)} %param.47) | copy-start | bytes 9220
  50.3 15.5 %copy-start.25 = (f32[768]{0:T(1024)S(1)}, f32[768]{0:T(1024)}, u32[]{:S(2)}) copy-start(f32[768]{0:T(1024)} %param.46) | copy-start | bytes 9220
  50.3 16.1 %copy-start.26 = (f32[768]{0:T(1024)S(1)}, f32[768]{0:T(1024)}, u32[]{:S(2)}) copy-start(f32[768]{0:T(1024)} %param.48) | copy-start | bytes 9220
  50.3 16.7 %copy-start.27 = (f32[768]{0:T(1024)S(1)}, f32[768]{0:T(1024)}, u32[]{:S(2)}) copy-start(f32[768]{0:T(1024)} %param.50) | copy-start | bytes 9220
  50.4 19.0 %copy-start.17 = (f32[33,64]{1,0:T(8,128)S(1)}, f32[33,64]{1,0:T(8,128)}, u32[]{:S(2)}) copy-start(f32[33,64]{1,0:T(8,128)} %param.38) | copy-start | bytes 25348
  50.4 19.0 %copy-start.39 = (f32[64]{0:T(128)S(1)}, f32[64]{0:T(128)}, u32[]{:S(2)}) copy-start(f32[64]{0:T(128)} %param.39) | copy-start | bytes 772
  50.4 20.2 %copy-start.16 = (f32[64]{0:T(128)S(1)}, f32[64]{0:T(128)}, u32[]{:S(2)}) copy-start(f32[64]{0:T(128)} %param.42) | copy-start | bytes 772
  50.4 20.2 %copy-start.36 = (f32[64]{0:T(128)S(1)}, f32[64]{0:T(128)}, u32[]{:S(2)}) copy-start(f32[64]{0:T(128)} %param.41) | copy-start | bytes 772
  50.4 90.9 %all-gather.9.cloned.1.call-start = ((), (), s32[]{:S(2)}) async-start(), calls=%async_computation.2 | async-start | bytes 1769472 | tf_op jit(solution)/shard_map/all_gather | solution.py:676
  51.2 90.2 %all-gather.11.cloned.1.call-start = ((), (), s32[]{:S(2)}) async-start(), calls=%async_computation.3 | async-start | bytes 1769472 | tf_op jit(solution)/shard_map/all_gather | solution.py:677
  51.9 110.3 %all-gather.15.cloned.1.call-start = ((), (), s32[]{:S(2)}) async-start(), calls=%async_computation.5 | async-start | bytes 1474560 | tf_op jit(solution)/shard_map/all_gather | solution.py:675
  58.3 270.1 %all-gather.13.cloned.1.call-start = ((), (), s32[]{:S(2)}) async-start(), calls=%async_computation.4 | async-start | bytes 1966080 | tf_op jit(solution)/shard_map/all_gather | solution.py:792
  58.5 18.3 %copy-start.20 = (f32[192]{0:T(256)}, f32[192]{0:T(256)S(1)}, u32[]{:S(2)}) copy-start(f32[192]{0:T(256)S(1)} %multiply_add_fusion) | copy-start | bytes 2308
  68.7 0.6 copy-start.11
  68.7 1.2 copy-start.13
  69.3 7.4 %copy-start.4 = (f32[3,1024,192]{2,1,0:T(8,128)S(1)}, f32[3,1024,192]{2,1,0:T(8,128)}, u32[]{:S(2)}) copy-start(f32[3,1024,192]{2,1,0:T(8,128)} %get-tuple-element.59.mixed_ref) | copy-start | bytes 7077892
  69.9 0.8 copy-start.8
  72.5 0.8 copy-start.5
  255.0 314.9 %reduce-scatter.2.cloned.1.call-start = ((), (), s32[]{:S(2)}) async-start(), calls=%async_computation.6 | async-start | bytes 98304 | tf_op jit(solution)/shard_map/reduce_scatter | solution.py:856
  257.9 56.2 %copy-start.31 = (f32[1,768]{1,0:T(1,128)S(1)}, f32[1,768]{1,0:T(1,128)}, u32[]{:S(2)}) copy-start(f32[1,768]{1,0:T(1,128)} %get-tuple-element.91) | copy-start | bytes 9220
  257.9 56.2 %copy-start.29 = (f32[1,768]{1,0:T(1,128)S(1)}, f32[1,768]{1,0:T(1,128)}, u32[]{:S(2)}) copy-start(f32[1,768]{1,0:T(1,128)} %get-tuple-element.92) | copy-start | bytes 9220
  320.4 2.5 copy-start.32
  320.5 2.6 copy-start.30
  320.5 2.6 copy-start.28
  320.5 4.5 copy-start.3
  332.1 22.3 %copy-start.6 = (f32[1536,64]{0,1:T(8,128)S(1)}, f32[1536,64]{0,1:T(8,128)}, u32[]{:S(2)}) copy-start(f32[1536,64]{0,1:T(8,128)} %copy-done.5) | copy-start | bytes 1179652
  332.1 22.3 %copy-start.21 = (f32[192]{0:T(256)S(1)}, f32[192]{0:T(256)}, u32[]{:S(2)}) copy-start(f32[192]{0:T(256)} %copy-done.20) | copy-start | bytes 2308
  354.3 4.7 copy-start.7
  359.0 2.4 copy-start.9
  388.8 2.2 copy-start.10
  430.4 3.4 copy-start.12
  430.4 3.4 copy-start.14
  430.4 3.9 copy-start.2
  494.7 8.4 %copy-start.19 = (f32[9,192]{1,0:T(8,128)S(1)}, f32[9,192]{1,0:T(8,128)}, u32[]{:S(2)}) copy-start(f32[9,192]{1,0:T(8,128)} %get-tuple-element.84) | copy-start | bytes 20740
  494.8 8.4 %slice-start = ((f32[2304,384]{1,0:T(8,128)}), f32[576,384]{1,0:T(8,128)S(1)}, s32[]{:S(2)}) async-start(f32[2304,384]{1,0:T(8,128)} %shard_map.463), calls=%async_computation.7 | async-start | bytes 1769472 | tf_op jit(solution)/shard_map/slice | solution.py:849
  505.5 2.7 copy-start.37
  505.5 2.7 copy-start.38
  505.5 2.7 copy-start.22
  505.5 2.7 copy-start.23
  505.5 2.7 copy-start.35
  505.5 26.1 %copy-start.33 = (f32[64]{0:T(128)S(1)}, f32[64]{0:T(128)}, u32[]{:S(2)}) copy-start(f32[64]{0:T(128)} %get-tuple-element.188) | copy-start | bytes 772
  505.5 26.1 %copy-start.34 = (f32[64]{0:T(128)S(1)}, f32[64]{0:T(128)}, u32[]{:S(2)}) copy-start(f32[64]{0:T(128)} %get-tuple-element.216) | copy-start | bytes 772
Sparse Core Ops, SparseCore 0:
  50.5 21.1 all-gather.6
  73.3 22.7 all-gather.8
  97.7 22.7 all-gather.10
  121.9 40.2 all-gather.14
  255.1 18.2 all-gather.12
  365.9 9.6 reduce-scatter.1

commit v2 on v1

v2 whole, which is shorter than its diff:
```python
import functools
import math

import jax
import jax.numpy as jnp
import numpy as np
from jax import lax
from jax.experimental import pallas as pl
from jax.experimental.pallas import tpu as pltpu
from jax.sharding import PartitionSpec as P

SEG = 256
DEPTH = 6
HEADS = 8
EXACT = lax.Precision.HIGHEST
EPSILON = 1e-05
SLOW_RATE = -math.log(0.01) / 1.5
FAST_RATE = -math.log(0.01) / 0.3
SHIFT_FLOOR = 0.05
F32 = jnp.float32
BF16 = jnp.bfloat16
MESH = pl.DeviceIdType.MESH
VM = pl.BlockSpec(memory_space=pltpu.VMEM)
SM = pl.BlockSpec(memory_space=pltpu.SMEM)
LIMIT = 60 << 20


def sds(shape, dtype):
    return jax.ShapeDtypeStruct(shape, dtype)


HB = pl.BlockSpec(memory_space=pl.ANY)


def call(kernel, out_shape, in_specs, scratch=(), collective=None, flops=0, traffic=0, out_specs=None):
    many = isinstance(out_shape, (tuple, list))
    return pl.pallas_call(
        kernel,
        out_shape=out_shape,
        in_specs=in_specs,
        out_specs=out_specs or (tuple(VM for _ in out_shape) if many else VM),
        scratch_shapes=list(scratch),
        compiler_params=pltpu.CompilerParams(
            vmem_limit_bytes=LIMIT,
            collective_id=collective,
            has_side_effects=collective is not None,
        ),
        cost_estimate=pl.CostEstimate(flops=flops, bytes_accessed=traffic, transcendentals=0),
    )


def spectral_constants(block_len):
    freq = np.arange(block_len)[:, None]
    place = np.arange(block_len)[None, :]
    angle = ((2 * freq + 1) * place % (4 * block_len)) * (2.0 * math.pi / (4 * block_len))
    table = np.concatenate([np.cos(angle), -np.sin(angle)], axis=0).astype(np.float32)
    high = table.astype(jnp.bfloat16)
    low = (table - high.astype(np.float32)).astype(jnp.bfloat16)
    sign = np.where(np.arange(block_len) % 2 == 0, 1.0, -1.0).astype(np.float32)[:, None]
    return high, low, np.ascontiguousarray(high.T), np.ascontiguousarray(low.T), sign


def normalize(values):
    mean_value = jnp.mean(values, axis=-1, keepdims=True)
    centered = values - mean_value
    variance = jnp.mean(centered * centered, axis=-1, keepdims=True)
    scale = lax.rsqrt(variance + EPSILON)
    return centered * scale, scale


def split(values):
    high = values.astype(BF16)
    return high, (values - high.astype(F32)).astype(BF16)


def mm(lhs, rhs):
    return jnp.dot(lhs, rhs, preferred_element_type=F32)


def mm_nt(lhs, rhs):
    return lax.dot_general(lhs, rhs, (((1,), (1,)), ((), ())), preferred_element_type=F32)


def mm_tn(lhs, rhs):
    return lax.dot_general(lhs, rhs, (((0,), (0,)), ((), ())), preferred_element_type=F32)


def mm_split(high, low, values):
    v_high, v_low = split(values)
    return mm(high, v_high) + (mm(low, v_high) + mm(high, v_low))


def mix_in_kernel(
    x_ref, xt_ref, pick_ref, w_ref, bias_ref, gain_ref, shift_ref, sw_ref, sb_ref,
    low_ref, proj_ref, head_ref, mixed_ref, carried_ref, ext_ref,
):
    gain, shift = gain_ref[...], shift_ref[...]
    tails = normalize(xt_ref[...].astype(F32))[0] * gain + shift
    tails = tails.astype(BF16)
    tail_proj = [mm(tails, w_ref[g]) + bias_ref[g : g + 1] for g in range(3)]
    blocks = x_ref.shape[0] // SEG

    def one(s, unused):
        rows = pl.ds(pl.multiple_of(s * SEG, SEG), SEG)
        low = (normalize(x_ref[rows].astype(F32))[0] * gain + shift).astype(BF16)
        low_ref[rows] = low
        out = []
        for g in range(3):
            projected = mm(low, w_ref[g]) + bias_ref[g : g + 1]
            proj_ref[g, rows] = projected
            head = jnp.dot(pick_ref[s], tail_proj[g], precision=EXACT, preferred_element_type=F32)
            head_ref[g, s] = head
            ext_ref[g, 0:HEADS] = head
            ext_ref[g, HEADS : HEADS + SEG] = projected
            mixed = (
                sw_ref[3 * g : 3 * g + 1] * ext_ref[g, HEADS - 2 : HEADS - 2 + SEG]
                + sw_ref[3 * g + 1 : 3 * g + 2] * ext_ref[g, HEADS - 1 : HEADS - 1 + SEG]
                + sw_ref[3 * g + 2 : 3 * g + 3] * projected
                + sb_ref[g : g + 1]
            )
            mixed_ref[g, rows] = mixed
            out.append(mixed)
        carried_ref[rows] = (out[2] * out[1]).astype(BF16)
        return unused

    lax.fori_loop(0, blocks, one, 0)


FT = 64


def lineage(par_ref, block):
    out = []
    current = block
    for _ in range(DEPTH - 1):
        parent = par_ref[0, jnp.maximum(current, 0)]
        current = jnp.where(current >= 0, parent, -1)
        out.append(current)
    return out


def blend(dst, terms, rows, conj):
    re = im = None
    for a, b in terms:
        ar, ai = a[0, rows], a[1, rows]
        br, bi = b[0, rows], b[1, rows]
        if conj:
            pr, pi = ar * br + ai * bi, ar * bi - ai * br
        else:
            pr, pi = ar * br - ai * bi, ar * bi + ai * br
        re, im = (pr, pi) if re is None else (re + pr, im + pi)
    dst[0, rows] = re
    dst[1, rows] = im


def blend_all(dst, terms, conj):
    for t in range(SEG // FT):
        blend(dst, terms, slice(t * FT, (t + 1) * FT), conj)


def unpack_spectrum(th, tl, ref):
    high_re, low_re = split(ref[0])
    high_im, low_im = split(ref[1])
    a, b = slice(0, SEG), slice(SEG, 2 * SEG)
    return (
        mm(th[:, a], high_re) + mm(th[:, b], high_im)
        + (mm(tl[:, a], high_re) + mm(tl[:, b], high_im))
        + (mm(th[:, a], low_re) + mm(th[:, b], low_im))
    )


def filter_kernel(ft_ref, w1_ref, w2_ref, last_ref, freq_ref, net_ref, taps_ref):
    units, channels = last_ref.shape
    length = ft_ref.shape[1]
    tp = lax.axis_index("tp")
    width = channels * lax.axis_size("tp")
    exact = dict(precision=EXACT, preferred_element_type=F32)
    freq = freq_ref[...]
    pad = net_ref.shape[1] - units
    ones = jnp.where(lax.broadcasted_iota(jnp.int32, (pad, length), 0) == 0, 1.0, 0.0)
    net_ref[...] = jnp.zeros(net_ref.shape, F32)
    pre = jnp.dot(w1_ref[...], ft_ref[...], **exact)
    net_ref[0, 0:units] = pre
    net_ref[1, 0:units] = jnp.cos(freq * pre)
    net_ref[2, 0:units] = jnp.sin(freq * pre)
    net_ref[2, units:] = ones
    pre = jnp.dot(w2_ref[...], net_ref[2], **exact)
    net_ref[3, 0:units] = pre
    net_ref[4, 0:units] = jnp.cos(freq * pre)
    second = jnp.sin(freq * pre)
    net_ref[5, 0:units] = second
    raw = lax.dot_general(second, last_ref[...], (((0,), (0,)), ((), ())), **exact)
    time_pos = lax.broadcasted_iota(jnp.int32, (length, 1), 0).astype(F32) * (1.0 / (length - 1))
    channel = (lax.broadcasted_iota(jnp.int32, (1, channels), 1) + tp * channels).astype(F32)
    rate = SLOW_RATE + (FAST_RATE - SLOW_RATE) * channel * (1.0 / (width - 1))
    taps_ref[...] = raw * (jnp.exp(-time_pos * rate) + SHIFT_FLOOR)


def conv_fwd_kernel(
    par_ref, own_ref, all_ref, taps_ref, gate_ref, skip_ref,
    fh_ref, fl_ref, th_ref, tl_ref, sign_ref,
    conv_ref, gated_ref, spec_ref, filt_ref, acc_ref,
):
    blocks = own_ref.shape[0]
    ctx = lax.axis_index("ctx")
    fh, fl, th, tl = fh_ref[...], fl_ref[...], th_ref, tl_ref

    def source(j, unused):
        for base, ref, off in ((0, all_ref, 0), (4, all_ref, 4), (8, own_ref, 0)):
            part = ref[off + j]
            out = mm(fh, part) + mm(fl, part)
            spec_ref[base + j, 0] = out[:SEG]
            spec_ref[base + j, 1] = out[SEG:]
        return unused

    lax.fori_loop(0, blocks, source, 0)
    spec_ref[12] = jnp.zeros(spec_ref.shape[1:], F32)
    sign = sign_ref[...]
    last = None
    for j in range(DEPTH):
        part = taps_ref[j * SEG : (j + 1) * SEG]
        out = mm_split(fh, fl, part)
        re, im = out[:SEG], out[SEG:]
        if last is None:
            filt_ref[j, 0] = re
            filt_ref[j, 1] = im
        else:
            filt_ref[j, 0] = re - sign * last[1]
            filt_ref[j, 1] = im + sign * (last[0] - last[2])
        last = (re, im, part[0:1])

    def dest(s, unused):
        above = lineage(par_ref, ctx * blocks + s)
        places = [8 + s] + [jnp.where(a >= 0, a, 12) for a in above]
        blend_all(acc_ref, [(filt_ref.at[d], spec_ref.at[places[d]]) for d in range(DEPTH)], False)
        long_out = unpack_spectrum(th, tl, acc_ref) * (1.0 / SEG)
        place = pl.ds(pl.multiple_of(s * SEG, SEG), SEG)
        convolved = long_out + skip_ref[...] * own_ref[s].astype(F32)
        conv_ref[place] = convolved
        gated_ref[place] = (convolved * gate_ref[place]).astype(BF16)
        return unused

    lax.fori_loop(0, blocks, dest, 0)


def filter_features(length, bands, rows):
    positions = np.arange(length)
    time_pos = positions / (length - 1)
    freq = np.linspace(0.0001, bands - 1, bands)
    phases = (2.0 * math.pi / length * positions)[None, :] * freq[:, None]
    table = np.zeros((rows, length), np.float32)
    table[0] = time_pos
    table[1 : bands + 1] = np.cos(phases)
    table[bands + 1 : 2 * bands + 1] = -np.sin(phases)
    table[2 * bands + 1] = 1.0
    return table


def spot(**changes):
    base = {name: lax.axis_index(name) for name in ("dp", "ctx", "tp")}
    base.update(changes)
    return (base["dp"], base["ctx"], base["tp"])


def remote(src, dst, send, recv, where):
    return pltpu.make_async_remote_copy(
        src_ref=src, dst_ref=dst, send_sem=send, recv_sem=recv, device_id=where, device_id_type=MESH
    )


def greet(partners):
    barrier = pltpu.get_barrier_semaphore()
    for where in partners:
        pl.semaphore_signal(barrier, inc=1, device_id=where, device_id_type=MESH)
    pl.semaphore_wait(barrier, len(partners))


CHUNK = 32
PER = SEG // (2 * CHUNK)
LAG = 2


def chunk(c):
    return pl.ds(pl.multiple_of(c * CHUNK, CHUNK), CHUNK)


class LineSum:
    scratch_count = 11

    @staticmethod
    def scratch(rows, width):
        count = rows // CHUNK
        return [
            pltpu.VMEM((rows, width), BF16),
            pltpu.VMEM((rows // 2, width), BF16),
            pltpu.VMEM((rows // 2, width), BF16),
        ] + [pltpu.SemaphoreType.DMA((count,)) for _ in range(8)]

    def __init__(self, part, total, scratch):
        self.part, self.total = part, total
        self.end, self.mid, self.out = scratch[:3]
        self.sems = scratch[3:]
        self.pairs = part.shape[0] // (2 * CHUNK)
        tp = lax.axis_index("tp")
        self.inner = jnp.logical_and(tp > 0, tp < 3)
        self.outer = jnp.logical_not(self.inner)
        self.side = jnp.where(tp < 2, 0, 1)
        near = jnp.where(self.side == 0, 0, 3)
        far = jnp.where(self.side == 0, 1, 2)
        self.mate = spot(tp=jnp.where(self.inner, near, far))
        self.cross = spot(tp=3 - tp)

    def to_mid(self, c):
        return remote(self.part.at[chunk(c)], self.end.at[chunk(c)], self.sems[0].at[c], self.sems[1].at[c], self.mate)

    def to_cross(self, k):
        return remote(self.out.at[chunk(k)], self.mid.at[chunk(k)], self.sems[2].at[k], self.sems[3].at[k], self.cross)

    def final_end(self, c):
        at = self.total.at[chunk(c)]
        return remote(at, at, self.sems[4].at[c], self.sems[5].at[c], self.mate)

    def final_cross(self, c):
        at = self.total.at[chunk(c)]
        return remote(at, at, self.sems[6].at[c], self.sems[7].at[c], self.cross)

    def send_block(self, s):
        @pl.when(self.outer)
        def _():
            def one(i, unused):
                self.to_mid(s * 2 * PER + i).start()
                return unused

            lax.fori_loop(0, 2 * PER, one, 0)

    def step(self, k):
        pairs, side = self.pairs, self.side

        @pl.when(k < pairs)
        def _():
            other = 2 * k + 1 - side
            self.to_mid(2 * k).wait_recv()
            self.to_mid(2 * k + 1).wait_recv()
            self.out[chunk(k)] = (
                self.part[chunk(other)].astype(F32) + self.end[chunk(other)].astype(F32)
            ).astype(BF16)
            self.to_cross(k).start()

        j = k - LAG

        @pl.when(jnp.logical_and(j >= 0, j < pairs))
        def _():
            mine = 2 * j + side
            self.to_cross(j).wait_recv()
            self.total[chunk(mine)] = (
                self.part[chunk(mine)].astype(F32)
                + self.end[chunk(mine)].astype(F32)
                + self.mid[chunk(j)].astype(F32)
            ).astype(BF16)
            self.final_cross(mine).start()
            self.final_end(mine).start()

        i = k - 2 * LAG

        @pl.when(jnp.logical_and(i >= 0, i < pairs))
        def _():
            other = 2 * i + 1 - side
            self.final_cross(other).wait_recv()
            self.final_end(other).start()

    def steps(self, first, last):
        @pl.when(self.inner)
        def _():
            def one(k, unused):
                self.step(k)
                return unused

            lax.fori_loop(first, last, one, 0)

    def wait_block(self, s):
        @pl.when(self.outer)
        def _():
            def one(i, unused):
                self.final_end(s * 2 * PER + i).wait_recv()
                return unused

            lax.fori_loop(0, 2 * PER, one, 0)

    def drain(self):
        @pl.when(self.outer)
        def _():
            def one(c, unused):
                self.to_mid(c).wait_send()
                return unused

            lax.fori_loop(0, 2 * self.pairs, one, 0)

        @pl.when(self.inner)
        def _():
            def one(k, unused):
                mine, other = 2 * k + self.side, 2 * k + 1 - self.side
                self.to_cross(k).wait_send()
                self.final_cross(mine).wait_send()
                self.final_end(mine).wait_send()
                self.final_end(other).wait_send()
                return unused

            lax.fori_loop(0, self.pairs, one, 0)


def signal_all(partners):
    barrier = pltpu.get_barrier_semaphore()
    for where in partners:
        pl.semaphore_signal(barrier, inc=1, device_id=where, device_id_type=MESH)
    return barrier, len(partners)


def store_shares(stage_ref, tile, rows_per_tile, value):
    owners = stage_ref.shape[1]
    piece = stage_ref.shape[2]
    first = tile * rows_per_tile // piece
    for q in range(rows_per_tile // piece):
        owner, half = divmod(first + q, 2)
        stage_ref[half, owner] = value[q * piece : (q + 1) * piece].astype(BF16)


def feed_kernel(
    gated_ref, out_ref, x_ref, g_ref, ob_ref, gain_ref, shift_ref, up_ref, ub_ref, down_ref,
    mixed_ref, conv_ref, carried_ref,
    resid_ref, dpart_ref, dres_ref, dconv_ref, dzero_ref, dall_ref, gup_ref, gdown_ref, gout_ref,
    small_ref, gskip_ref,
    low_ref, hidden_ref, dpre_ref, npart_ref, nsum_ref, dmix_ref, own_ref, s_long, r_long, *line,
):
    groups = gated_ref.shape[0]
    width = x_ref.shape[1]
    blocks = x_ref.shape[0] // SEG
    tp, ctx = lax.axis_index("tp"), lax.axis_index("ctx")
    chain = LineSum(npart_ref, nsum_ref, line)
    barrier, count = signal_all([chain.mate, chain.cross] + [spot(ctx=lax.rem(ctx + i, 4)) for i in range(1, 4)])
    small_ref[...] = jnp.zeros(small_ref.shape, F32)
    gskip_ref[...] = jnp.zeros(gskip_ref.shape, F32)

    def core(s, unused):
        rows = pl.ds(pl.multiple_of(s * SEG, SEG), SEG)
        mixed = mm_nt(gated_ref[0, rows], out_ref[0])
        for z in range(1, groups):
            mixed = mixed + mm_nt(gated_ref[z, rows], out_ref[z])
        residual = x_ref[rows].astype(F32) + mixed + ob_ref[...]
        resid_ref[rows] = residual
        low = (normalize(residual)[0] * gain_ref[...] + shift_ref[...]).astype(BF16)
        low_ref[rows] = low
        pre = mm(low, up_ref[...]) + ub_ref[...]
        cdf = 0.5 * (1.0 + lax.erf(pre * math.sqrt(0.5)))
        hidden_ref[rows] = (pre * cdf).astype(BF16)
        slope = cdf + pre * (jnp.exp(-0.5 * pre * pre) * (1.0 / math.sqrt(2.0 * math.pi)))
        grad = g_ref[rows]
        d_pre = (mm(grad, down_ref[...]) * slope).astype(BF16)
        dpre_ref[rows] = d_pre
        npart_ref[rows] = mm_nt(d_pre, up_ref[...]).astype(BF16)
        small_ref[0:1] += jnp.sum(grad.astype(F32), axis=0, keepdims=True)
        small_ref[6:7] += jnp.sum(d_pre.astype(F32), axis=0, keepdims=True)

        @pl.when(s == 0)
        def _():
            pl.semaphore_wait(barrier, count)

        chain.send_block(s)
        return unused

    lax.fori_loop(0, blocks, core, 0)
    chain.steps(0, PER)

    def down(s, unused):
        rows = pl.ds(pl.multiple_of(s * SEG, SEG), SEG)
        dpart_ref[rows] = mm_nt(hidden_ref[rows], down_ref[...]).astype(BF16)
        return unused

    lax.fori_loop(0, blocks, down, 0)
    half = width // 2
    for t in range(2):
        columns = slice(t * half, (t + 1) * half)
        store_shares(gup_ref, t, half, mm_tn(low_ref[:, columns], dpre_ref[...]))
        store_shares(gdown_ref, t, half, mm_tn(g_ref[:, columns], hidden_ref[...]))

    def to_ctx(s, other):
        return remote(own_ref.at[s], dall_ref.at[ctx * blocks + s], s_long.at[other, s], r_long.at[ctx, s], spot(ctx=other))

    def back(s, unused):
        chain.steps((s + 1) * PER, (s + 2) * PER)
        chain.wait_block(s)
        rows = pl.ds(pl.multiple_of(s * SEG, SEG), SEG)
        xhat, scale = normalize(resid_ref[rows])
        dn = nsum_ref[rows].astype(F32)
        e = dn * gain_ref[...]
        d_res = g_ref[rows].astype(F32) + scale * (
            e - jnp.mean(e, axis=-1, keepdims=True) - xhat * jnp.mean(e * xhat, axis=-1, keepdims=True)
        )
        dres_ref[rows] = d_res
        small_ref[2:3] += jnp.sum(dn * xhat, axis=0, keepdims=True)
        small_ref[3:4] += jnp.sum(dn, axis=0, keepdims=True)
        d_mix = d_res.astype(BF16)
        dmix_ref[rows] = d_mix
        small_ref[1:2] += jnp.sum(d_mix.astype(F32), axis=0, keepdims=True)
        d_gated = mm(d_mix, out_ref[tp])
        d_conv = d_gated * mixed_ref[rows]
        dconv_ref[rows] = d_conv
        own_ref[s] = d_conv.astype(BF16)
        for other in range(3):
            @pl.when(other < ctx)
            def _():
                to_ctx(s, other).start()

        dzero_ref[rows] = d_gated * conv_ref[rows]
        gskip_ref[...] += jnp.sum(d_conv * carried_ref[rows].astype(F32), axis=0, keepdims=True)
        return unused

    lax.fori_loop(0, blocks, back, 0)
    for s in range(blocks):
        dall_ref[ctx * blocks + s] = own_ref[s]
    for t in range(2):
        columns = slice(t * half, (t + 1) * half)
        store_shares(gout_ref, t, half, mm_tn(dmix_ref[:, columns], gated_ref[tp]))
    chain.drain()
    for other in range(4):
        @pl.when(other < ctx)
        def _():
            for s in range(blocks):
                to_ctx(s, other).wait_send()

        @pl.when(other > ctx)
        def _():
            for s in range(blocks):
                at = dall_ref.at[other * blocks + s]
                remote(at, at, s_long.at[other, s], r_long.at[other, s], chain.mate).wait_recv()


def line_sum_kernel(part_ref, total_ref, *line):
    chain = LineSum(part_ref, total_ref, line)
    barrier, count = signal_all([chain.mate, chain.cross])
    pl.semaphore_wait(barrier, count)
    blocks = part_ref.shape[0] // SEG

    def send(s, unused):
        chain.send_block(s)
        return unused

    def wait(s, unused):
        chain.wait_block(s)
        return unused

    lax.fori_loop(0, blocks, send, 0)
    chain.steps(0, chain.pairs + 2 * LAG)
    lax.fori_loop(0, blocks, wait, 0)
    chain.drain()


def chain_sum(part, collective):
    rows, width = part.shape
    return call(line_sum_kernel, sds((rows, width), BF16), [VM], LineSum.scratch(rows, width), collective,
                traffic=rows * width * 8)(part)


def line_gather_kernel(x_ref, out_ref, local_sem, send_sem, recv_sem):
    tp = lax.axis_index("tp")
    count = out_ref.shape[0]
    greet([spot(tp=lax.rem(tp + i, count)) for i in range(1, count)])
    copies = [
        remote(x_ref, out_ref.at[tp], send_sem.at[i], recv_sem.at[tp], spot(tp=lax.rem(tp + i, count)))
        for i in range(1, count)
    ]
    for copy in copies:
        copy.start()
    own = pltpu.make_async_copy(x_ref, out_ref.at[tp], local_sem)
    own.start()
    for i in range(1, count):
        source = lax.rem(tp + i, count)
        remote(x_ref, out_ref.at[source], send_sem.at[0], recv_sem.at[source], spot()).wait_recv()
    for copy in copies:
        copy.wait_send()
    own.wait()


def line_gather(x, count, collective):
    return call(
        line_gather_kernel,
        sds((count,) + x.shape, x.dtype),
        [VM],
        [pltpu.SemaphoreType.DMA, pltpu.SemaphoreType.DMA((count,)), pltpu.SemaphoreType.DMA((count,))],
        collective,
        traffic=x.size * 2 * count,
    )(x)


class OwnerSum:
    scratch_count = 17

    @staticmethod
    def scratch(owners, shape):
        many = max(owners - 1, 1)
        return [
            pltpu.VMEM((owners,) + shape, BF16),
            pltpu.VMEM((owners,) + shape, BF16),
            pltpu.VMEM((many,) + shape, BF16),
            pltpu.VMEM(shape, BF16),
            pltpu.VMEM(shape, BF16),
            pltpu.SemaphoreType.DMA,
            pltpu.SemaphoreType.DMA,
            pltpu.SemaphoreType.DMA,
            pltpu.SemaphoreType.DMA((many,)),
            pltpu.SemaphoreType.DMA((many,)),
            pltpu.SemaphoreType.DMA,
            pltpu.SemaphoreType.DMA,
            pltpu.SemaphoreType.DMA,
            pltpu.SemaphoreType.DMA,
        ]

    def __init__(self, stage, out, scratch):
        self.stage, self.result = stage, out
        self.recv, self.keep, self.parts, self.y_own, self.y_in = scratch[:5]
        self.sems = scratch[5:]
        self.owners = stage.shape[1]
        self.dp, ctx = lax.axis_index("dp"), lax.axis_index("ctx")
        self.low = lax.rem(ctx, 2)
        self.mate = spot(ctx=ctx + 1 - 2 * self.low)
        self.across = spot(ctx=lax.rem(ctx + 2, 4))

    def load(self):
        return pltpu.make_async_copy(self.stage.at[self.low], self.keep, self.sems[0])

    def to_mate(self):
        return remote(self.stage.at[1 - self.low], self.recv, self.sems[1], self.sems[2], self.mate)

    def to_owner(self, i):
        owner = lax.rem(self.dp + i, self.owners)
        return remote(
            self.keep.at[owner], self.parts.at[self.owners - 1 - i], self.sems[3].at[i - 1],
            self.sems[4].at[self.owners - 1 - i], spot(dp=owner),
        )

    def from_owner(self, i):
        return remote(self.parts.at[i - 1], self.parts.at[i - 1], self.sems[3].at[i - 1], self.sems[4].at[i - 1], self.mate)

    def to_across(self):
        return remote(self.y_own, self.y_in, self.sems[5], self.sems[6], self.across)

    def to_back(self):
        at = self.result.at[self.low]
        return remote(at, at, self.sems[7], self.sems[8], self.mate)

    def begin(self):
        self.to_mate().start()
        self.load().start()

    def pair(self):
        self.load().wait()
        self.to_mate().wait_recv()
        for o in range(self.owners):
            self.keep[o] = (self.keep[o].astype(F32) + self.recv[o].astype(F32)).astype(BF16)
        for i in range(1, self.owners):
            self.to_owner(i).start()

    def own(self):
        total = self.keep[self.dp].astype(F32)
        for i in range(1, self.owners):
            self.from_owner(i).wait_recv()
            total = total + self.parts[i - 1].astype(F32)
        self.y_own[...] = total.astype(BF16)
        self.to_across().start()

    def cross(self):
        self.to_across().wait_recv()
        self.result[self.low] = self.y_own[...].astype(F32) + self.y_in[...].astype(F32)
        self.to_back().start()

    def finish(self):
        self.to_mate().wait_send()
        for i in range(1, self.owners):
            self.to_owner(i).wait_send()
        self.to_across().wait_send()
        self.to_back().wait_send()
        at = self.result.at[1 - self.low]
        remote(at, at, self.sems[7], self.sems[8], self.mate).wait_recv()


class SmallSum:
    @staticmethod
    def scratch(count, shape):
        return [
            pltpu.VMEM((count,) + shape, F32),
            pltpu.SemaphoreType.DMA((count,)),
            pltpu.SemaphoreType.DMA((count,)),
        ]

    def __init__(self, axis, scratch):
        self.axis = axis
        self.slots, self.send, self.recv = scratch
        self.count = self.slots.shape[0]
        self.me = lax.axis_index(axis)

    def copy(self, i):
        at = self.slots.at[self.me]
        other = lax.rem(self.me + i, self.count)
        return remote(at, at, self.send.at[i], self.recv.at[self.me], spot(**{self.axis: other}))

    def start(self, value):
        self.slots[self.me] = value
        for i in range(1, self.count):
            self.copy(i).start()

    def total(self):
        for i in range(1, self.count):
            other = lax.rem(self.me + i, self.count)
            at = self.slots.at[other]
            remote(at, at, self.send.at[i], self.recv.at[other], spot(**{self.axis: lax.rem(self.me + i, self.count)})).wait_recv()
        out = self.slots[0]
        for i in range(1, self.count):
            out = out + self.slots[i]
        return out

    def finish(self):
        for i in range(1, self.count):
            self.copy(i).wait_send()


def back_kernel(
    par_ref, dall_ref, dconv_ref, dzero_ref, mixed_ref, low_ref, w_ref, x_ref, dpart_ref,
    fh_ref, fl_ref, th_ref, tl_ref, sign_ref, sw_ref, skip_ref, mgain_ref, fbias_ref,
    ft_ref, w2_ref, last_ref, freq_ref, small_ref, gskip_ref,
    resid_hbm, dres_hbm, proj_hbm, head_hbm, spec_hbm, filt_hbm, net_hbm, sup_hbm, sdown_hbm, sout_hbm,
    result_hbm, gradx_hbm, oup_ref, odown_ref, oout_ref, oin_ref, va_ref, vd_ref, vl_ref, vf_ref,
    yown_ref, dcar_ref, dtaps_ref, stage_in, ppart_ref, dsum_ref, psum_ref, hd_ref, s_hd, r_hd, local, *rest,
):
    width = x_ref.shape[1]
    channels = dconv_ref.shape[1]
    total_rows = x_ref.shape[0]
    blocks = total_rows // SEG
    owners = sup_hbm.shape[1]
    ctx, tp, dp = lax.axis_index("ctx"), lax.axis_index("tp"), lax.axis_index("dp")
    rest = list(rest)

    def take(n):
        out = rest[:n]
        del rest[:n]
        return out

    down = LineSum(dpart_ref, dsum_ref, take(11))
    proj = LineSum(ppart_ref, psum_ref, take(11))
    early = [OwnerSum(s, o, take(14)) for s, o in ((sup_hbm, oup_ref), (sdown_hbm, odown_ref), (sout_hbm, oout_ref))]
    late = OwnerSum(stage_in, oin_ref, take(14))
    a_ctx, a_dp = SmallSum("ctx", take(3)), SmallSum("dp", take(3))
    d_ctx, d_dp, d_tp = SmallSum("ctx", take(3)), SmallSum("dp", take(3)), SmallSum("tp", take(3))
    l_ctx, l_dp = SmallSum("ctx", take(3)), SmallSum("dp", take(3))
    f_ctx, f_dp, f_tp = SmallSum("ctx", take(3)), SmallSum("dp", take(3)), SmallSum("tp", take(3))

    partners = [spot(tp=lax.rem(tp + i, 4)) for i in range(1, 4)]
    partners += [spot(ctx=lax.rem(ctx + i, 4)) for i in range(1, 4)]
    partners += [spot(dp=lax.rem(dp + i, owners)) for i in range(1, owners)]
    barrier, count = signal_all(partners)
    pl.semaphore_wait(barrier, count)
    for s in range(blocks):
        down.send_block(s)
    for job in early:
        job.begin()
    fh, fl, th, tl = fh_ref[...], fl_ref[...], th_ref, tl_ref
    scale = 1.0 / SEG

    def put(dst, value):
        dst[0] = value[:SEG] * scale
        dst[1] = value[SEG:] * scale

    def conv_inputs(filt_ref, more_ref, acc_ref):
        load = pltpu.make_async_copy(filt_hbm, filt_ref, local.at[0])
        load.start()

        def transform(s, unused):
            part = dall_ref[ctx * blocks + s]
            put(yown_ref.at[s], mm(fh, part) + mm(fl, part))
            return unused

        lax.fori_loop(0, blocks, transform, 0)
        load.wait()

        def leaf_sum(match):
            total = None
            for leaf in range(8, 16):
                term = jnp.where(match(leaf), 1.0, 0.0) * dall_ref[leaf].astype(F32)
                total = term if total is None else total + term
            return total

        def from_leaf(b):
            return lambda leaf: par_ref[0, leaf] == b

        def finish(s, terms):
            blend_all(acc_ref, terms, True)
            place = pl.ds(pl.multiple_of(s * SEG, SEG), SEG)
            dcar_ref[place] = unpack_spectrum(th, tl, acc_ref) + skip_ref[...] * dconv_ref[place]

        @pl.when(ctx == 0)
        def _():
            def gather(k, unused):
                p = k + 1
                total = None
                for b in range(4, 8):
                    term = jnp.where(par_ref[0, b] == p, 1.0, 0.0) * dall_ref[b].astype(F32)
                    total = term if total is None else total + term
                put(more_ref.at[k], mm_split(fh, fl, total))
                total = leaf_sum(lambda leaf: par_ref[0, par_ref[0, leaf]] == p)
                put(more_ref.at[3 + k], mm_split(fh, fl, total))
                return unused

            lax.fori_loop(0, 3, gather, 0)
            for a in range(4):
                terms = [(filt_ref.at[s - a], yown_ref.at[s]) for s in range(a, 4)]
                for p in range(max(a, 1), 4):
                    terms.append((filt_ref.at[p - a + 1], more_ref.at[p - 1]))
                    terms.append((filt_ref.at[p - a + 2], more_ref.at[p + 2]))
                finish(a, terms)

        @pl.when(ctx == 1)
        def _():
            def one(b, unused):
                put(more_ref.at[0], mm_split(fh, fl, leaf_sum(from_leaf(b + 4))))
                finish(b, [(filt_ref.at[0], yown_ref.at[b]), (filt_ref.at[1], more_ref.at[0])])
                return unused

            lax.fori_loop(0, 4, one, 0)

        @pl.when(ctx > 1)
        def _():
            def one(b, unused):
                finish(b, [(filt_ref.at[0], yown_ref.at[b])])
                return unused

            lax.fori_loop(0, 4, one, 0)

    pl.run_scoped(
        conv_inputs,
        pltpu.VMEM((DEPTH, 2, SEG, channels), F32),
        pltpu.VMEM((6, 2, SEG, channels), F32),
        pltpu.VMEM((2, SEG, channels), F32),
    )

    def to_ctx(i):
        at = hd_ref.at[pl.ds(ctx * blocks, blocks)]
        return remote(at, at, s_hd.at[i], r_hd.at[ctx], spot(ctx=lax.rem(ctx + i, 4)))

    for s in range(blocks):
        top = slice(s * SEG, s * SEG + HEADS)
        d_car = dcar_ref[top]
        rows = [dzero_ref[top], d_car * mixed_ref[1, top], d_car * mixed_ref[0, top]]
        for g in range(3):
            hd_ref[ctx * blocks + s, 2 * g : 2 * g + 2] = rows[g][0:2]
        hd_ref[ctx * blocks + s, 6:8] = jnp.zeros((2, channels), F32)
    for i in range(1, 4):
        to_ctx(i).start()
    down.steps(0, 3)
    for job in early:
        job.pair()

    def conv_filters(spec_ref, dfilt_ref):
        load = pltpu.make_async_copy(spec_hbm, spec_ref, local.at[0])
        load.start()
        load.wait()

        @pl.when(ctx == 0)
        def _():
            for d in range(4):
                blend_all(dfilt_ref.at[d], [(spec_ref.at[8 + s - d], yown_ref.at[s]) for s in range(d, 4)], True)
            dfilt_ref[4:6] = jnp.zeros((2, 2, SEG, channels), F32)

        @pl.when(ctx > 0)
        def _():
            places = []
            for s in range(blocks):
                above = lineage(par_ref, ctx * blocks + s)
                places.append([8 + s] + [jnp.where(a >= 0, a, 12) for a in above])
            for d in range(DEPTH):
                terms = [(spec_ref.at[places[s][d]], yown_ref.at[s]) for s in range(blocks)]
                blend_all(dfilt_ref.at[d], terms, True)

        down.steps(3, 6)
        sign = sign_ref[...]
        first_row = lax.broadcasted_iota(jnp.int32, (SEG, 1), 0) == 0
        for j in range(DEPTH):
            fix = None
            if j + 1 < DEPTH:
                nr, ni = dfilt_ref[j + 1, 0], dfilt_ref[j + 1, 1]
                fix = jnp.sum(sign * ni, axis=0, keepdims=True)
                dfilt_ref[j, 0] = dfilt_ref[j, 0] + sign * ni
                dfilt_ref[j, 1] = dfilt_ref[j, 1] - sign * nr
            taps = unpack_spectrum(th, tl, dfilt_ref.at[j])
            if fix is not None:
                taps = jnp.where(first_row, taps - fix, taps)
            dtaps_ref[j * SEG : (j + 1) * SEG] = taps

    pl.run_scoped(
        conv_filters,
        pltpu.VMEM((13, 2, SEG, channels), F32),
        pltpu.VMEM((DEPTH, 2, SEG, channels), F32),
    )
    down.steps(6, 9)

    va_ref[...] = jnp.zeros(va_ref.shape, F32)
    vd_ref[...] = small_ref[...]
    va_ref[15:16] = gskip_ref[...]
    for i in range(1, 4):
        other = lax.rem(ctx + i, 4)
        at = hd_ref.at[pl.ds(other * blocks, blocks)]
        remote(at, at, s_hd.at[i], r_hd.at[other], spot(ctx=other)).wait_recv()

    def mix_back(dp_ref, ext_ref, dm_ref, pin_ref, hin_ref):
        load_heads = pltpu.make_async_copy(head_hbm, hin_ref, local.at[1])
        load_heads.start()

        def fetch(s):
            rows = pl.ds(pl.multiple_of(s * SEG, SEG), SEG)
            return pltpu.make_async_copy(proj_hbm.at[:, rows], pin_ref.at[lax.rem(s, 2)], local.at[2 + lax.rem(s, 2)])

        fetch(0).start()
        load_heads.wait()

        def one(s, unused):
            rows = pl.ds(pl.multiple_of(s * SEG, SEG), SEG)
            slot = lax.rem(s, 2)
            fetch(s).wait()

            @pl.when(s + 1 < blocks)
            def _():
                fetch(s + 1).start()

            mine = ctx * blocks + s
            child = None
            for b in range(1, 16):
                term = jnp.where(par_ref[0, b] == mine, 1.0, 0.0) * hd_ref[b]
                child = term if child is None else child + term
            part = None
            for g in range(3):
                if g == 0:
                    dm = dzero_ref[rows]
                else:
                    dm = dcar_ref[rows] * mixed_ref[2 - g, rows]
                ext_ref[0:HEADS] = hin_ref[g, s]
                ext_ref[HEADS : HEADS + SEG] = pin_ref[slot, g]
                for k in range(3):
                    piece = ext_ref[HEADS - 2 + k : HEADS - 2 + k + SEG]
                    va_ref[3 * g + k : 3 * g + k + 1] += jnp.sum(piece * dm, axis=0, keepdims=True)
                va_ref[12 + g : 13 + g] += jnp.sum(dm, axis=0, keepdims=True)
                dm_ref[0:SEG] = dm
                dm_ref[SEG : SEG + 2] = child[2 * g : 2 * g + 2]
                d_proj = (
                    sw_ref[3 * g + 2 : 3 * g + 3] * dm
                    + sw_ref[3 * g + 1 : 3 * g + 2] * dm_ref[1 : 1 + SEG]
                    + sw_ref[3 * g : 3 * g + 1] * dm_ref[2 : 2 + SEG]
                ).astype(BF16)
                dp_ref[g, rows] = d_proj
                va_ref[9 + g : 10 + g] += jnp.sum(d_proj.astype(F32), axis=0, keepdims=True)
                term = mm_nt(d_proj, w_ref[g])
                part = term if part is None else part + term
            ppart_ref[rows] = part.astype(BF16)
            proj.send_block(s)
            xhat = normalize(x_ref[rows].astype(F32))[0]
            vd_ref[4:5] += jnp.sum(part * xhat, axis=0, keepdims=True)
            vd_ref[5:6] += jnp.sum(part, axis=0, keepdims=True)
            down.steps(9 + s, 10 + s)
            return unused

        lax.fori_loop(0, blocks, one, 0)
        half = width // 2
        piece = stage_in.shape[3]
        for t in range(2):
            columns = slice(t * half, (t + 1) * half)
            for g in range(3):
                value = mm_tn(low_ref[:, columns], dp_ref[g])
                first = t * half // piece
                for q in range(half // piece):
                    owner, side = divmod(first + q, 2)
                    stage_in[side, owner, g] = value[q * piece : (q + 1) * piece].astype(BF16)

    pl.run_scoped(
        mix_back,
        pltpu.VMEM((3, total_rows, channels), BF16),
        pltpu.VMEM((HEADS + SEG, channels), F32),
        pltpu.VMEM((HEADS + SEG, channels), F32),
        pltpu.VMEM((2, 3, SEG, channels), F32),
        pltpu.VMEM((3, blocks, HEADS, channels), F32),
    )
    late.begin()
    for job in early:
        job.own()
    down.steps(13, 15)

    def filter_back(net_ref):
        load = pltpu.make_async_copy(net_hbm, net_ref, local.at[1])
        load.start()
        time_pos = lax.broadcasted_iota(jnp.int32, (DEPTH * SEG, 1), 0).astype(F32) * (1.0 / (DEPTH * SEG - 1))
        channel = (lax.broadcasted_iota(jnp.int32, (1, channels), 1) + tp * channels).astype(F32)
        rate = SLOW_RATE + (FAST_RATE - SLOW_RATE) * channel * (1.0 / (width - 1))
        d_raw = dtaps_ref[...] * (jnp.exp(-time_pos * rate) + SHIFT_FLOOR)
        load.wait()
        exact = dict(precision=EXACT, preferred_element_type=F32)
        nt = (((1,), (1,)), ((), ()))
        units = last_ref.shape[0]
        freq = freq_ref[...]
        l_ctx.start(jnp.dot(net_ref[5, 0:units], d_raw, **exact))
        d_two = lax.dot_general(last_ref[...], d_raw, nt, **exact)
        s_two = d_two * net_ref[4, 0:units]
        p_two = s_two * freq
        g_two = lax.dot_general(p_two, net_ref[2], nt, **exact)
        d_one = lax.dot_general(w2_ref[...], p_two, (((0,), (0,)), ((), ())), **exact)[0:units]
        s_one = d_one * net_ref[1, 0:units]
        p_one = s_one * freq
        g_one = lax.dot_general(p_one, ft_ref[...], nt, **exact)
        g_freq = jnp.sum(s_one * net_ref[0, 0:units] + s_two * net_ref[3, 0:units], axis=1, keepdims=True)
        vf_ref[...] = jnp.zeros(vf_ref.shape, F32)
        vf_ref[0, :, 0 : g_one.shape[1]] = g_one
        vf_ref[1, :, 0 : g_two.shape[1]] = g_two
        vf_ref[2, :, 0:1] = g_freq
        f_ctx.start(vf_ref[...])

    pl.run_scoped(filter_back, pltpu.VMEM(net_hbm.shape, F32))
    a_ctx.start(va_ref[...])
    d_ctx.start(vd_ref[...])
    late.pair()
    down.steps(15, 17)
    for job in early:
        job.cross()
    for one, two in ((a_ctx, a_dp), (d_ctx, d_dp), (l_ctx, l_dp), (f_ctx, f_dp)):
        two.start(one.total())
    down.steps(17, 20)
    late.own()

    def results(in_ref, out_ref):
        def fetch(src, s):
            rows = pl.ds(pl.multiple_of(s * SEG, SEG), SEG)
            return pltpu.make_async_copy(src.at[rows], in_ref.at[lax.rem(s, 2)], local.at[lax.rem(s, 2)])

        def flush(dst, s):
            rows = pl.ds(pl.multiple_of(s * SEG, SEG), SEG)
            return pltpu.make_async_copy(out_ref.at[s], dst.at[rows], local.at[4 + s])

        fetch(resid_hbm, 0).start()

        def one(s, unused):
            rows = pl.ds(pl.multiple_of(s * SEG, SEG), SEG)
            fetch(resid_hbm, s).wait()

            @pl.when(s + 1 < blocks)
            def _():
                fetch(resid_hbm, s + 1).start()

            proj.steps(s, s + 1)
            down.wait_block(s)
            out_ref[s] = in_ref[lax.rem(s, 2)] + dsum_ref[rows].astype(F32) + fbias_ref[...]
            flush(result_hbm, s).start()
            return unused

        lax.fori_loop(0, blocks, one, 0)
        va_ref[...] = a_dp.total()
        vl_ref[...] = l_dp.total()
        sums = d_dp.total()
        vd_ref[...] = sums
        d_tp.start(sums)
        f_tp.start(f_dp.total())
        fetch(dres_hbm, 0).start()

        def two(s, unused):
            rows = pl.ds(pl.multiple_of(s * SEG, SEG), SEG)
            fetch(dres_hbm, s).wait()

            @pl.when(s + 1 < blocks)
            def _():
                fetch(dres_hbm, s + 1).start()

            xhat, spread = normalize(x_ref[rows].astype(F32))
            proj.steps((s + 1) * PER, (s + 2) * PER)
            proj.wait_block(s)
            e = psum_ref[rows].astype(F32) * mgain_ref[...]
            flush(result_hbm, s).wait()
            out_ref[s] = in_ref[lax.rem(s, 2)] + spread * (
                e - jnp.mean(e, axis=-1, keepdims=True) - xhat * jnp.mean(e * xhat, axis=-1, keepdims=True)
            )
            flush(gradx_hbm, s).start()

            @pl.when(s == 0)
            def _():
                late.cross()

            return unused

        lax.fori_loop(0, blocks, two, 0)
        for s in range(blocks):
            flush(gradx_hbm, s).wait()

    pl.run_scoped(
        results,
        pltpu.VMEM((2, SEG, width), F32),
        pltpu.VMEM((blocks, SEG, width), F32),
    )
    vd_ref[4:6] = d_tp.total()[4:6]
    vf_ref[...] = f_tp.total()
    for job in (a_ctx, a_dp, d_ctx, d_dp, d_tp, l_ctx, l_dp, f_ctx, f_dp, f_tp):
        job.finish()
    for job in early + [late]:
        job.finish()
    for i in range(1, 4):
        to_ctx(i).wait_send()
    down.drain()
    proj.drain()


def body(
    block_in, out_grad, parents, mixer_gain, mixer_shift, in_proj, in_bias, short_weight, short_bias,
    filter_one, filter_one_bias, filter_two, filter_two_bias, filter_freq, filter_out, skip_gain,
    out_proj, out_bias, feed_gain, feed_shift, feed_up, feed_up_bias, feed_down, feed_down_bias,
):
    x = block_in[0]
    g = out_grad[0]
    total_rows, width = x.shape
    channels = skip_gain.shape[0]
    blocks = total_rows // SEG
    hidden = feed_up.shape[1]
    tp_count = lax.axis_size("tp")
    tp_index = lax.axis_index("tp")
    owners = lax.axis_size("dp")
    first = lax.axis_index("ctx") * blocks
    all_blocks = parents.shape[1]

    in_all = jnp.transpose(lax.all_gather(in_proj, "dp", axis=0, tiled=True), (1, 0, 2))
    tails = lax.all_gather(x.reshape(blocks, SEG, width)[:, SEG - 2 :], "ctx", axis=0, tiled=True)
    tails = tails.reshape(2 * all_blocks, width)
    out_own = lax.all_gather(out_proj.T, "dp", axis=0, tiled=True)
    out_all = lax.all_gather(out_own, "tp", axis=0)
    up_all = lax.all_gather(feed_up, "dp", axis=0, tiled=True)
    down_all = lax.all_gather(feed_down.T, "dp", axis=0, tiled=True)
    last_all = lax.all_gather(filter_out, "dp", axis=0, tiled=True)

    own_par = lax.dynamic_slice_in_dim(parents[0], first, blocks, 0)
    row_id = jnp.arange(HEADS)
    tail_id = jnp.arange(2 * all_blocks)
    pick = (
        (tail_id[None, None, :] == (2 * own_par[:, None] + row_id[None, :] - (HEADS - 2))[:, :, None])
        & (row_id[None, :, None] >= HEADS - 2)
        & (own_par[:, None, None] >= 0)
    ).astype(F32)
    units, features = filter_one.shape[1], filter_one.shape[0]
    feat_rows = 40
    ft = jnp.asarray(filter_features(DEPTH * SEG, (features - 1) // 2, feat_rows))
    w1 = jnp.concatenate(
        [filter_one.T, filter_one_bias[:, None], jnp.zeros((units, feat_rows - features - 1), F32)], axis=1
    )
    w2 = jnp.concatenate([filter_two.T, filter_two_bias[:, None], jnp.zeros((units, 7), F32)], axis=1)
    last = last_all.astype(F32)
    freq = filter_freq[:, None]
    net, filter_taps = call(
        filter_kernel,
        (sds((6, units + 8, DEPTH * SEG), F32), sds((DEPTH * SEG, channels), F32)),
        [VM] * 5,
    )(ft, w1, w2, last, freq)

    row = lambda v: v.reshape(1, -1)
    sw = short_weight.reshape(9, channels)
    low, proj, head, mixed, carried = call(
        mix_in_kernel,
        (
            sds((total_rows, width), BF16),
            sds((3, total_rows, channels), F32),
            sds((3, blocks, HEADS, channels), F32),
            sds((3, total_rows, channels), F32),
            sds((total_rows, channels), BF16),
        ),
        [VM] * 9,
        [pltpu.VMEM((3, HEADS + SEG, channels), F32)],
    )(x, tails, pick, in_all, in_bias, row(mixer_gain), row(mixer_shift), sw, short_bias)

    carried_b = carried.reshape(blocks, SEG, channels)
    incoming = lax.all_gather(carried_b, "ctx", axis=0, tiled=True)
    fh, fl, th, tl, sign = (jnp.asarray(t) for t in spectral_constants(SEG))
    skip = row(skip_gain)
    conv, gated, spec, filt = call(
        conv_fwd_kernel,
        (
            sds((total_rows, channels), F32),
            sds((total_rows, channels), BF16),
            sds((13, 2, SEG, channels), F32),
            sds((DEPTH, 2, SEG, channels), F32),
        ),
        [SM] + [VM] * 10,
        [pltpu.VMEM((2, SEG, channels), F32)],
    )(parents, carried_b, incoming, filter_taps, mixed[0], skip, fh, fl, th, tl, sign)

    gated_all = line_gather(gated, tp_count, 1)
    piece = width // owners // 2
    (residual, down_part, d_res, d_conv, d_zero, d_all, stage_up, stage_down, stage_out,
     small, grad_skip) = call(
        feed_kernel,
        (
            sds((total_rows, width), F32),
            sds((total_rows, width), BF16),
            sds((total_rows, width), F32),
            sds((total_rows, channels), F32),
            sds((total_rows, channels), F32),
            sds((all_blocks, SEG, channels), BF16),
            sds((2, owners, piece, hidden), BF16),
            sds((2, owners, piece, hidden), BF16),
            sds((2, owners, piece, channels), BF16),
            sds((8, width), F32),
            sds((1, channels), F32),
        ),
        [VM] * 13,
        [
            pltpu.VMEM((total_rows, width), BF16),
            pltpu.VMEM((total_rows, hidden), BF16),
            pltpu.VMEM((total_rows, hidden), BF16),
            pltpu.VMEM((total_rows, width), BF16),
            pltpu.VMEM((total_rows, width), BF16),
            pltpu.VMEM((total_rows, width), BF16),
            pltpu.VMEM((blocks, SEG, channels), BF16),
            pltpu.SemaphoreType.DMA((4, blocks)),
            pltpu.SemaphoreType.DMA((4, blocks)),
        ]
        + LineSum.scratch(total_rows, width),
        2,
    )(
        gated_all, out_all, x, g, row(out_bias), row(feed_gain), row(feed_shift), up_all, row(feed_up_bias), down_all,
        mixed[0], conv, carried,
    )
    flat_shapes = [(piece, hidden), (piece, hidden), (piece, channels), (3, piece, channels)]
    scratch = [
        pltpu.VMEM((blocks, 2, SEG, channels), F32),
        pltpu.VMEM((total_rows, channels), F32),
        pltpu.VMEM((DEPTH * SEG, channels), F32),
        pltpu.VMEM((2, owners, 3, piece, channels), BF16),
        pltpu.VMEM((total_rows, width), BF16),
        pltpu.VMEM((total_rows, width), BF16),
        pltpu.VMEM((total_rows, width), BF16),
        pltpu.VMEM((all_blocks, HEADS, channels), F32),
        pltpu.SemaphoreType.DMA((4,)),
        pltpu.SemaphoreType.DMA((4,)),
        pltpu.SemaphoreType.DMA((8,)),
    ]
    scratch += LineSum.scratch(total_rows, width) * 2
    for shape in flat_shapes:
        scratch += OwnerSum.scratch(owners, shape)
    for shape, axes in (
        ((16, channels), 2), ((8, width), 3), ((units, channels), 2), ((3, units, 128), 3),
    ):
        for count in (4, owners, tp_count)[:axes]:
            scratch += SmallSum.scratch(count, shape)
    result, grad_x, own_up, own_down, own_out, own_in, va, vd, vl, vf = call(
        back_kernel,
        (
            sds((total_rows, width), F32),
            sds((total_rows, width), F32),
            sds((2, piece, hidden), F32),
            sds((2, piece, hidden), F32),
            sds((2, piece, channels), F32),
            sds((2, 3, piece, channels), F32),
            sds((16, channels), F32),
            sds((8, width), F32),
            sds((units, channels), F32),
            sds((3, units, 128), F32),
        ),
        [SM] + [VM] * 23 + [HB] * 10,
        scratch,
        3,
        out_specs=(HB, HB) + (VM,) * 8,
    )(
        parents, d_all, d_conv, d_zero, mixed[1:], low, in_all, x, down_part, fh, fl, th, tl, sign, sw, skip,
        row(mixer_gain), row(feed_down_bias), ft, w2, last, freq, small, grad_skip,
        residual, d_res, proj, head, spec, filt, net, stage_up, stage_down, stage_out,
    )
    dp_index = lax.axis_index("dp")
    own_last = lax.dynamic_slice_in_dim(vl, dp_index * (units // owners), units // owners, 0)
    return (
        result[None], grad_x[None], vd[4], vd[5],
        jnp.transpose(own_in, (0, 2, 1, 3)).reshape(width // owners, 3, channels),
        va[9:12], va[0:9].reshape(3, 3, channels), va[12:15],
        vf[0, :, :features].T, vf[0, :, features], vf[1, :, :units].T, vf[1, :, units], vf[2, :, 0],
        own_last, va[15], own_out.reshape(width // owners, channels).T, vd[1], vd[2], vd[3],
        own_up.reshape(width // owners, hidden), vd[6], own_down.reshape(width // owners, hidden).T, vd[0],
    )


def solution(mesh):
    in_specs = (
        P("dp", "ctx", None), P("dp", "ctx", None), P("dp", None), P(), P(), P("dp", None, "tp"), P(None, "tp"),
        P(None, None, "tp"), P(None, "tp"), P(), P(), P(), P(), P(), P("dp", "tp"), P("tp"), P("tp", "dp"), P(),
        P(), P(), P("dp", "tp"), P("tp"), P("tp", "dp"), P(),
    )
    out_specs = (
        P("dp", "ctx", None), P("dp", "ctx", None), P(), P(), P("dp", None, "tp"), P(None, "tp"),
        P(None, None, "tp"), P(None, "tp"), P(), P(), P(), P(), P(), P("dp", "tp"), P("tp"), P("tp", "dp"), P(),
        P(), P(), P("dp", "tp"), P("tp"), P("tp", "dp"), P(),
    )
    return jax.shard_map(body, mesh=mesh, in_specs=in_specs, out_specs=out_specs, check_vma=False)
```

time: 594 us -> 389 us (0.65)
  blocking collectives: 113 us -> 35.8 us
  Pallas kernels: 354 us -> 281 us
  waiting for transfers between devices: 22.3 us -> 0.77 us
  other arithmetic: 21.1 us -> 2.93 us
  matrix products: 17.8 us -> 0 us
    pallas_call x8 -> x2, Pallas kernels: 267 us -> 137 us  [the longest x1 130 us: body(): call(back_kernel, (sds((total_rows, width), F32), sds((total_rows, width)...]
    psum x3 -> x0, blocking collectives: 74.2 us -> none  [the longest x1 38.3 us: body(): lax.psum((g1, g1b, g2, g2b, gfreq), ('dp', 'ctx', 'tp'))]
    pallas_call x1, Pallas kernels: 18.3 us -> 80.3 us  [body(): call(feed_kernel, (sds((total_rows, width), F32), sds((total_rows, width)...]
    all_gather x1, waiting for transfers between devices: 20.8 us -> 0.01 us  [body(): out_all = lax.all_gather(out_own, 'tp', axis=0)]
    dot_general x8 -> x0, matrix products: 17.8 us -> none  [the longest x3 10.6 us: implicit_filter(): raw_taps = jnp.dot(hidden, last_weight, precision=EXACT)]
    convert_element_type x8 -> x0, local copies, waits for them, and re-layouts: 8.57 us -> none  [the longest x2 3.98 us: body(): share_cols(grad_down).astype(BF16)]
    convert_element_type x8 -> x1, other arithmetic: 7.71 us -> 0.62 us  [body(): last = last_all.astype(F32)]
    unnamed x84 -> x43, local copies, waits for them, and re-layouts: 7.02 us -> 12.2 us
  transfers between devices with their start and end apart: 6 -> 4, of which waited for: 1 -> 0; matrix products, arithmetic and copies ran while one was open for 9% -> 7% of each run, Pallas kernels for 39% -> 18%
where the time goes in v2:
time: 389 us; the launch traced here: 383 us
  Pallas kernels  281 us (72%)
  local copies, waits for them, and re-layouts  48.6 us (12%)
  blocking collectives  35.8 us (9%)
  between operations  14.2 us (4%)
    pallas_call x1, Pallas kernels, body(): call(back_kernel, (sds((total_rows, width), F32), sds((total_rows, width)...  130 us
    pallas_call x1, Pallas kernels, body(): call(feed_kernel, (sds((total_rows, width), F32), sds((total_rows, width)...  80.3 us
    pallas_call x1, Pallas kernels, line_gather(): call(line_gather_kernel, sds((count,) + x.shape, x.dtype), [VM], [pltpu.S...  39.9 us
    all_gather x1, blocking collectives, body(): lax.all_gather(in_proj, 'dp', axis=0, tiled=True)  16.3 us
    pallas_call x1, Pallas kernels, body(): call(conv_fwd_kernel, (sds((total_rows, channels), F32), sds((total_rows,...  14.3 us
    unnamed x43, local copies, waits for them, and re-layouts  12.2 us
    pallas_call x1, Pallas kernels, body(): call(mix_in_kernel, (sds((total_rows, width), BF16), sds((3, total_rows,...  9.51 us
    all_gather x1, blocking collectives, body(): out_own = lax.all_gather(out_proj.T, 'dp', axis=0, tiled=True)  9.35 us
  transfers between devices with their start and end apart: 4, of which 0 were waited for; matrix products, arithmetic and copies ran while one was open for 7% of the time, Pallas kernels for 18%

profile of v2, /device:TPU:0, one launch (start us, length us, event | category | flops | bytes accessed | tf_op | source)
XLA Modules:
  0.0 383.4 jit_solution(1231319682955782333)
XLA Ops:
  7.2 9.3 %all_gather.31 = bf16[768,192]{0,1:T(8,128)(2,1)} all-gather(bf16[384,192]{0,1:T(8,128)(2,1)} %bitcast.59), channel_id=1, replica_groups=mesh['dp'=2,'ctx'=4,'tp'=4] {'dp'}, dimensions={0}, use_global_device_ids=true | all-gather | bytes 442368 | tf_op jit(solution)/shard_map/all_gather | solution.py:1131
  16.7 1.3 reshape.143.gain_ref.mgain_ref
  18.0 1.3 reshape.144.shift_ref
  19.2 0.8 slice.77
  20.0 1.3 reshape.145.sw_ref
  21.4 5.2 %all_gather.27 = bf16[16,2,768]{2,1,0:T(2,128)(2,1)S(1)} all-gather(bf16[4,2,768]{2,1,0:T(2,128)(2,1)S(1)} %slice.77), channel_id=1, replica_groups=mesh['dp'=2,'ctx'=4,'tp'=4] {'ctx'}, dimensions={0}, use_global_device_ids=true | all-gather | bytes 61440 | tf_op jit(solution)/shard_map/all_gather | solution.py:1129
  26.6 0.6 reshape.142.xt_ref
  27.2 1.2 copy.80
  28.6 16.3 %all_gather.28 = bf16[768,3,192]{2,0,1:T(8,128)(2,1)} all-gather(bf16[384,3,192]{2,0,1:T(8,128)(2,1)S(1)} %copy.80), channel_id=1, replica_groups=mesh['dp'=2,'ctx'=4,'tp'=4] {'dp'}, dimensions={0}, use_global_device_ids=true | all-gather | bytes 1327104 | tf_op jit(solution)/shard_map/all_gather | solution.py:1128
  45.0 0.7 fusion.2.pick_ref
  45.7 9.5 %shard_map.461 = (bf16[1024,768]{1,0:T(8,128)(2,1)}, f32[3,1024,192]{2,1,0:T(8,128)}, f32[3,4,8,192]{3,2,1,0:T(8,128)}, f32[3,1024,192]{2,1,0:T(8,128)}, bf16[1024,192]{1,0:T(8,128)(2,1)}) custom-call(bf16[1024,768]{1,0:T(8,128)(2,1)} %bitcast.41, bf16[32,768]{1,0:T(8,128)(2,1)} %reshape.142.xt_ref, f32[4,8,32]{2,1,0:T(8,128)} %fusion.2.pick_ref, ...), custom_call_target="tpu_custom_call" | custom-call | tf_op jit(solution)/shard_map/pallas_call | solution.py:1162
  55.3 2.0 copy.81
  57.4 0.7 all-gather.8.cloned.1.call-update
  58.2 2.3 copy.89
  60.7 0.6 reshape.148.ob_ref
  61.2 0.6 reshape.149.gain_ref
  61.8 0.6 reshape.150.shift_ref
  63.6 0.7 copy.86.freq_ref
  64.7 4.9 %all_gather.30 = bf16[64,192]{1,0:T(8,128)(2,1)S(1)} all-gather(bf16[32,192]{1,0:T(8,128)(2,1)S(1)} %copy-done.6), channel_id=1, replica_groups=mesh['dp'=2,'ctx'=4,'tp'=4] {'dp'}, dimensions={0}, use_global_device_ids=true | all-gather | bytes 36864 | tf_op jit(solution)/shard_map/all_gather | solution.py:1135
  69.6 0.6 convert_element_type.7.last_ref
  70.2 1.5 slice.60.mixed_ref
  71.7 0.7 maximum_maximum_fusion.w1_ref
  72.4 0.7 maximum_maximum_fusion.1.w2_ref
  73.1 6.7 %shard_map.462 = (f32[6,72,1536]{2,1,0:T(8,128)}, f32[1536,192]{1,0:T(8,128)}) custom-call(f32[40,1536]{1,0:T(8,128)} %constant.45.clone.ft_ref, f32[64,40]{1,0:T(8,128)} %maximum_maximum_fusion.w1_ref, f32[64,72]{1,0:T(8,128)} %maximum_maximum_fusion.1.w2_ref, f32[64,192]{1,0:T(8,128)} %convert_element_type.7.last_ref, f32[64,1]{1,0:T(8,128)} %copy.86.freq_ref), custom_call_target="tpu_custom_call" | custom-call | tf_op jit(solution)/shard_map/pallas_call | solution.py:1154
  79.8 1.0 slice_bitcast_fusion.gate_ref.mixed_ref
  80.8 2.5 copy.88
  83.3 3.8 copy.87.all_ref
  87.1 14.3 %shard_map.463 = (f32[1024,192]{1,0:T(8,128)}, bf16[1024,192]{1,0:T(8,128)(2,1)}, f32[13,2,256,192]{3,2,1,0:T(8,128)}, f32[6,2,256,192]{3,2,1,0:T(8,128)}) custom-call(s32[1,16]{1,0:T(1,128)} %par_ref.3, bf16[4,256,192]{2,1,0:T(8,128)(2,1)} %bitcast.48, bf16[16,256,192]{2,1,0:T(8,128)(2,1)} %copy.87.all_ref, f32[1536,192]{1,0:T(8,128)} %get-tuple-element.56.taps_ref, ...), custom_call_target="tpu_custom_call" | custom-call | tf_op jit(solution)/shard_map/pallas_call | solution.py:1179
  101.4 39.9 %shard_map.464.gated_ref = bf16[4,1024,192]{2,1,0:T(8,128)(2,1)} custom-call(bf16[1024,192]{1,0:T(8,128)(2,1)} %get-tuple-element.58.x_ref), custom_call_target="tpu_custom_call" | custom-call | bytes 1572864 | tf_op jit(solution)/shard_map/pallas_call | solution.py:584
  141.3 80.3 %shard_map.465 = (f32[1024,768]{1,0:T(8,128)}, bf16[1024,768]{1,0:T(8,128)(2,1)}, f32[1024,768]{1,0:T(8,128)}, f32[1024,192]{1,0:T(8,128)}, f32[1024,192]{1,0:T(...) custom-call(bf16[4,1024,192]{2,1,0:T(8,128)(2,1)} %shard_map.464.gat, ...), custom_call_target="tpu_custom_call" | custom-call | tf_op jit(solution)/shard_map/pallas_call | solution.py:1194
  221.6 130.2 %shard_map.466 = (f32[1024,768]{1,0:T(8,128)}, f32[1024,768]{1,0:T(8,128)}, f32[2,192,768]{2,1,0:T(8,128)}, f32[2,192,768]{2,1,0:T(8,128)}, f32[2,192,192]{2,1,0...) custom-call(s32[1,16]{1,0:T(1,128)} %par_ref.3, ...), custom_call_target="tpu_custom_call" | custom-call | tf_op jit(solution)/shard_map/pallas_call | solution.py:1249
  351.8 1.3 slice.71
  353.1 1.4 fusion.3
  354.5 1.5 slice_reduce_fusion
  356.0 0.8 slice_bitcast_fusion.1
  356.8 0.8 slice_bitcast_fusion.2
  357.5 1.3 reshape.154
  358.8 1.7 slice_reduce_fusion.3
  360.5 0.7 copy.94
  361.2 0.7 copy.95
  361.9 1.9 copy.92
  363.8 1.9 copy.91
  365.7 1.8 reshape.153
  367.5 1.4 copy.93
  368.9 0.6 constant_dynamic-slice_fusion
  369.5 3.9 %copy.99 = f32[1,1024,768]{2,1,0:T(8,128)} copy(f32[1,1024,768]{2,1,0:T(8,128)} %bitcast.50) | data formatting | bytes 6291456
  373.4 1.7 copy.100
  375.5 1.0 copy.101
  (59 shorter events, 2.7 us)
Async XLA Ops:
  7.2 21.3 %copy-start.13 = (s32[1,16]{1,0:T(1,128)S(1)}, s32[1,16]{1,0:T(1,128)}, u32[]{:S(2)}) copy-start(s32[1,16]{1,0:T(1,128)} %par_ref.3) | copy-start | bytes 196
  7.2 73.6 %all-gather.12.cloned.1.call-start = ((), (), s32[]{:S(2)}) async-start(), calls=%async_computation.3 | async-start | bytes 1474560 | tf_op jit(solution)/shard_map/all_gather | solution.py:1132
  16.6 66.7 %all-gather.6.cloned.1.call-start = ((), (), s32[]{:S(2)}) async-start(), calls=%async_computation | async-start | bytes 1966080 | tf_op jit(solution)/shard_map/all_gather | solution.py:1176
  55.2 7.2 %copy-start.11 = (f32[768]{0:T(1024)S(1)}, f32[768]{0:T(1024)}, u32[]{:S(2)}) copy-start(f32[768]{0:T(1024)} %param.51) | copy-start | bytes 9220
  55.2 7.8 %copy-start.12 = (f32[768]{0:T(1024)S(1)}, f32[768]{0:T(1024)}, u32[]{:S(2)}) copy-start(f32[768]{0:T(1024)} %param.53) | copy-start | bytes 9220
  55.2 8.3 %copy-start.14 = (f32[64]{0:T(128)S(1)}, f32[64]{0:T(128)}, u32[]{:S(2)}) copy-start(f32[64]{0:T(128)} %param.43) | copy-start | bytes 772
  55.2 9.0 %copy-start.5 = (f32[33,64]{1,0:T(8,128)S(1)}, f32[33,64]{1,0:T(8,128)}, u32[]{:S(2)}) copy-start(f32[33,64]{1,0:T(8,128)} %param.39) | copy-start | bytes 25348
  55.3 9.1 %copy-start.15 = (f32[64]{0:T(128)S(1)}, f32[64]{0:T(128)}, u32[]{:S(2)}) copy-start(f32[64]{0:T(128)} %param.40) | copy-start | bytes 772
  55.3 9.3 %copy-start.16 = (f32[64]{0:T(128)S(1)}, f32[64]{0:T(128)}, u32[]{:S(2)}) copy-start(f32[64]{0:T(128)} %param.42) | copy-start | bytes 772
  55.3 9.4 %copy-start.6 = (bf16[32,192]{1,0:T(8,128)(2,1)S(1)}, bf16[32,192]{1,0:T(8,128)(2,1)}, u32[]{:S(2)}) copy-start(bf16[32,192]{1,0:T(8,128)(2,1)} %param.44) | copy-start | bytes 36868
  57.3 3.3 copy-start.8
  57.3 3.9 %copy-start.9 = (f32[768]{0:T(1024)S(1)}, f32[768]{0:T(1024)}, u32[]{:S(2)}) copy-start(f32[768]{0:T(1024)} %param.48) | copy-start | bytes 9220
  57.3 4.5 %copy-start.10 = (f32[768]{0:T(1024)S(1)}, f32[768]{0:T(1024)}, u32[]{:S(2)}) copy-start(f32[768]{0:T(1024)} %param.49) | copy-start | bytes 9220
  57.3 7.1 %copy-start.4 = (f32[64,64]{1,0:T(8,128)S(1)}, f32[64,64]{1,0:T(8,128)}, u32[]{:S(2)}) copy-start(f32[64,64]{1,0:T(8,128)} %param.41) | copy-start | bytes 49156
  57.4 12.9 %copy-start.1 = (f32[3,1024,192]{2,1,0:T(8,128)S(1)}, f32[3,1024,192]{2,1,0:T(8,128)}, u32[]{:S(2)}) copy-start(f32[3,1024,192]{2,1,0:T(8,128)} %get-tuple-element.57) | copy-start | bytes 7077892
  57.4 83.9 %all-gather.8.cloned.1.call-start = ((), (), s32[]{:S(2)}) async-start(), calls=%async_computation.1 | async-start | bytes 1769472 | tf_op jit(solution)/shard_map/all_gather | solution.py:1133
  58.1 83.2 %all-gather.10.cloned.1.call-start = ((), (), s32[]{:S(2)}) async-start(), calls=%async_computation.2 | async-start | bytes 1769472 | tf_op jit(solution)/shard_map/all_gather | solution.py:1134
  365.7 1.9 copy-start.3
  367.5 1.4 copy-start.7
  369.5 3.9 %copy-start = (f32[1024,768]{1,0:T(8,128)S(1)}, f32[1024,768]{1,0:T(8,128)}, u32[]{:S(2)}) copy-start(f32[1024,768]{1,0:T(8,128)} %get-tuple-element.78) | copy-start | bytes 9437188
  373.4 2.1 copy-start.2
Sparse Core Ops, SparseCore 0:
  16.7 30.7 all-gather.11
  57.5 19.9 all-gather.5
  79.1 22.7 all-gather.7
  103.9 22.7 all-gather.9

commit v3 on v2

--- a/solution.py
+++ b/solution.py
@@ -90,43 +90,7 @@
     return mm(high, v_high) + (mm(low, v_high) + mm(high, v_low))
 
 
-def mix_in_kernel(
-    x_ref, xt_ref, pick_ref, w_ref, bias_ref, gain_ref, shift_ref, sw_ref, sb_ref,
-    low_ref, proj_ref, head_ref, mixed_ref, carried_ref, ext_ref,
-):
-    gain, shift = gain_ref[...], shift_ref[...]
-    tails = normalize(xt_ref[...].astype(F32))[0] * gain + shift
-    tails = tails.astype(BF16)
-    tail_proj = [mm(tails, w_ref[g]) + bias_ref[g : g + 1] for g in range(3)]
-    blocks = x_ref.shape[0] // SEG
-
-    def one(s, unused):
-        rows = pl.ds(pl.multiple_of(s * SEG, SEG), SEG)
-        low = (normalize(x_ref[rows].astype(F32))[0] * gain + shift).astype(BF16)
-        low_ref[rows] = low
-        out = []
-        for g in range(3):
-            projected = mm(low, w_ref[g]) + bias_ref[g : g + 1]
-            proj_ref[g, rows] = projected
-            head = jnp.dot(pick_ref[s], tail_proj[g], precision=EXACT, preferred_element_type=F32)
-            head_ref[g, s] = head
-            ext_ref[g, 0:HEADS] = head
-            ext_ref[g, HEADS : HEADS + SEG] = projected
-            mixed = (
-                sw_ref[3 * g : 3 * g + 1] * ext_ref[g, HEADS - 2 : HEADS - 2 + SEG]
-                + sw_ref[3 * g + 1 : 3 * g + 2] * ext_ref[g, HEADS - 1 : HEADS - 1 + SEG]
-                + sw_ref[3 * g + 2 : 3 * g + 3] * projected
-                + sb_ref[g : g + 1]
-            )
-            mixed_ref[g, rows] = mixed
-            out.append(mixed)
-        carried_ref[rows] = (out[2] * out[1]).astype(BF16)
-        return unused
-
-    lax.fori_loop(0, blocks, one, 0)
-
-
-FT = 64
+FT = 32
 
 
 def lineage(par_ref, block):
@@ -139,23 +103,23 @@
     return out
 
 
-def blend(dst, terms, rows, conj):
-    re = im = None
-    for a, b in terms:
-        ar, ai = a[0, rows], a[1, rows]
-        br, bi = b[0, rows], b[1, rows]
-        if conj:
-            pr, pi = ar * br + ai * bi, ar * bi - ai * br
-        else:
-            pr, pi = ar * br - ai * bi, ar * bi + ai * br
-        re, im = (pr, pi) if re is None else (re + pr, im + pi)
-    dst[0, rows] = re
-    dst[1, rows] = im
-
-
 def blend_all(dst, terms, conj):
-    for t in range(SEG // FT):
-        blend(dst, terms, slice(t * FT, (t + 1) * FT), conj)
+    def tile(t, unused):
+        rows = pl.ds(pl.multiple_of(t * FT, FT), FT)
+        re = im = None
+        for a, b in terms:
+            ar, ai = a[0, rows], a[1, rows]
+            br, bi = b[0, rows], b[1, rows]
+            if conj:
+                pr, pi = ar * br + ai * bi, ar * bi - ai * br
+            else:
+                pr, pi = ar * br - ai * bi, ar * bi + ai * br
+            re, im = (pr, pi) if re is None else (re + pr, im + pi)
+        dst[0, rows] = re
+        dst[1, rows] = im
+        return unused
+
+    lax.fori_loop(0, SEG // FT, tile, 0)
 
 
 def unpack_spectrum(th, tl, ref):
@@ -167,80 +131,6 @@
         + (mm(tl[:, a], high_re) + mm(tl[:, b], high_im))
         + (mm(th[:, a], low_re) + mm(th[:, b], low_im))
     )
-
-
-def filter_kernel(ft_ref, w1_ref, w2_ref, last_ref, freq_ref, net_ref, taps_ref):
-    units, channels = last_ref.shape
-    length = ft_ref.shape[1]
-    tp = lax.axis_index("tp")
-    width = channels * lax.axis_size("tp")
-    exact = dict(precision=EXACT, preferred_element_type=F32)
-    freq = freq_ref[...]
-    pad = net_ref.shape[1] - units
-    ones = jnp.where(lax.broadcasted_iota(jnp.int32, (pad, length), 0) == 0, 1.0, 0.0)
-    net_ref[...] = jnp.zeros(net_ref.shape, F32)
-    pre = jnp.dot(w1_ref[...], ft_ref[...], **exact)
-    net_ref[0, 0:units] = pre
-    net_ref[1, 0:units] = jnp.cos(freq * pre)
-    net_ref[2, 0:units] = jnp.sin(freq * pre)
-    net_ref[2, units:] = ones
-    pre = jnp.dot(w2_ref[...], net_ref[2], **exact)
-    net_ref[3, 0:units] = pre
-    net_ref[4, 0:units] = jnp.cos(freq * pre)
-    second = jnp.sin(freq * pre)
-    net_ref[5, 0:units] = second
-    raw = lax.dot_general(second, last_ref[...], (((0,), (0,)), ((), ())), **exact)
-    time_pos = lax.broadcasted_iota(jnp.int32, (length, 1), 0).astype(F32) * (1.0 / (length - 1))
-    channel = (lax.broadcasted_iota(jnp.int32, (1, channels), 1) + tp * channels).astype(F32)
-    rate = SLOW_RATE + (FAST_RATE - SLOW_RATE) * channel * (1.0 / (width - 1))
-    taps_ref[...] = raw * (jnp.exp(-time_pos * rate) + SHIFT_FLOOR)
-
-
-def conv_fwd_kernel(
-    par_ref, own_ref, all_ref, taps_ref, gate_ref, skip_ref,
-    fh_ref, fl_ref, th_ref, tl_ref, sign_ref,
-    conv_ref, gated_ref, spec_ref, filt_ref, acc_ref,
-):
-    blocks = own_ref.shape[0]
-    ctx = lax.axis_index("ctx")
-    fh, fl, th, tl = fh_ref[...], fl_ref[...], th_ref, tl_ref
-
-    def source(j, unused):
-        for base, ref, off in ((0, all_ref, 0), (4, all_ref, 4), (8, own_ref, 0)):
-            part = ref[off + j]
-            out = mm(fh, part) + mm(fl, part)
-            spec_ref[base + j, 0] = out[:SEG]
-            spec_ref[base + j, 1] = out[SEG:]
-        return unused
-
-    lax.fori_loop(0, blocks, source, 0)
-    spec_ref[12] = jnp.zeros(spec_ref.shape[1:], F32)
-    sign = sign_ref[...]
-    last = None
-    for j in range(DEPTH):
-        part = taps_ref[j * SEG : (j + 1) * SEG]
-        out = mm_split(fh, fl, part)
-        re, im = out[:SEG], out[SEG:]
-        if last is None:
-            filt_ref[j, 0] = re
-            filt_ref[j, 1] = im
-        else:
-            filt_ref[j, 0] = re - sign * last[1]
-            filt_ref[j, 1] = im + sign * (last[0] - last[2])
-        last = (re, im, part[0:1])
-
-    def dest(s, unused):
-        above = lineage(par_ref, ctx * blocks + s)
-        places = [8 + s] + [jnp.where(a >= 0, a, 12) for a in above]
-        blend_all(acc_ref, [(filt_ref.at[d], spec_ref.at[places[d]]) for d in range(DEPTH)], False)
-        long_out = unpack_spectrum(th, tl, acc_ref) * (1.0 / SEG)
-        place = pl.ds(pl.multiple_of(s * SEG, SEG), SEG)
-        convolved = long_out + skip_ref[...] * own_ref[s].astype(F32)
-        conv_ref[place] = convolved
-        gated_ref[place] = (convolved * gate_ref[place]).astype(BF16)
-        return unused
-
-    lax.fori_loop(0, blocks, dest, 0)
 
 
 def filter_features(length, bands, rows):
@@ -415,55 +305,83 @@
     return barrier, len(partners)
 
 
-def store_shares(stage_ref, tile, rows_per_tile, value):
-    owners = stage_ref.shape[1]
-    piece = stage_ref.shape[2]
-    first = tile * rows_per_tile // piece
-    for q in range(rows_per_tile // piece):
-        owner, half = divmod(first + q, 2)
-        stage_ref[half, owner] = value[q * piece : (q + 1) * piece].astype(BF16)
+def store_columns(stage, half, value):
+    owners, share = stage.shape[1], stage.shape[-1]
+    for o in range(owners):
+        stage[half, o] = value[:, o * share : (o + 1) * share].astype(BF16)
+
+
+def store_rows(stage, first, value):
+    size = stage.shape[2]
+    for q in range(value.shape[0] // size):
+        owner, half = divmod(first // size + q, 2)
+        stage[half, owner] = value[q * size : (q + 1) * size].astype(BF16)
 
 
 def feed_kernel(
-    gated_ref, out_ref, x_ref, g_ref, ob_ref, gain_ref, shift_ref, up_ref, ub_ref, down_ref,
+    gated_ref, out_in, x_ref, g_ref, ob_ref, gain_ref, shift_ref, up_ref, ub_ref, down_in,
     mixed_ref, conv_ref, carried_ref,
     resid_ref, dpart_ref, dres_ref, dconv_ref, dzero_ref, dall_ref, gup_ref, gdown_ref, gout_ref,
     small_ref, gskip_ref,
-    low_ref, hidden_ref, dpre_ref, npart_ref, nsum_ref, dmix_ref, own_ref, s_long, r_long, *line,
+    low_ref, hidden_ref, dpre_ref, npart_ref, nsum_ref, dmix_ref, own_ref, gall_ref, out_ref, down_ref,
+    s_gate, r_gate, s_long, r_long, *line,
 ):
-    groups = gated_ref.shape[0]
+    groups, owners = out_in.shape[:2]
     width = x_ref.shape[1]
     blocks = x_ref.shape[0] // SEG
+    share = width // owners
     tp, ctx = lax.axis_index("tp"), lax.axis_index("ctx")
     chain = LineSum(npart_ref, nsum_ref, line)
-    barrier, count = signal_all([chain.mate, chain.cross] + [spot(ctx=lax.rem(ctx + i, 4)) for i in range(1, 4)])
+    barrier, count = signal_all(
+        [spot(tp=lax.rem(tp + i, groups)) for i in range(1, groups)]
+        + [spot(ctx=lax.rem(ctx + i, 4)) for i in range(1, 4)]
+    )
+
+    def gate_copy(s, i):
+        rows = pl.ds(pl.multiple_of(s * SEG, SEG), SEG)
+        return remote(
+            gated_ref.at[rows], gall_ref.at[tp, rows], s_gate.at[i, s], r_gate.at[tp, s],
+            spot(tp=lax.rem(tp + i, groups)),
+        )
+
+    gall_ref[tp] = gated_ref[...]
+    pl.semaphore_wait(barrier, count)
+    for s in range(blocks):
+        for i in range(1, groups):
+            gate_copy(s, i).start()
+    for o in range(owners):
+        columns = slice(o * share, (o + 1) * share)
+        down_ref[:, columns] = down_in[o]
+        for z in range(groups):
+            out_ref[z, :, columns] = out_in[z, o]
+    ob, gain, shift = (ref[...].reshape(1, -1) for ref in (ob_ref, gain_ref, shift_ref))
+    ub = ub_ref[...].reshape(1, -1)
     small_ref[...] = jnp.zeros(small_ref.shape, F32)
     gskip_ref[...] = jnp.zeros(gskip_ref.shape, F32)
 
     def core(s, unused):
         rows = pl.ds(pl.multiple_of(s * SEG, SEG), SEG)
-        mixed = mm_nt(gated_ref[0, rows], out_ref[0])
+        for i in range(1, groups):
+            source = lax.rem(tp + i, groups)
+            at = gall_ref.at[source, rows]
+            remote(at, at, s_gate.at[i, s], r_gate.at[source, s], chain.mate).wait_recv()
+        mixed = mm(gall_ref[0, rows], out_ref[0])
         for z in range(1, groups):
-            mixed = mixed + mm_nt(gated_ref[z, rows], out_ref[z])
-        residual = x_ref[rows].astype(F32) + mixed + ob_ref[...]
+            mixed = mixed + mm(gall_ref[z, rows], out_ref[z])
+        residual = x_ref[rows].astype(F32) + mixed + ob
         resid_ref[rows] = residual
-        low = (normalize(residual)[0] * gain_ref[...] + shift_ref[...]).astype(BF16)
+        low = (normalize(residual)[0] * gain + shift).astype(BF16)
         low_ref[rows] = low
-        pre = mm(low, up_ref[...]) + ub_ref[...]
+        pre = mm(low, up_ref[...]) + ub
         cdf = 0.5 * (1.0 + lax.erf(pre * math.sqrt(0.5)))
         hidden_ref[rows] = (pre * cdf).astype(BF16)
         slope = cdf + pre * (jnp.exp(-0.5 * pre * pre) * (1.0 / math.sqrt(2.0 * math.pi)))
         grad = g_ref[rows]
-        d_pre = (mm(grad, down_ref[...]) * slope).astype(BF16)
+        d_pre = (mm_nt(grad, down_ref[...]) * slope).astype(BF16)
         dpre_ref[rows] = d_pre
         npart_ref[rows] = mm_nt(d_pre, up_ref[...]).astype(BF16)
         small_ref[0:1] += jnp.sum(grad.astype(F32), axis=0, keepdims=True)
         small_ref[6:7] += jnp.sum(d_pre.astype(F32), axis=0, keepdims=True)
-
-        @pl.when(s == 0)
-        def _():
-            pl.semaphore_wait(barrier, count)
-
         chain.send_block(s)
         return unused
 
@@ -472,15 +390,15 @@
 
     def down(s, unused):
         rows = pl.ds(pl.multiple_of(s * SEG, SEG), SEG)
-        dpart_ref[rows] = mm_nt(hidden_ref[rows], down_ref[...]).astype(BF16)
+        dpart_ref[rows] = mm(hidden_ref[rows], down_ref[...]).astype(BF16)
         return unused
 
     lax.fori_loop(0, blocks, down, 0)
-    half = width // 2
     for t in range(2):
-        columns = slice(t * half, (t + 1) * half)
-        store_shares(gup_ref, t, half, mm_tn(low_ref[:, columns], dpre_ref[...]))
-        store_shares(gdown_ref, t, half, mm_tn(g_ref[:, columns], hidden_ref[...]))
+        part = slice(t * width // 2, (t + 1) * width // 2)
+        store_rows(gup_ref, t * width // 2, mm_tn(low_ref[:, part], dpre_ref[...]))
+        units = hidden_ref.shape[1] // 2
+        store_columns(gdown_ref, t, mm_tn(hidden_ref[:, t * units : (t + 1) * units], g_ref[...]))
 
     def to_ctx(s, other):
         return remote(own_ref.at[s], dall_ref.at[ctx * blocks + s], s_long.at[other, s], r_long.at[ctx, s], spot(ctx=other))
@@ -491,7 +409,7 @@
         rows = pl.ds(pl.multiple_of(s * SEG, SEG), SEG)
         xhat, scale = normalize(resid_ref[rows])
         dn = nsum_ref[rows].astype(F32)
-        e = dn * gain_ref[...]
+        e = dn * gain
         d_res = g_ref[rows].astype(F32) + scale * (
             e - jnp.mean(e, axis=-1, keepdims=True) - xhat * jnp.mean(e * xhat, axis=-1, keepdims=True)
         )
@@ -501,7 +419,7 @@
         d_mix = d_res.astype(BF16)
         dmix_ref[rows] = d_mix
         small_ref[1:2] += jnp.sum(d_mix.astype(F32), axis=0, keepdims=True)
-        d_gated = mm(d_mix, out_ref[tp])
+        d_gated = mm_nt(d_mix, out_ref[tp])
         d_conv = d_gated * mixed_ref[rows]
         dconv_ref[rows] = d_conv
         own_ref[s] = d_conv.astype(BF16)
@@ -517,9 +435,12 @@
     lax.fori_loop(0, blocks, back, 0)
     for s in range(blocks):
         dall_ref[ctx * blocks + s] = own_ref[s]
+    value = mm_tn(gated_ref[...], dmix_ref[...])
     for t in range(2):
-        columns = slice(t * half, (t + 1) * half)
-        store_shares(gout_ref, t, half, mm_tn(dmix_ref[:, columns], gated_ref[tp]))
+        store_columns(gout_ref, t, value[t * gout_ref.shape[2] : (t + 1) * gout_ref.shape[2]])
+    for s in range(blocks):
+        for i in range(1, groups):
+            gate_copy(s, i).wait_send()
     chain.drain()
     for other in range(4):
         @pl.when(other < ctx)
@@ -534,61 +455,338 @@
                 remote(at, at, s_long.at[other, s], r_long.at[other, s], chain.mate).wait_recv()
 
 
-def line_sum_kernel(part_ref, total_ref, *line):
-    chain = LineSum(part_ref, total_ref, line)
-    barrier, count = signal_all([chain.mate, chain.cross])
+def extend_weights(ref, weight, bias):
+    rows = weight.shape[0]
+    ref[...] = jnp.zeros(ref.shape, F32)
+    ref[0:rows] = weight[...]
+    ref[rows : rows + 1] = bias[...].reshape(1, -1)
+
+
+def decay(length, channels, tp, width):
+    time_pos = lax.broadcasted_iota(jnp.int32, (length, 1), 0).astype(F32) * (1.0 / (length - 1))
+    channel = (lax.broadcasted_iota(jnp.int32, (1, channels), 1) + tp * channels).astype(F32)
+    rate = SLOW_RATE + (FAST_RATE - SLOW_RATE) * channel * (1.0 / (width - 1))
+    return jnp.exp(-time_pos * rate) + SHIFT_FLOOR
+
+
+EXACT_DOT = dict(precision=EXACT, preferred_element_type=F32)
+TN = (((0,), (0,)), ((), ()))
+NT = (((1,), (1,)), ((), ()))
+
+
+def front_kernel(
+    par_ref, x_ref, win_ref, last_ref, out_in, up_in, down_in, ft_ref, f1_ref, f1b_ref, f2_ref, f2b_ref, freq_ref,
+    gain_ref, shift_ref, ib_ref, sw_ref, sb_ref, skip_ref, fh_ref, fl_ref, th_ref, tl_ref, sign_ref,
+    low_hbm, proj_hbm, head_hbm, mixed_hbm, spec_hbm, filt_hbm, net_hbm, in_hbm, out_hbm, up_hbm, down_hbm,
+    lasts_ref, gate_ref, conv_ref, gated_ref, carried_ref,
+    w_ref, low_ref, proj_ref, head_ref, mixed_ref, spec_ref, filt_ref, net_ref, taps_ref, shared_ref,
+    xt_ref, tail_ref, ext_ref, w1_ref, w2_ref, acc_ref, lastb_ref, wb_ref,
+    s_in, r_in, s_last, r_last, s_out, r_out, s_up, r_up, s_down, r_down, s_xt, r_xt, s_car, r_car, s_fwd, local,
+):
+    total_rows, width = x_ref.shape
+    channels = ib_ref.shape[1]
+    blocks = total_rows // SEG
+    tp, ctx, dp = lax.axis_index("tp"), lax.axis_index("ctx"), lax.axis_index("dp")
+    owners, lines = out_hbm.shape[1], out_hbm.shape[0]
+    share = win_ref.shape[2]
+    last_share = last_ref.shape[0]
+    up_share = up_in.shape[0]
+
+    def cell(i):
+        flat = lax.rem(tp * owners + dp + i, owners * lines)
+        return flat // owners, lax.rem(flat, owners)
+
+    def owner(i):
+        return lax.rem(dp + i, owners)
+
+    def ctx_at(i):
+        return lax.rem(ctx + i, 4)
+
+    partners = [spot(ctx=ctx_at(i)) for i in range(1, 4)]
+    for i in range(1, owners * lines):
+        line, own = cell(i)
+        partners.append(spot(tp=line, dp=own))
+    barrier, count = signal_all(partners)
+
+    def rows_of(ref, who, size):
+        return ref.at[pl.ds(pl.multiple_of(who * size, size), size)]
+
+    def send_in(i):
+        return remote(win_ref, wb_ref.at[dp], s_in.at[i], r_in.at[dp], spot(dp=owner(i)))
+
+    def send_last(i):
+        return remote(last_ref, lastb_ref.at[dp], s_last.at[i], r_last.at[dp], spot(dp=owner(i)))
+
+    def send_xt(i):
+        at = xt_ref.at[ctx]
+        return remote(at, at, s_xt.at[i], r_xt.at[ctx], spot(ctx=ctx_at(i)))
+
+    for s in range(blocks):
+        tail = x_ref[s * SEG + SEG - 16 : s * SEG + SEG].astype(F32)
+        xt_ref[ctx, 2 * s : 2 * s + 2] = tail[14:16]
     pl.semaphore_wait(barrier, count)
-    blocks = part_ref.shape[0] // SEG
-
-    def send(s, unused):
-        chain.send_block(s)
+    for i in range(1, owners):
+        send_in(i).start()
+        send_last(i).start()
+    for i in range(1, 4):
+        send_xt(i).start()
+    wb_ref[dp] = win_ref[...]
+    lastb_ref[dp] = last_ref[...]
+
+    gain, shift = gain_ref[...].reshape(1, -1), shift_ref[...].reshape(1, -1)
+
+    def norm(s, unused):
+        rows = pl.ds(pl.multiple_of(s * SEG, SEG), SEG)
+        low_ref[rows] = (normalize(x_ref[rows].astype(F32))[0] * gain + shift).astype(BF16)
         return unused
 
-    def wait(s, unused):
-        chain.wait_block(s)
+    lax.fori_loop(0, blocks, norm, 0)
+    saves = [pltpu.make_async_copy(low_ref, low_hbm, local.at[1])]
+    saves[-1].start()
+
+    units = f1_ref.shape[1]
+    length = ft_ref.shape[1]
+    extend_weights(w1_ref, f1_ref, f1b_ref)
+    extend_weights(w2_ref, f2_ref, f2b_ref)
+    freq = freq_ref[...].reshape(1, -1)
+    net_ref[...] = jnp.zeros(net_ref.shape, F32)
+    angle = lax.dot_general(w1_ref[...] * freq, ft_ref[...], TN, **EXACT_DOT)
+    net_ref[0, 0:units] = jnp.cos(angle)
+    net_ref[1, 0:units] = jnp.sin(angle)
+    pad = net_ref.shape[1] - units
+    net_ref[1, units:] = jnp.where(lax.broadcasted_iota(jnp.int32, (pad, length), 0) == 0, 1.0, 0.0)
+    angle = lax.dot_general(w2_ref[...] * freq, net_ref[1], TN, **EXACT_DOT)
+    net_ref[2, 0:units] = jnp.cos(angle)
+    second = jnp.sin(angle)
+    net_ref[3, 0:units] = second
+    saves.append(pltpu.make_async_copy(net_ref, net_hbm, local.at[2]))
+    saves[-1].start()
+    for i in range(1, owners):
+        at = lastb_ref.at[owner(i)]
+        remote(at, at, s_last.at[i], r_last.at[owner(i)], spot(dp=owner(i))).wait_recv()
+    for o in range(owners):
+        lasts_ref[o * last_share : (o + 1) * last_share] = lastb_ref[o].astype(F32)
+    raw = lax.dot_general(second, lasts_ref[...], TN, **EXACT_DOT)
+    taps_ref[...] = raw * decay(length, channels, tp, channels * lines)
+    fh, fl, th, tl = fh_ref[...], fl_ref[...], th_ref, tl_ref
+    sign = sign_ref[...]
+    for j in range(DEPTH):
+        part = taps_ref[j * SEG : (j + 1) * SEG]
+        out = mm_split(fh, fl, part)
+        re, im = out[:SEG], out[SEG:]
+        filt_ref[j, 0] = re
+        filt_ref[j, 1] = im
+    for j in range(DEPTH - 1, 0, -1):
+        first = taps_ref[(j - 1) * SEG : (j - 1) * SEG + 1]
+        filt_ref[j, 0] = filt_ref[j, 0] - sign * filt_ref[j - 1, 1]
+        filt_ref[j, 1] = filt_ref[j, 1] + sign * (filt_ref[j - 1, 0] - first)
+    saves.append(pltpu.make_async_copy(filt_ref, filt_hbm, local.at[3]))
+    saves[-1].start()
+
+    for i in range(1, owners):
+        at = wb_ref.at[owner(i)]
+        remote(at, at, s_in.at[i], r_in.at[owner(i)], spot(dp=owner(i))).wait_recv()
+    for o in range(owners):
+        w_ref[:, :, o * share : (o + 1) * share] = wb_ref[o]
+    saves.append(pltpu.make_async_copy(w_ref, in_hbm, local.at[4]))
+    saves[-1].start()
+
+    def send_out(i):
+        line, own = cell(i)
+        return remote(out_in, out_hbm.at[tp, dp], s_out.at[i], r_out.at[tp, dp], spot(tp=line, dp=own))
+
+    def send_up(i):
+        return remote(up_in, rows_of(up_hbm, dp, up_share), s_up.at[i], r_up.at[dp], spot(dp=owner(i)))
+
+    def send_down(i):
+        return remote(down_in, down_hbm.at[dp], s_down.at[i], r_down.at[dp], spot(dp=owner(i)))
+
+    for i in range(1, owners * lines):
+        send_out(i).start()
+    for i in range(1, owners):
+        send_up(i).start()
+        send_down(i).start()
+    for k, (src, dst) in enumerate(
+        ((out_in, out_hbm.at[tp, dp]), (up_in, rows_of(up_hbm, dp, up_share)), (down_in, down_hbm.at[dp]))
+    ):
+        saves.append(pltpu.make_async_copy(src, dst, local.at[5 + k]))
+        saves[-1].start()
+
+    for i in range(1, 4):
+        at = xt_ref.at[ctx_at(i)]
+        remote(at, at, s_xt.at[i], r_xt.at[ctx_at(i)], spot(ctx=ctx_at(i))).wait_recv()
+    tail_ref[...] = jnp.zeros(tail_ref.shape, F32)
+    for half in range(2):
+        tails = (normalize(xt_ref[half])[0] * gain + shift).astype(BF16)
+        for g in range(3):
+            value = mm_nt(tails, w_ref[g]) + ib_ref[g : g + 1]
+            for s in range(4):
+                tail_ref[g, 4 * half + s, 6:8] = value[2 * s : 2 * s + 2]
+
+    def share_block(s, other):
+        return remote(
+            carried_ref.at[pl.ds(pl.multiple_of(s * SEG, SEG), SEG)], shared_ref.at[4 * ctx + s],
+            s_car.at[other, s], r_car.at[ctx, s], spot(ctx=other),
+        )
+
+    def forward_block(s, group):
+        at = shared_ref.at[4 * group + s]
+        return remote(at, at, s_fwd.at[s], r_car.at[group, s], spot(ctx=5 - ctx))
+
+    def mix(s, unused):
+        rows = pl.ds(pl.multiple_of(s * SEG, SEG), SEG)
+        parent = par_ref[0, ctx * blocks + s]
+        slot = jnp.where(parent >= 0, parent, 8)
+        out = []
+        for g in range(3):
+            projected = mm_nt(low_ref[rows], w_ref[g]) + ib_ref[g : g + 1]
+            proj_ref[g, rows] = projected
+            head = tail_ref[g, slot]
+            head_ref[g, s] = head
+            ext_ref[g, 0:HEADS] = head
+            ext_ref[g, HEADS : HEADS + SEG] = projected
+            mixed = (
+                sw_ref[g, 0:1] * ext_ref[g, HEADS - 2 : HEADS - 2 + SEG]
+                + sw_ref[g, 1:2] * ext_ref[g, HEADS - 1 : HEADS - 1 + SEG]
+                + sw_ref[g, 2:3] * projected
+                + sb_ref[g : g + 1]
+            )
+            if g == 0:
+                gate_ref[rows] = mixed
+            else:
+                mixed_ref[g - 1, rows] = mixed
+            out.append(mixed)
+        carried = (out[2] * out[1]).astype(BF16)
+        carried_ref[rows] = carried
+
+        @pl.when(ctx == 0)
+        def _():
+            share_block(s, 2).start()
+            share_block(s, 1).start()
+
+        @pl.when(ctx == 1)
+        def _():
+            share_block(s, 3).start()
+
+        spec = mm(fh_ref[...], carried) + mm(fl_ref[...], carried)
+        spec_ref[8 + s, 0] = spec[:SEG]
+        spec_ref[8 + s, 1] = spec[SEG:]
         return unused
 
-    lax.fori_loop(0, blocks, send, 0)
-    chain.steps(0, chain.pairs + 2 * LAG)
-    lax.fori_loop(0, blocks, wait, 0)
-    chain.drain()
-
-
-def chain_sum(part, collective):
-    rows, width = part.shape
-    return call(line_sum_kernel, sds((rows, width), BF16), [VM], LineSum.scratch(rows, width), collective,
-                traffic=rows * width * 8)(part)
-
-
-def line_gather_kernel(x_ref, out_ref, local_sem, send_sem, recv_sem):
-    tp = lax.axis_index("tp")
-    count = out_ref.shape[0]
-    greet([spot(tp=lax.rem(tp + i, count)) for i in range(1, count)])
-    copies = [
-        remote(x_ref, out_ref.at[tp], send_sem.at[i], recv_sem.at[tp], spot(tp=lax.rem(tp + i, count)))
-        for i in range(1, count)
-    ]
-    for copy in copies:
-        copy.start()
-    own = pltpu.make_async_copy(x_ref, out_ref.at[tp], local_sem)
-    own.start()
-    for i in range(1, count):
-        source = lax.rem(tp + i, count)
-        remote(x_ref, out_ref.at[source], send_sem.at[0], recv_sem.at[source], spot()).wait_recv()
-    for copy in copies:
-        copy.wait_send()
-    own.wait()
-
-
-def line_gather(x, count, collective):
-    return call(
-        line_gather_kernel,
-        sds((count,) + x.shape, x.dtype),
-        [VM],
-        [pltpu.SemaphoreType.DMA, pltpu.SemaphoreType.DMA((count,)), pltpu.SemaphoreType.DMA((count,))],
-        collective,
-        traffic=x.size * 2 * count,
-    )(x)
+    lax.fori_loop(0, blocks, mix, 0)
+    for k, (src, dst) in enumerate(((proj_ref, proj_hbm), (head_ref, head_hbm), (mixed_ref, mixed_hbm))):
+        saves.append(pltpu.make_async_copy(src, dst, local.at[8 + k]))
+        saves[-1].start()
+
+    def spectrum(slot, part):
+        out = mm(fh_ref[...], part) + mm(fl_ref[...], part)
+        spec_ref[slot, 0] = out[:SEG]
+        spec_ref[slot, 1] = out[SEG:]
+
+    spec_ref[12] = jnp.zeros(spec_ref.shape[1:], F32)
+
+    def arrived(group, s):
+        at = shared_ref.at[4 * group + s]
+        return remote(at, at, s_fwd.at[s], r_car.at[group, s], spot(ctx=ctx_at(1)))
+
+    def copy_own(group):
+        def one(s, unused):
+            spec_ref[4 * group + s] = spec_ref[8 + s]
+            return unused
+
+        lax.fori_loop(0, 4, one, 0)
+
+    def receive(group):
+        def one(s, unused):
+            arrived(group, s).wait_recv()
+            spectrum(4 * group + s, shared_ref[4 * group + s])
+            return unused
+
+        lax.fori_loop(0, 4, one, 0)
+
+    def receive_forward(group):
+        def one(s, unused):
+            arrived(group, s).wait_recv()
+            forward_block(s, group).start()
+            spectrum(4 * group + s, shared_ref[4 * group + s])
+            return unused
+
+        lax.fori_loop(0, 4, one, 0)
+
+    @pl.when(ctx == 0)
+    def _():
+        copy_own(0)
+
+    @pl.when(ctx == 1)
+    def _():
+        copy_own(1)
+        receive(0)
+
+    @pl.when(ctx == 2)
+    def _():
+        receive_forward(0)
+        receive(1)
+
+    @pl.when(ctx == 3)
+    def _():
+        receive_forward(1)
+        receive(0)
+
+    saves.append(pltpu.make_async_copy(spec_ref, spec_hbm, local.at[11]))
+    saves[-1].start()
+
+    def dest(s, unused):
+        above = lineage(par_ref, ctx * blocks + s)
+        places = [8 + s] + [jnp.where(a >= 0, a, 12) for a in above]
+        blend_all(acc_ref, [(filt_ref.at[d], spec_ref.at[places[d]]) for d in range(DEPTH)], False)
+        long_out = unpack_spectrum(th, tl, acc_ref) * (1.0 / SEG)
+        place = pl.ds(pl.multiple_of(s * SEG, SEG), SEG)
+        convolved = long_out + skip_ref[...].reshape(1, -1) * carried_ref[place].astype(F32)
+        conv_ref[place] = convolved
+        gated_ref[place] = (convolved * gate_ref[place]).astype(BF16)
+        return unused
+
+    lax.fori_loop(0, blocks, dest, 0)
+
+    for save in saves:
+        save.wait()
+    for i in range(1, owners):
+        send_in(i).wait_send()
+        send_last(i).wait_send()
+        send_up(i).wait_send()
+        send_down(i).wait_send()
+        at = rows_of(up_hbm, owner(i), up_share)
+        remote(at, at, s_up.at[i], r_up.at[owner(i)], spot(dp=owner(i))).wait_recv()
+        at = down_hbm.at[owner(i)]
+        remote(at, at, s_down.at[i], r_down.at[owner(i)], spot(dp=owner(i))).wait_recv()
+    for i in range(1, owners * lines):
+        line, own = cell(i)
+        send_out(i).wait_send()
+        at = out_hbm.at[line, own]
+        remote(at, at, s_out.at[i], r_out.at[line, own], spot(tp=line, dp=own)).wait_recv()
+    for i in range(1, 4):
+        send_xt(i).wait_send()
+
+    @pl.when(ctx == 0)
+    def _():
+        for s in range(blocks):
+            share_block(s, 2).wait_send()
+            share_block(s, 1).wait_send()
+
+    @pl.when(ctx == 1)
+    def _():
+        for s in range(blocks):
+            share_block(s, 3).wait_send()
+
+    @pl.when(ctx == 2)
+    def _():
+        for s in range(blocks):
+            forward_block(s, 0).wait_send()
+
+    @pl.when(ctx == 3)
+    def _():
+        for s in range(blocks):
+            forward_block(s, 1).wait_send()
 
 
 class OwnerSum:
@@ -724,11 +922,11 @@
 
 def back_kernel(
     par_ref, dall_ref, dconv_ref, dzero_ref, mixed_ref, low_ref, w_ref, x_ref, dpart_ref,
-    fh_ref, fl_ref, th_ref, tl_ref, sign_ref, sw_ref, skip_ref, mgain_ref, fbias_ref,
-    ft_ref, w2_ref, last_ref, freq_ref, small_ref, gskip_ref,
-    resid_hbm, dres_hbm, proj_hbm, head_hbm, spec_hbm, filt_hbm, net_hbm, sup_hbm, sdown_hbm, sout_hbm,
-    result_hbm, gradx_hbm, oup_ref, odown_ref, oout_ref, oin_ref, va_ref, vd_ref, vl_ref, vf_ref,
-    yown_ref, dcar_ref, dtaps_ref, stage_in, ppart_ref, dsum_ref, psum_ref, hd_ref, s_hd, r_hd, local, *rest,
+    fh_ref, fl_ref, th_ref, tl_ref, sign_ref, sw_ref, skip_ref,
+    ft_ref, f1_ref, f1b_ref, f2_ref, f2b_ref, freq_ref, last_ref, small_ref, gskip_ref,
+    proj_hbm, head_hbm, spec_hbm, filt_hbm, net_hbm, sup_hbm, sdown_hbm, sout_hbm,
+    dsum_ref, psum_ref, oup_ref, odown_ref, oout_ref, oin_ref, va_ref, vd_ref, vl_ref, vf_ref,
+    yown_ref, dcar_ref, dtaps_ref, stage_in, ppart_ref, w1_ref, w2_ref, hd_ref, s_hd, r_hd, local, *rest,
 ):
     width = x_ref.shape[1]
     channels = dconv_ref.shape[1]
@@ -762,6 +960,7 @@
     for job in early:
         job.begin()
     fh, fl, th, tl = fh_ref[...], fl_ref[...], th_ref, tl_ref
+    skip = skip_ref[...].reshape(1, -1)
     scale = 1.0 / SEG
 
     def put(dst, value):
@@ -793,7 +992,7 @@
         def finish(s, terms):
             blend_all(acc_ref, terms, True)
             place = pl.ds(pl.multiple_of(s * SEG, SEG), SEG)
-            dcar_ref[place] = unpack_spectrum(th, tl, acc_ref) + skip_ref[...] * dconv_ref[place]
+            dcar_ref[place] = unpack_spectrum(th, tl, acc_ref) + skip * dconv_ref[place]
 
         @pl.when(ctx == 0)
         def _():
@@ -948,13 +1147,13 @@
                 dm_ref[0:SEG] = dm
                 dm_ref[SEG : SEG + 2] = child[2 * g : 2 * g + 2]
                 d_proj = (
-                    sw_ref[3 * g + 2 : 3 * g + 3] * dm
-                    + sw_ref[3 * g + 1 : 3 * g + 2] * dm_ref[1 : 1 + SEG]
-                    + sw_ref[3 * g : 3 * g + 1] * dm_ref[2 : 2 + SEG]
+                    sw_ref[g, 2:3] * dm
+                    + sw_ref[g, 1:2] * dm_ref[1 : 1 + SEG]
+                    + sw_ref[g, 0:1] * dm_ref[2 : 2 + SEG]
                 ).astype(BF16)
                 dp_ref[g, rows] = d_proj
                 va_ref[9 + g : 10 + g] += jnp.sum(d_proj.astype(F32), axis=0, keepdims=True)
-                term = mm_nt(d_proj, w_ref[g])
+                term = mm(d_proj, w_ref[g])
                 part = term if part is None else part + term
             ppart_ref[rows] = part.astype(BF16)
             proj.send_block(s)
@@ -965,16 +1164,11 @@
             return unused
 
         lax.fori_loop(0, blocks, one, 0)
-        half = width // 2
-        piece = stage_in.shape[3]
-        for t in range(2):
-            columns = slice(t * half, (t + 1) * half)
-            for g in range(3):
-                value = mm_tn(low_ref[:, columns], dp_ref[g])
-                first = t * half // piece
-                for q in range(half // piece):
-                    owner, side = divmod(first + q, 2)
-                    stage_in[side, owner, g] = value[q * piece : (q + 1) * piece].astype(BF16)
+        rows = stage_in.shape[3]
+        for g in range(3):
+            value = mm_tn(dp_ref[g], low_ref[...])
+            for t in range(2):
+                store_columns(stage_in.at[:, :, g], t, value[t * rows : (t + 1) * rows])
 
     pl.run_scoped(
         mix_back,
@@ -992,29 +1186,24 @@
     def filter_back(net_ref):
         load = pltpu.make_async_copy(net_hbm, net_ref, local.at[1])
         load.start()
-        time_pos = lax.broadcasted_iota(jnp.int32, (DEPTH * SEG, 1), 0).astype(F32) * (1.0 / (DEPTH * SEG - 1))
-        channel = (lax.broadcasted_iota(jnp.int32, (1, channels), 1) + tp * channels).astype(F32)
-        rate = SLOW_RATE + (FAST_RATE - SLOW_RATE) * channel * (1.0 / (width - 1))
-        d_raw = dtaps_ref[...] * (jnp.exp(-time_pos * rate) + SHIFT_FLOOR)
+        d_raw = dtaps_ref[...] * decay(DEPTH * SEG, channels, tp, width)
+        extend_weights(w1_ref, f1_ref, f1b_ref)
+        extend_weights(w2_ref, f2_ref, f2b_ref)
+        freq = freq_ref[...].reshape(1, -1)
         load.wait()
-        exact = dict(precision=EXACT, preferred_element_type=F32)
-        nt = (((1,), (1,)), ((), ()))
         units = last_ref.shape[0]
-        freq = freq_ref[...]
-        l_ctx.start(jnp.dot(net_ref[5, 0:units], d_raw, **exact))
-        d_two = lax.dot_general(last_ref[...], d_raw, nt, **exact)
-        s_two = d_two * net_ref[4, 0:units]
-        p_two = s_two * freq
-        g_two = lax.dot_general(p_two, net_ref[2], nt, **exact)
-        d_one = lax.dot_general(w2_ref[...], p_two, (((0,), (0,)), ((), ())), **exact)[0:units]
-        s_one = d_one * net_ref[1, 0:units]
-        p_one = s_one * freq
-        g_one = lax.dot_general(p_one, ft_ref[...], nt, **exact)
-        g_freq = jnp.sum(s_one * net_ref[0, 0:units] + s_two * net_ref[3, 0:units], axis=1, keepdims=True)
+        l_ctx.start(jnp.dot(net_ref[3, 0:units], d_raw, **EXACT_DOT))
+        s_two = lax.dot_general(last_ref[...], d_raw, NT, **EXACT_DOT) * net_ref[2, 0:units]
+        g_two = lax.dot_general(net_ref[1], s_two, NT, **EXACT_DOT)
+        d_one = jnp.dot(w2_ref[...] * freq, s_two, **EXACT_DOT)[0:units]
+        g_one = lax.dot_general(ft_ref[...], d_one * net_ref[0, 0:units], NT, **EXACT_DOT)
+        g_freq = jnp.sum(w1_ref[...] * g_one, axis=0, keepdims=True) + jnp.sum(
+            w2_ref[...] * g_two, axis=0, keepdims=True
+        )
         vf_ref[...] = jnp.zeros(vf_ref.shape, F32)
-        vf_ref[0, :, 0 : g_one.shape[1]] = g_one
-        vf_ref[1, :, 0 : g_two.shape[1]] = g_two
-        vf_ref[2, :, 0:1] = g_freq
+        vf_ref[0, 0 : g_one.shape[0]] = g_one * freq
+        vf_ref[1, 0 : g_two.shape[0]] = g_two * freq
+        vf_ref[2, 0:1] = g_freq
         f_ctx.start(vf_ref[...])
 
     pl.run_scoped(filter_back, pltpu.VMEM(net_hbm.shape, F32))
@@ -1029,73 +1218,22 @@
     down.steps(17, 20)
     late.own()
 
-    def results(in_ref, out_ref):
-        def fetch(src, s):
-            rows = pl.ds(pl.multiple_of(s * SEG, SEG), SEG)
-            return pltpu.make_async_copy(src.at[rows], in_ref.at[lax.rem(s, 2)], local.at[lax.rem(s, 2)])
-
-        def flush(dst, s):
-            rows = pl.ds(pl.multiple_of(s * SEG, SEG), SEG)
-            return pltpu.make_async_copy(out_ref.at[s], dst.at[rows], local.at[4 + s])
-
-        fetch(resid_hbm, 0).start()
-
-        def one(s, unused):
-            rows = pl.ds(pl.multiple_of(s * SEG, SEG), SEG)
-            fetch(resid_hbm, s).wait()
-
-            @pl.when(s + 1 < blocks)
-            def _():
-                fetch(resid_hbm, s + 1).start()
-
-            proj.steps(s, s + 1)
-            down.wait_block(s)
-            out_ref[s] = in_ref[lax.rem(s, 2)] + dsum_ref[rows].astype(F32) + fbias_ref[...]
-            flush(result_hbm, s).start()
-            return unused
-
-        lax.fori_loop(0, blocks, one, 0)
-        va_ref[...] = a_dp.total()
-        vl_ref[...] = l_dp.total()
-        sums = d_dp.total()
-        vd_ref[...] = sums
-        d_tp.start(sums)
-        f_tp.start(f_dp.total())
-        fetch(dres_hbm, 0).start()
-
-        def two(s, unused):
-            rows = pl.ds(pl.multiple_of(s * SEG, SEG), SEG)
-            fetch(dres_hbm, s).wait()
-
-            @pl.when(s + 1 < blocks)
-            def _():
-                fetch(dres_hbm, s + 1).start()
-
-            xhat, spread = normalize(x_ref[rows].astype(F32))
-            proj.steps((s + 1) * PER, (s + 2) * PER)
-            proj.wait_block(s)
-            e = psum_ref[rows].astype(F32) * mgain_ref[...]
-            flush(result_hbm, s).wait()
-            out_ref[s] = in_ref[lax.rem(s, 2)] + spread * (
-                e - jnp.mean(e, axis=-1, keepdims=True) - xhat * jnp.mean(e * xhat, axis=-1, keepdims=True)
-            )
-            flush(gradx_hbm, s).start()
-
-            @pl.when(s == 0)
-            def _():
-                late.cross()
-
-            return unused
-
-        lax.fori_loop(0, blocks, two, 0)
-        for s in range(blocks):
-            flush(gradx_hbm, s).wait()
-
-    pl.run_scoped(
-        results,
-        pltpu.VMEM((2, SEG, width), F32),
-        pltpu.VMEM((blocks, SEG, width), F32),
-    )
+    proj.steps(0, 4)
+    va_ref[...] = a_dp.total()
+    last_sum = l_dp.total()
+    for o in range(owners):
+        held = vl_ref.shape[1]
+        vl_ref[o] = last_sum[o * held : (o + 1) * held]
+    sums = d_dp.total()
+    vd_ref[...] = sums
+    d_tp.start(sums)
+    f_tp.start(f_dp.total())
+    proj.steps(4, 8)
+    late.cross()
+    proj.steps(8, proj.pairs + 2 * LAG)
+    for s in range(blocks):
+        down.wait_block(s)
+        proj.wait_block(s)
     vd_ref[4:6] = d_tp.total()[4:6]
     vf_ref[...] = f_tp.total()
     for job in (a_ctx, a_dp, d_ctx, d_dp, d_tp, l_ctx, l_dp, f_ctx, f_dp, f_tp):
@@ -1106,6 +1244,52 @@
         to_ctx(i).wait_send()
     down.drain()
     proj.drain()
+
+
+def final_kernel(
+    resid_ref, dsum_ref, dres_ref, psum_ref, x_ref, gain_ref, bias_ref, va_ref, vd_ref, vl_ref, vf_ref,
+    oup_ref, odown_ref, oout_ref, oin_ref,
+    result_ref, gradx_ref, up_ref, down_ref, out_ref, in_ref,
+    mgain_ref, mshift_ref, inb_ref, sw_ref, sb_ref, f1_ref, f1b_ref, f2_ref, f2b_ref, freq_ref, last_ref,
+    skip_ref, ob_ref, fgain_ref, fshift_ref, ub_ref, db_ref,
+):
+    step = pl.program_id(0)
+
+    @pl.when(step == 0)
+    def _():
+        up_ref[...] = oup_ref[...]
+        down_ref[...] = odown_ref[...]
+        out_ref[...] = oout_ref[...]
+        rows = oin_ref.shape[2]
+        for h in range(2):
+            in_ref[:, h * rows : (h + 1) * rows] = oin_ref[h]
+        mgain_ref[...] = vd_ref[4]
+        mshift_ref[...] = vd_ref[5]
+        db_ref[...] = vd_ref[0]
+        ob_ref[...] = vd_ref[1]
+        fgain_ref[...] = vd_ref[2]
+        fshift_ref[...] = vd_ref[3]
+        ub_ref[...] = vd_ref[6]
+        for g in range(3):
+            sw_ref[g] = va_ref[3 * g : 3 * g + 3]
+        inb_ref[...] = va_ref[9:12]
+        sb_ref[...] = va_ref[12:15]
+        skip_ref[...] = va_ref[15]
+        units = f1_ref.shape[1]
+        rows_one, rows_two = f1_ref.shape[0], f2_ref.shape[0]
+        f1_ref[...] = vf_ref[0, 0:rows_one]
+        f1b_ref[...] = vf_ref[0, rows_one]
+        f2_ref[...] = vf_ref[1, 0:rows_two]
+        f2b_ref[...] = vf_ref[1, rows_two]
+        freq_ref[...] = vf_ref[2, 0]
+        last_ref[...] = vl_ref[lax.axis_index("dp")]
+
+    result_ref[...] = resid_ref[...] + dsum_ref[...].astype(F32) + bias_ref[...].reshape(1, -1)
+    xhat, spread = normalize(x_ref[...].astype(F32))
+    e = psum_ref[...].astype(F32) * gain_ref[...].reshape(1, -1)
+    gradx_ref[...] = dres_ref[...] + spread * (
+        e - jnp.mean(e, axis=-1, keepdims=True) - xhat * jnp.mean(e * xhat, axis=-1, keepdims=True)
+    )
 
 
 def body(
@@ -1125,73 +1309,70 @@
     first = lax.axis_index("ctx") * blocks
     all_blocks = parents.shape[1]
 
-    in_all = jnp.transpose(lax.all_gather(in_proj, "dp", axis=0, tiled=True), (1, 0, 2))
-    tails = lax.all_gather(x.reshape(blocks, SEG, width)[:, SEG - 2 :], "ctx", axis=0, tiled=True)
-    tails = tails.reshape(2 * all_blocks, width)
-    out_own = lax.all_gather(out_proj.T, "dp", axis=0, tiled=True)
-    out_all = lax.all_gather(out_own, "tp", axis=0)
-    up_all = lax.all_gather(feed_up, "dp", axis=0, tiled=True)
-    down_all = lax.all_gather(feed_down.T, "dp", axis=0, tiled=True)
-    last_all = lax.all_gather(filter_out, "dp", axis=0, tiled=True)
-
-    own_par = lax.dynamic_slice_in_dim(parents[0], first, blocks, 0)
-    row_id = jnp.arange(HEADS)
-    tail_id = jnp.arange(2 * all_blocks)
-    pick = (
-        (tail_id[None, None, :] == (2 * own_par[:, None] + row_id[None, :] - (HEADS - 2))[:, :, None])
-        & (row_id[None, :, None] >= HEADS - 2)
-        & (own_par[:, None, None] >= 0)
-    ).astype(F32)
+    half = hidden // 2
+    share = width // owners
     units, features = filter_one.shape[1], filter_one.shape[0]
-    feat_rows = 40
-    ft = jnp.asarray(filter_features(DEPTH * SEG, (features - 1) // 2, feat_rows))
-    w1 = jnp.concatenate(
-        [filter_one.T, filter_one_bias[:, None], jnp.zeros((units, feat_rows - features - 1), F32)], axis=1
+    feat_rows, mid_rows = 40, units + 8
+    length = DEPTH * SEG
+    ft = jnp.asarray(filter_features(length, (features - 1) // 2, feat_rows))
+    fh, fl, th, tl, sign = (jnp.asarray(t) for t in spectral_constants(SEG))
+    dma = pltpu.SemaphoreType.DMA
+    front_out = (
+        sds((total_rows, width), BF16),
+        sds((3, total_rows, channels), F32),
+        sds((3, blocks, HEADS, channels), F32),
+        sds((2, total_rows, channels), F32),
+        sds((13, 2, SEG, channels), F32),
+        sds((DEPTH, 2, SEG, channels), F32),
+        sds((4, mid_rows, length), F32),
+        sds((3, channels, width), BF16),
+        sds((tp_count, owners, channels, share), BF16),
+        sds((width, hidden), BF16),
+        sds((owners, hidden, share), BF16),
+        sds((units, channels), F32),
+        sds((total_rows, channels), F32),
+        sds((total_rows, channels), F32),
+        sds((total_rows, channels), BF16),
+        sds((total_rows, channels), BF16),
     )
-    w2 = jnp.concatenate([filter_two.T, filter_two_bias[:, None], jnp.zeros((units, 7), F32)], axis=1)
-    last = last_all.astype(F32)
-    freq = filter_freq[:, None]
-    net, filter_taps = call(
-        filter_kernel,
-        (sds((6, units + 8, DEPTH * SEG), F32), sds((DEPTH * SEG, channels), F32)),
-        [VM] * 5,
-    )(ft, w1, w2, last, freq)
-
-    row = lambda v: v.reshape(1, -1)
-    sw = short_weight.reshape(9, channels)
-    low, proj, head, mixed, carried = call(
-        mix_in_kernel,
-        (
-            sds((total_rows, width), BF16),
-            sds((3, total_rows, channels), F32),
-            sds((3, blocks, HEADS, channels), F32),
-            sds((3, total_rows, channels), F32),
-            sds((total_rows, channels), BF16),
-        ),
-        [VM] * 9,
-        [pltpu.VMEM((3, HEADS + SEG, channels), F32)],
-    )(x, tails, pick, in_all, in_bias, row(mixer_gain), row(mixer_shift), sw, short_bias)
-
-    carried_b = carried.reshape(blocks, SEG, channels)
-    incoming = lax.all_gather(carried_b, "ctx", axis=0, tiled=True)
-    fh, fl, th, tl, sign = (jnp.asarray(t) for t in spectral_constants(SEG))
-    skip = row(skip_gain)
-    conv, gated, spec, filt = call(
-        conv_fwd_kernel,
-        (
-            sds((total_rows, channels), F32),
-            sds((total_rows, channels), BF16),
-            sds((13, 2, SEG, channels), F32),
-            sds((DEPTH, 2, SEG, channels), F32),
-        ),
-        [SM] + [VM] * 10,
-        [pltpu.VMEM((2, SEG, channels), F32)],
-    )(parents, carried_b, incoming, filter_taps, mixed[0], skip, fh, fl, th, tl, sign)
-
-    gated_all = line_gather(gated, tp_count, 1)
-    piece = width // owners // 2
-    (residual, down_part, d_res, d_conv, d_zero, d_all, stage_up, stage_down, stage_out,
-     small, grad_skip) = call(
+    low, proj, head, mixed, spec, filt, net, in_all, out_all, up_all, down_all, last, gate, conv, gated, carried = call(
+        front_kernel,
+        front_out,
+        [SM] + [VM] * 23,
+        [
+            pltpu.VMEM((3, channels, width), BF16),
+            pltpu.VMEM((total_rows, width), BF16),
+            pltpu.VMEM((3, total_rows, channels), F32),
+            pltpu.VMEM((3, blocks, HEADS, channels), F32),
+            pltpu.VMEM((2, total_rows, channels), F32),
+            pltpu.VMEM((13, 2, SEG, channels), F32),
+            pltpu.VMEM((DEPTH, 2, SEG, channels), F32),
+            pltpu.VMEM((4, mid_rows, length), F32),
+            pltpu.VMEM((length, channels), F32),
+            pltpu.VMEM((8, SEG, channels), BF16),
+            pltpu.VMEM((4, 2 * blocks, width), F32),
+            pltpu.VMEM((3, 9, HEADS, channels), F32),
+            pltpu.VMEM((3, HEADS + SEG, channels), F32),
+            pltpu.VMEM((feat_rows, units), F32),
+            pltpu.VMEM((mid_rows, units), F32),
+            pltpu.VMEM((2, SEG, channels), F32),
+            pltpu.VMEM((owners,) + filter_out.shape, BF16),
+            pltpu.VMEM((owners, 3, channels, share), BF16),
+            dma((owners,)), dma((owners,)), dma((owners,)), dma((owners,)),
+            dma((owners * tp_count,)), dma((tp_count, owners)),
+            dma((owners,)), dma((owners,)), dma((owners,)), dma((owners,)),
+            dma((4,)), dma((4,)), dma((4, 4)), dma((4, 4)), dma((4,)), dma((12,)),
+        ],
+        1,
+        out_specs=(HB,) * 11 + (VM,) * 5,
+    )(
+        parents, x, jnp.transpose(in_proj, (1, 2, 0)), filter_out, out_proj, feed_up, feed_down, ft,
+        filter_one, filter_one_bias, filter_two, filter_two_bias, filter_freq, mixer_gain, mixer_shift,
+        in_bias, short_weight, short_bias, skip_gain, fh, fl, th, tl, sign,
+    )
+
+    piece = share // 2
+    residual, down_part, d_res, d_conv, d_zero, d_all, stage_up, stage_down, stage_out, small, grad_skip = call(
         feed_kernel,
         (
             sds((total_rows, width), F32),
@@ -1201,8 +1382,8 @@
             sds((total_rows, channels), F32),
             sds((all_blocks, SEG, channels), BF16),
             sds((2, owners, piece, hidden), BF16),
-            sds((2, owners, piece, hidden), BF16),
-            sds((2, owners, piece, channels), BF16),
+            sds((2, owners, half, share), BF16),
+            sds((2, owners, channels // 2, share), BF16),
             sds((8, width), F32),
             sds((1, channels), F32),
         ),
@@ -1215,69 +1396,96 @@
             pltpu.VMEM((total_rows, width), BF16),
             pltpu.VMEM((total_rows, width), BF16),
             pltpu.VMEM((blocks, SEG, channels), BF16),
-            pltpu.SemaphoreType.DMA((4, blocks)),
-            pltpu.SemaphoreType.DMA((4, blocks)),
+            pltpu.VMEM((tp_count, total_rows, channels), BF16),
+            pltpu.VMEM((tp_count, channels, width), BF16),
+            pltpu.VMEM((hidden, width), BF16),
+            dma((tp_count, blocks)), dma((tp_count, blocks)), dma((4, blocks)), dma((4, blocks)),
         ]
         + LineSum.scratch(total_rows, width),
         2,
     )(
-        gated_all, out_all, x, g, row(out_bias), row(feed_gain), row(feed_shift), up_all, row(feed_up_bias), down_all,
-        mixed[0], conv, carried,
+        gated, out_all, x, g, out_bias, feed_gain, feed_shift, up_all, feed_up_bias, down_all, gate, conv, carried
     )
-    flat_shapes = [(piece, hidden), (piece, hidden), (piece, channels), (3, piece, channels)]
+
+    shapes = [(piece, hidden), (half, share), (channels // 2, share), (3, channels // 2, share)]
     scratch = [
         pltpu.VMEM((blocks, 2, SEG, channels), F32),
         pltpu.VMEM((total_rows, channels), F32),
-        pltpu.VMEM((DEPTH * SEG, channels), F32),
-        pltpu.VMEM((2, owners, 3, piece, channels), BF16),
+        pltpu.VMEM((length, channels), F32),
+        pltpu.VMEM((2, owners) + shapes[3], BF16),
         pltpu.VMEM((total_rows, width), BF16),
-        pltpu.VMEM((total_rows, width), BF16),
-        pltpu.VMEM((total_rows, width), BF16),
+        pltpu.VMEM((feat_rows, units), F32),
+        pltpu.VMEM((mid_rows, units), F32),
         pltpu.VMEM((all_blocks, HEADS, channels), F32),
-        pltpu.SemaphoreType.DMA((4,)),
-        pltpu.SemaphoreType.DMA((4,)),
-        pltpu.SemaphoreType.DMA((8,)),
+        dma((4,)), dma((4,)), dma((8,)),
     ]
     scratch += LineSum.scratch(total_rows, width) * 2
-    for shape in flat_shapes:
+    for shape in shapes:
         scratch += OwnerSum.scratch(owners, shape)
-    for shape, axes in (
-        ((16, channels), 2), ((8, width), 3), ((units, channels), 2), ((3, units, 128), 3),
-    ):
+    smalls = ((16, channels), (8, width), (units, channels), (3, mid_rows, units))
+    for shape, axes in zip(smalls, (2, 3, 2, 3)):
         for count in (4, owners, tp_count)[:axes]:
             scratch += SmallSum.scratch(count, shape)
-    result, grad_x, own_up, own_down, own_out, own_in, va, vd, vl, vf = call(
+    down_sum, proj_sum, own_up, own_down, own_out, own_in, va, vd, vl, vf = call(
         back_kernel,
         (
-            sds((total_rows, width), F32),
-            sds((total_rows, width), F32),
-            sds((2, piece, hidden), F32),
-            sds((2, piece, hidden), F32),
-            sds((2, piece, channels), F32),
-            sds((2, 3, piece, channels), F32),
-            sds((16, channels), F32),
-            sds((8, width), F32),
-            sds((units, channels), F32),
-            sds((3, units, 128), F32),
+            sds((total_rows, width), BF16),
+            sds((total_rows, width), BF16),
+        )
+        + tuple(sds((2,) + shape, F32) for shape in shapes)
+        + (
+            sds(smalls[0], F32),
+            sds(smalls[1], F32),
+            sds((owners,) + filter_out.shape, F32),
+            sds(smalls[3], F32),
         ),
-        [SM] + [VM] * 23 + [HB] * 10,
+        [SM] + [VM] * 24 + [HB] * 8,
         scratch,
         3,
-        out_specs=(HB, HB) + (VM,) * 8,
     )(
-        parents, d_all, d_conv, d_zero, mixed[1:], low, in_all, x, down_part, fh, fl, th, tl, sign, sw, skip,
-        row(mixer_gain), row(feed_down_bias), ft, w2, last, freq, small, grad_skip,
-        residual, d_res, proj, head, spec, filt, net, stage_up, stage_down, stage_out,
+        parents, d_all, d_conv, d_zero, mixed, low, in_all, x, down_part, fh, fl, th, tl, sign, short_weight,
+        skip_gain, ft, filter_one, filter_one_bias, filter_two, filter_two_bias, filter_freq, last, small, grad_skip,
+        proj, head, spec, filt, net, stage_up, stage_down, stage_out,
     )
-    dp_index = lax.axis_index("dp")
-    own_last = lax.dynamic_slice_in_dim(vl, dp_index * (units // owners), units // owners, 0)
+
+    def by_block(*shape):
+        return pl.BlockSpec((SEG,) + shape, lambda i: (i,) + (0,) * len(shape))
+
+    def whole(v):
+        return pl.BlockSpec(v.shape, lambda i: (0,) * len(v.shape))
+
+    wide = by_block(width)
+    vectors = [
+        sds(v.shape, F32)
+        for v in (
+            mixer_gain, mixer_shift, in_bias, short_weight, short_bias, filter_one, filter_one_bias, filter_two,
+            filter_two_bias, filter_freq, filter_out, skip_gain, out_bias, feed_gain, feed_shift, feed_up_bias,
+            feed_down_bias,
+        )
+    ]
+    out = pl.pallas_call(
+        final_kernel,
+        grid=(blocks,),
+        out_shape=[
+            sds((total_rows, width), F32), sds((total_rows, width), F32), own_up, own_down, own_out,
+            sds((3, channels, share), F32),
+        ]
+        + vectors,
+        in_specs=[wide] * 5 + [whole(v) for v in (mixer_gain, feed_down_bias, va, vd, vl, vf, own_up, own_down, own_out, own_in)],
+        out_specs=[wide, wide]
+        + [whole(v) for v in (own_up, own_down, own_out, sds((3, channels, share), F32))]
+        + [whole(v) for v in vectors],
+        compiler_params=pltpu.CompilerParams(vmem_limit_bytes=LIMIT),
+    )(
+        residual, down_sum, d_res, proj_sum, x, mixer_gain, feed_down_bias, va, vd, vl, vf,
+        own_up, own_down, own_out, own_in,
+    )
+    (result, grad_x, g_up, g_down, g_out, g_in, g_mgain, g_mshift, g_inb, g_sw, g_sb, g_f1, g_f1b, g_f2, g_f2b,
+     g_freq, g_last, g_skip, g_ob, g_fgain, g_fshift, g_ub, g_db) = out
     return (
-        result[None], grad_x[None], vd[4], vd[5],
-        jnp.transpose(own_in, (0, 2, 1, 3)).reshape(width // owners, 3, channels),
-        va[9:12], va[0:9].reshape(3, 3, channels), va[12:15],
-        vf[0, :, :features].T, vf[0, :, features], vf[1, :, :units].T, vf[1, :, units], vf[2, :, 0],
-        own_last, va[15], own_out.reshape(width // owners, channels).T, vd[1], vd[2], vd[3],
-        own_up.reshape(width // owners, hidden), vd[6], own_down.reshape(width // owners, hidden).T, vd[0],
+        result[None], grad_x[None], g_mgain, g_mshift, jnp.transpose(g_in, (2, 0, 1)), g_inb, g_sw, g_sb,
+        g_f1, g_f1b, g_f2, g_f2b, g_freq, g_last, g_skip, g_out.reshape(channels, share), g_ob, g_fgain, g_fshift,
+        g_up.reshape(share, hidden), g_ub, g_down.reshape(hidden, share), g_db,
     )
 
 

time: 389 us -> 317 us (0.81)
  local copies, waits for them, and re-layouts: 48.6 us -> 0 us
  blocking collectives: 35.8 us -> 0 us
  Pallas kernels: 281 us -> 314 us
  between operations: 14.2 us -> 0.88 us
    all_gather x4 -> x0, blocking collectives: 35.8 us -> none  [the longest x1 16.3 us: body(): lax.all_gather(in_proj, 'dp', axis=0, tiled=True)]
    pallas_call x1, Pallas kernels: 80.3 us -> 108 us  [body(): call(feed_kernel, (sds((total_rows, width), F32), sds((total_rows, width)...]
    reshape x14 -> x0, local copies, waits for them, and re-layouts: 15.9 us -> none  [the longest x7 5.44 us: body(): row = lambda v: v.reshape(1, -1)]
    unnamed x43 -> x0, local copies, waits for them, and re-layouts: 12.2 us -> none
    slice x6 -> x0, local copies, waits for them, and re-layouts: 8.12 us -> none  [the longest x1 1.67 us: body(): vd[0]]
    all_gather x2 -> x0, local copies, waits for them, and re-layouts: 6.27 us -> none  [the longest x1 3.76 us: body(): incoming = lax.all_gather(carried_b, 'ctx', axis=0, tiled=True)]
    pallas_call x5 -> x3, Pallas kernels: 201 us -> 206 us  [the longest x1 129 us: body(): call(back_kernel, (sds((total_rows, width), BF16), sds((total_rows, width...]
  transfers between devices with their start and end apart: 4 -> 0, of which waited for: 0 -> 0; matrix products, arithmetic and copies ran while one was open for 7% -> 0% of each run, Pallas kernels for 18% -> 0%
where the time goes in v3:
time: 317 us; the launch traced here: 315 us
  Pallas kernels  314 us (99%)
    pallas_call x1, Pallas kernels, body(): call(back_kernel, (sds((total_rows, width), BF16), sds((total_rows, width...  129 us
    pallas_call x1, Pallas kernels, body(): call(feed_kernel, (sds((total_rows, width), F32), sds((total_rows, width)...  108 us
    pallas_call x1, Pallas kernels, body(): call(front_kernel, front_out, [SM] + [VM] * 23, [pltpu.VMEM((3, channels,...  66.5 us
    pallas_call x1, Pallas kernels, body(): pl.pallas_call(final_kernel, grid=(blocks,), out_shape=[sds((total_rows,...  10.2 us

profile of v3, /device:TPU:0, one launch (start us, length us, event | category | flops | bytes accessed | tf_op | source)
XLA Modules:
  0.0 314.9 jit_solution(15456801822860478633)
XLA Ops:
  0.7 66.5 %shard_map.461 = (bf16[1024,768]{1,0:T(8,128)(2,1)}, f32[3,1024,192]{2,1,0:T(8,128)}, f32[3,4,8,192]{3,2,1,0:T(8,128)}, f32[2,1024,192]{2,1,0:T(8,128)}, f32[13,...) custom-call(s32[1,16]{1,0:T(1,128)} %par_ref.3, ...), custom_call_target="tpu_custom_call" | custom-call | tf_op jit(solution)/shard_map/pallas_call | solution.py:1338
  67.2 108.3 %shard_map.462 = (f32[1024,768]{1,0:T(8,128)}, bf16[1024,768]{1,0:T(8,128)(2,1)}, f32[1024,768]{1,0:T(8,128)}, f32[1024,192]{1,0:T(8,128)}, f32[1024,192]{1,0:T(...) custom-call(bf16[1024,192]{1,0:T(8,128)(2,1)} %get-tuple-element.83., ...), custom_call_target="tpu_custom_call" | custom-call | tf_op jit(solution)/shard_map/pallas_call | solution.py:1375
  175.5 129.0 %shard_map.463 = (bf16[1024,768]{1,0:T(8,128)(2,1)}, bf16[1024,768]{1,0:T(8,128)(2,1)}, f32[2,192,768]{2,1,0:T(8,128)}, f32[2,384,384]{2,1,0:T(8,128)}, f32[2,96...) custom-call(s32[1,16]{1,0:T(1,128)} %par_ref.3, ...), custom_call_target="tpu_custom_call" | custom-call | tf_op jit(solution)/shard_map/pallas_call | solution.py:1429
  304.5 10.2 %shard_map.464 = (f32[1024,768]{1,0:T(8,128)}, f32[1024,768]{1,0:T(8,128)}, f32[2,192,768]{2,1,0:T(8,128)}, f32[2,384,384]{2,1,0:T(8,128)}, f32[2,96,384]{2,1,0:...) custom-call(f32[1024,768]{1,0:T(8,128)} %get-tuple-element.90.resid_, ...), custom_call_target="tpu_custom_call" | custom-call | tf_op jit(solution)/shard_map/pallas_call | solution.py:1466

commit v4 on v3

--- a/solution.py
+++ b/solution.py
@@ -22,7 +22,7 @@
 MESH = pl.DeviceIdType.MESH
 VM = pl.BlockSpec(memory_space=pltpu.VMEM)
 SM = pl.BlockSpec(memory_space=pltpu.SMEM)
-LIMIT = 60 << 20
+LIMIT = 62 << 20
 
 
 def sds(shape, dtype):
@@ -319,10 +319,12 @@
 
 
 def feed_kernel(
-    gated_ref, out_in, x_ref, g_ref, ob_ref, gain_ref, shift_ref, up_ref, ub_ref, down_in,
-    mixed_ref, conv_ref, carried_ref,
-    resid_ref, dpart_ref, dres_ref, dconv_ref, dzero_ref, dall_ref, gup_ref, gdown_ref, gout_ref,
-    small_ref, gskip_ref,
+    gated_ref, ob_ref, gain_ref, shift_ref, ub_ref,
+    out_hbm, x_hbm, g_hbm, up_hbm, down_hbm, mixed_hbm, conv_hbm, carried_hbm,
+    resid_hbm, dpart_hbm, dres_hbm, dconv_hbm, dzero_hbm, gup_hbm, gdown_hbm,
+    dall_ref, gout_ref, small_ref, gskip_ref,
+    out_in, x_ref, g_ref, up_ref, down_in, mixed_ref, conv_ref, carried_ref,
+    resid_ref, dpart_ref, dres_ref, dconv_ref, dzero_ref, gup_ref, gdown_ref, s_load, s_save, s_block,
     low_ref, hidden_ref, dpre_ref, npart_ref, nsum_ref, dmix_ref, own_ref, gall_ref, out_ref, down_ref,
     s_gate, r_gate, s_long, r_long, *line,
 ):
@@ -344,11 +346,34 @@
             spot(tp=lax.rem(tp + i, groups)),
         )
 
+    loads = [
+        pltpu.make_async_copy(src, dst, s_load.at[k])
+        for k, (src, dst) in enumerate(
+            (
+                (out_hbm, out_in), (x_hbm, x_ref), (up_hbm, up_ref), (down_hbm, down_in), (g_hbm, g_ref),
+                (mixed_hbm, mixed_ref), (conv_hbm, conv_ref), (carried_hbm, carried_ref),
+            )
+        )
+    ]
+    for load in loads:
+        load.start()
+
+    def save(k, src, dst, s):
+        rows = pl.ds(pl.multiple_of(s * SEG, SEG), SEG)
+        return pltpu.make_async_copy(src.at[rows], dst.at[rows], s_block.at[k, s])
+
+    blockwise = ((resid_ref, resid_hbm), (dres_ref, dres_hbm), (dconv_ref, dconv_hbm), (dzero_ref, dzero_hbm))
+    saves = [
+        pltpu.make_async_copy(src, dst, s_save.at[k])
+        for k, (src, dst) in enumerate(((dpart_ref, dpart_hbm), (gup_ref, gup_hbm), (gdown_ref, gdown_hbm)))
+    ]
     gall_ref[tp] = gated_ref[...]
     pl.semaphore_wait(barrier, count)
     for s in range(blocks):
         for i in range(1, groups):
             gate_copy(s, i).start()
+    for load in loads:
+        load.wait()
     for o in range(owners):
         columns = slice(o * share, (o + 1) * share)
         down_ref[:, columns] = down_in[o]
@@ -370,6 +395,7 @@
             mixed = mixed + mm(gall_ref[z, rows], out_ref[z])
         residual = x_ref[rows].astype(F32) + mixed + ob
         resid_ref[rows] = residual
+        save(0, *blockwise[0], s).start()
         low = (normalize(residual)[0] * gain + shift).astype(BF16)
         low_ref[rows] = low
         pre = mm(low, up_ref[...]) + ub
@@ -399,6 +425,9 @@
         store_rows(gup_ref, t * width // 2, mm_tn(low_ref[:, part], dpre_ref[...]))
         units = hidden_ref.shape[1] // 2
         store_columns(gdown_ref, t, mm_tn(hidden_ref[:, t * units : (t + 1) * units], g_ref[...]))
+
+    for job in saves:
+        job.start()
 
     def to_ctx(s, other):
         return remote(own_ref.at[s], dall_ref.at[ctx * blocks + s], s_long.at[other, s], r_long.at[ctx, s], spot(ctx=other))
@@ -430,6 +459,8 @@
 
         dzero_ref[rows] = d_gated * conv_ref[rows]
         gskip_ref[...] += jnp.sum(d_conv * carried_ref[rows].astype(F32), axis=0, keepdims=True)
+        for k in (1, 2, 3):
+            save(k, *blockwise[k], s).start()
         return unused
 
     lax.fori_loop(0, blocks, back, 0)
@@ -442,6 +473,11 @@
         for i in range(1, groups):
             gate_copy(s, i).wait_send()
     chain.drain()
+    for job in saves:
+        job.wait()
+    for s in range(blocks):
+        for k in range(4):
+            save(k, *blockwise[k], s).wait()
     for other in range(4):
         @pl.when(other < ctx)
         def _():
@@ -481,7 +517,8 @@
     lasts_ref, gate_ref, conv_ref, gated_ref, carried_ref,
     w_ref, low_ref, proj_ref, head_ref, mixed_ref, spec_ref, filt_ref, net_ref, taps_ref, shared_ref,
     xt_ref, tail_ref, ext_ref, w1_ref, w2_ref, acc_ref, lastb_ref, wb_ref,
-    s_in, r_in, s_last, r_last, s_out, r_out, s_up, r_up, s_down, r_down, s_xt, r_xt, s_car, r_car, s_fwd, local,
+    s_in, r_in, s_last, r_last, s_out, r_out, s_up, r_up, s_down, r_down, s_line, r_line, s_swap,
+    s_xt, r_xt, s_car, r_car, s_fwd, local,
 ):
     total_rows, width = x_ref.shape
     channels = ib_ref.shape[1]
@@ -591,21 +628,59 @@
     saves.append(pltpu.make_async_copy(w_ref, in_hbm, local.at[4]))
     saves[-1].start()
 
-    def send_out(i):
-        line, own = cell(i)
-        return remote(out_in, out_hbm.at[tp, dp], s_out.at[i], r_out.at[tp, dp], spot(tp=line, dp=own))
+    low_half = lax.rem(ctx, 2)
+    mate = spot(ctx=ctx + 1 - 2 * low_half)
+
+    def half_of(ref, half):
+        size = ref.shape[0] // 2
+        return ref.at[pl.ds(pl.multiple_of(half * size, 16), size)]
+
+    def up_half(ref, half):
+        size = ref.shape[1] // 2
+        return ref.at[:, pl.ds(pl.multiple_of(half * size, size), size)]
+
+    def line_out(i):
+        return remote(
+            out_in, out_hbm.at[tp, dp], s_line.at[i], r_line.at[tp], spot(tp=lax.rem(tp + i, lines))
+        )
+
+    def send_out(i, j):
+        return remote(
+            half_of(out_in, low_half), half_of(out_hbm.at[tp, dp], low_half), s_out.at[i, j], r_out.at[0, tp, dp],
+            spot(dp=owner(i), tp=lax.rem(tp + j, lines)),
+        )
+
+    def swap_out(i, line):
+        at = half_of(out_hbm.at[line, owner(i)], low_half)
+        return remote(at, at, s_swap.at[2, i, line], r_out.at[1, line, owner(i)], mate)
 
     def send_up(i):
-        return remote(up_in, rows_of(up_hbm, dp, up_share), s_up.at[i], r_up.at[dp], spot(dp=owner(i)))
+        return remote(
+            up_half(up_in, low_half), up_half(rows_of(up_hbm, dp, up_share), low_half), s_up.at[i], r_up.at[0, dp],
+            spot(dp=owner(i)),
+        )
+
+    def swap_up(i):
+        at = up_half(rows_of(up_hbm, owner(i), up_share), low_half)
+        return remote(at, at, s_swap.at[0, i, 0], r_up.at[1, owner(i)], mate)
 
     def send_down(i):
-        return remote(down_in, down_hbm.at[dp], s_down.at[i], r_down.at[dp], spot(dp=owner(i)))
-
-    for i in range(1, owners * lines):
-        send_out(i).start()
+        return remote(
+            half_of(down_in, low_half), half_of(down_hbm.at[dp], low_half), s_down.at[i], r_down.at[0, dp],
+            spot(dp=owner(i)),
+        )
+
+    def swap_down(i):
+        at = half_of(down_hbm.at[owner(i)], low_half)
+        return remote(at, at, s_swap.at[1, i, 0], r_down.at[1, owner(i)], mate)
+
     for i in range(1, owners):
+        for j in range(lines):
+            send_out(i, j).start()
         send_up(i).start()
         send_down(i).start()
+    for i in range(1, lines):
+        line_out(i).start()
     for k, (src, dst) in enumerate(
         ((out_in, out_hbm.at[tp, dp]), (up_in, rows_of(up_hbm, dp, up_share)), (down_in, down_hbm.at[dp]))
     ):
@@ -748,22 +823,43 @@
 
     lax.fori_loop(0, blocks, dest, 0)
 
+    def take_halves(stage, half):
+        for i in range(1, owners):
+            who = owner(i)
+            at = up_half(rows_of(up_hbm, who, up_share), half)
+            remote(at, at, s_up.at[i], r_up.at[stage, who], mate).wait_recv()
+            if stage == 0:
+                swap_up(i).start()
+            at = half_of(down_hbm.at[who], half)
+            remote(at, at, s_down.at[i], r_down.at[stage, who], mate).wait_recv()
+            if stage == 0:
+                swap_down(i).start()
+            for line in range(lines):
+                at = half_of(out_hbm.at[line, who], half)
+                remote(at, at, s_out.at[i, line], r_out.at[stage, line, who], mate).wait_recv()
+                if stage == 0:
+                    swap_out(i, line).start()
+
+    take_halves(0, low_half)
+
     for save in saves:
         save.wait()
+    take_halves(1, 1 - low_half)
     for i in range(1, owners):
         send_in(i).wait_send()
         send_last(i).wait_send()
         send_up(i).wait_send()
         send_down(i).wait_send()
-        at = rows_of(up_hbm, owner(i), up_share)
-        remote(at, at, s_up.at[i], r_up.at[owner(i)], spot(dp=owner(i))).wait_recv()
-        at = down_hbm.at[owner(i)]
-        remote(at, at, s_down.at[i], r_down.at[owner(i)], spot(dp=owner(i))).wait_recv()
-    for i in range(1, owners * lines):
-        line, own = cell(i)
-        send_out(i).wait_send()
-        at = out_hbm.at[line, own]
-        remote(at, at, s_out.at[i], r_out.at[line, own], spot(tp=line, dp=own)).wait_recv()
+        swap_up(i).wait_send()
+        swap_down(i).wait_send()
+        for j in range(lines):
+            send_out(i, j).wait_send()
+            swap_out(i, j).wait_send()
+    for i in range(1, lines):
+        line_out(i).wait_send()
+        line = lax.rem(tp + i, lines)
+        at = out_hbm.at[line, dp]
+        remote(at, at, s_line.at[i], r_line.at[line], mate).wait_recv()
     for i in range(1, 4):
         send_xt(i).wait_send()
 
@@ -921,12 +1017,13 @@
 
 
 def back_kernel(
-    par_ref, dall_ref, dconv_ref, dzero_ref, mixed_ref, low_ref, w_ref, x_ref, dpart_ref,
+    par_ref, dall_ref, dconv_ref, dzero_ref, dpart_ref,
     fh_ref, fl_ref, th_ref, tl_ref, sign_ref, sw_ref, skip_ref,
     ft_ref, f1_ref, f1b_ref, f2_ref, f2b_ref, freq_ref, last_ref, small_ref, gskip_ref,
-    proj_hbm, head_hbm, spec_hbm, filt_hbm, net_hbm, sup_hbm, sdown_hbm, sout_hbm,
+    mixed_hbm, low_hbm, w_hbm, x_hbm, proj_hbm, head_hbm, spec_hbm, filt_hbm, net_hbm, sup_hbm, sdown_hbm, sout_hbm,
     dsum_ref, psum_ref, oup_ref, odown_ref, oout_ref, oin_ref, va_ref, vd_ref, vl_ref, vf_ref,
-    yown_ref, dcar_ref, dtaps_ref, stage_in, ppart_ref, w1_ref, w2_ref, hd_ref, s_hd, r_hd, local, *rest,
+    yown_ref, dcar_ref, dtaps_ref, stage_in, ppart_ref, w1_ref, w2_ref,
+    mixed_ref, low_ref, w_ref, x_ref, hd_ref, s_hd, r_hd, local, *rest,
 ):
     width = x_ref.shape[1]
     channels = dconv_ref.shape[1]
@@ -957,6 +1054,12 @@
     pl.semaphore_wait(barrier, count)
     for s in range(blocks):
         down.send_block(s)
+    loads = [
+        pltpu.make_async_copy(src, dst, local.at[4 + k])
+        for k, (src, dst) in enumerate(((mixed_hbm, mixed_ref), (w_hbm, w_ref), (x_hbm, x_ref), (low_hbm, low_ref)))
+    ]
+    for load in loads:
+        load.start()
     for job in early:
         job.begin()
     fh, fl, th, tl = fh_ref[...], fl_ref[...], th_ref, tl_ref
@@ -1039,6 +1142,9 @@
         pltpu.VMEM((2, SEG, channels), F32),
     )
 
+    for load in loads:
+        load.wait()
+
     def to_ctx(i):
         at = hd_ref.at[pl.ds(ctx * blocks, blocks)]
         return remote(at, at, s_hd.at[i], r_hd.at[ctx], spot(ctx=lax.rem(ctx + i, 4)))
@@ -1052,52 +1158,9 @@
         hd_ref[ctx * blocks + s, 6:8] = jnp.zeros((2, channels), F32)
     for i in range(1, 4):
         to_ctx(i).start()
-    down.steps(0, 3)
+    down.steps(0, 4)
     for job in early:
         job.pair()
-
-    def conv_filters(spec_ref, dfilt_ref):
-        load = pltpu.make_async_copy(spec_hbm, spec_ref, local.at[0])
-        load.start()
-        load.wait()
-
-        @pl.when(ctx == 0)
-        def _():
-            for d in range(4):
-                blend_all(dfilt_ref.at[d], [(spec_ref.at[8 + s - d], yown_ref.at[s]) for s in range(d, 4)], True)
-            dfilt_ref[4:6] = jnp.zeros((2, 2, SEG, channels), F32)
-
-        @pl.when(ctx > 0)
-        def _():
-            places = []
-            for s in range(blocks):
-                above = lineage(par_ref, ctx * blocks + s)
-                places.append([8 + s] + [jnp.where(a >= 0, a, 12) for a in above])
-            for d in range(DEPTH):
-                terms = [(spec_ref.at[places[s][d]], yown_ref.at[s]) for s in range(blocks)]
-                blend_all(dfilt_ref.at[d], terms, True)
-
-        down.steps(3, 6)
-        sign = sign_ref[...]
-        first_row = lax.broadcasted_iota(jnp.int32, (SEG, 1), 0) == 0
-        for j in range(DEPTH):
-            fix = None
-            if j + 1 < DEPTH:
-                nr, ni = dfilt_ref[j + 1, 0], dfilt_ref[j + 1, 1]
-                fix = jnp.sum(sign * ni, axis=0, keepdims=True)
-                dfilt_ref[j, 0] = dfilt_ref[j, 0] + sign * ni
-                dfilt_ref[j, 1] = dfilt_ref[j, 1] - sign * nr
-            taps = unpack_spectrum(th, tl, dfilt_ref.at[j])
-            if fix is not None:
-                taps = jnp.where(first_row, taps - fix, taps)
-            dtaps_ref[j * SEG : (j + 1) * SEG] = taps
-
-    pl.run_scoped(
-        conv_filters,
-        pltpu.VMEM((13, 2, SEG, channels), F32),
-        pltpu.VMEM((DEPTH, 2, SEG, channels), F32),
-    )
-    down.steps(6, 9)
 
     va_ref[...] = jnp.zeros(va_ref.shape, F32)
     vd_ref[...] = small_ref[...]
@@ -1107,81 +1170,123 @@
         at = hd_ref.at[pl.ds(other * blocks, blocks)]
         remote(at, at, s_hd.at[i], r_hd.at[other], spot(ctx=other)).wait_recv()
 
-    def mix_back(dp_ref, ext_ref, dm_ref, pin_ref, hin_ref):
-        load_heads = pltpu.make_async_copy(head_hbm, hin_ref, local.at[1])
-        load_heads.start()
-
-        def fetch(s):
-            rows = pl.ds(pl.multiple_of(s * SEG, SEG), SEG)
-            return pltpu.make_async_copy(proj_hbm.at[:, rows], pin_ref.at[lax.rem(s, 2)], local.at[2 + lax.rem(s, 2)])
-
-        fetch(0).start()
-        load_heads.wait()
-
-        def one(s, unused):
-            rows = pl.ds(pl.multiple_of(s * SEG, SEG), SEG)
-            slot = lax.rem(s, 2)
-            fetch(s).wait()
-
-            @pl.when(s + 1 < blocks)
+    def with_spectra(spec_ref):
+        pltpu.make_async_copy(spec_hbm, spec_ref, local.at[0]).start()
+
+        def mix_back(dp_ref, ext_ref, dm_ref, pin_ref, hin_ref):
+            load_heads = pltpu.make_async_copy(head_hbm, hin_ref, local.at[1])
+            load_heads.start()
+
+            def fetch(s):
+                rows = pl.ds(pl.multiple_of(s * SEG, SEG), SEG)
+                return pltpu.make_async_copy(proj_hbm.at[:, rows], pin_ref.at[lax.rem(s, 2)], local.at[2 + lax.rem(s, 2)])
+
+            fetch(0).start()
+            load_heads.wait()
+
+            def one(s, unused):
+                rows = pl.ds(pl.multiple_of(s * SEG, SEG), SEG)
+                slot = lax.rem(s, 2)
+                fetch(s).wait()
+
+                @pl.when(s + 1 < blocks)
+                def _():
+                    fetch(s + 1).start()
+
+                mine = ctx * blocks + s
+                child = None
+                for b in range(1, 16):
+                    term = jnp.where(par_ref[0, b] == mine, 1.0, 0.0) * hd_ref[b]
+                    child = term if child is None else child + term
+                part = None
+                for g in range(3):
+                    if g == 0:
+                        dm = dzero_ref[rows]
+                    else:
+                        dm = dcar_ref[rows] * mixed_ref[2 - g, rows]
+                    ext_ref[0:HEADS] = hin_ref[g, s]
+                    ext_ref[HEADS : HEADS + SEG] = pin_ref[slot, g]
+                    for k in range(3):
+                        piece = ext_ref[HEADS - 2 + k : HEADS - 2 + k + SEG]
+                        va_ref[3 * g + k : 3 * g + k + 1] += jnp.sum(piece * dm, axis=0, keepdims=True)
+                    va_ref[12 + g : 13 + g] += jnp.sum(dm, axis=0, keepdims=True)
+                    dm_ref[0:SEG] = dm
+                    dm_ref[SEG : SEG + 2] = child[2 * g : 2 * g + 2]
+                    d_proj = (
+                        sw_ref[g, 2:3] * dm
+                        + sw_ref[g, 1:2] * dm_ref[1 : 1 + SEG]
+                        + sw_ref[g, 0:1] * dm_ref[2 : 2 + SEG]
+                    ).astype(BF16)
+                    dp_ref[g, rows] = d_proj
+                    va_ref[9 + g : 10 + g] += jnp.sum(d_proj.astype(F32), axis=0, keepdims=True)
+                    term = mm(d_proj, w_ref[g])
+                    part = term if part is None else part + term
+                ppart_ref[rows] = part.astype(BF16)
+                proj.send_block(s)
+                xhat = normalize(x_ref[rows].astype(F32))[0]
+                vd_ref[4:5] += jnp.sum(part * xhat, axis=0, keepdims=True)
+                vd_ref[5:6] += jnp.sum(part, axis=0, keepdims=True)
+                down.steps(4 + s, 5 + s)
+                return unused
+
+            lax.fori_loop(0, blocks, one, 0)
+            rows = stage_in.shape[3]
+            for g in range(3):
+                value = mm_tn(dp_ref[g], low_ref[...])
+                for t in range(2):
+                    store_columns(stage_in.at[:, :, g], t, value[t * rows : (t + 1) * rows])
+
+        pl.run_scoped(
+            mix_back,
+            pltpu.VMEM((3, total_rows, channels), BF16),
+            pltpu.VMEM((HEADS + SEG, channels), F32),
+            pltpu.VMEM((HEADS + SEG, channels), F32),
+            pltpu.VMEM((2, 3, SEG, channels), F32),
+            pltpu.VMEM((3, blocks, HEADS, channels), F32),
+        )
+        a_ctx.start(va_ref[...])
+        d_ctx.start(vd_ref[...])
+        late.begin()
+        down.steps(8, 11)
+
+        def conv_filters(dfilt_ref):
+            pltpu.make_async_copy(spec_hbm, spec_ref, local.at[0]).wait()
+
+            @pl.when(ctx == 0)
             def _():
-                fetch(s + 1).start()
-
-            mine = ctx * blocks + s
-            child = None
-            for b in range(1, 16):
-                term = jnp.where(par_ref[0, b] == mine, 1.0, 0.0) * hd_ref[b]
-                child = term if child is None else child + term
-            part = None
-            for g in range(3):
-                if g == 0:
-                    dm = dzero_ref[rows]
-                else:
-                    dm = dcar_ref[rows] * mixed_ref[2 - g, rows]
-                ext_ref[0:HEADS] = hin_ref[g, s]
-                ext_ref[HEADS : HEADS + SEG] = pin_ref[slot, g]
-                for k in range(3):
-                    piece = ext_ref[HEADS - 2 + k : HEADS - 2 + k + SEG]
-                    va_ref[3 * g + k : 3 * g + k + 1] += jnp.sum(piece * dm, axis=0, keepdims=True)
-                va_ref[12 + g : 13 + g] += jnp.sum(dm, axis=0, keepdims=True)
-                dm_ref[0:SEG] = dm
-                dm_ref[SEG : SEG + 2] = child[2 * g : 2 * g + 2]
-                d_proj = (
-                    sw_ref[g, 2:3] * dm
-                    + sw_ref[g, 1:2] * dm_ref[1 : 1 + SEG]
-                    + sw_ref[g, 0:1] * dm_ref[2 : 2 + SEG]
-                ).astype(BF16)
-                dp_ref[g, rows] = d_proj
-                va_ref[9 + g : 10 + g] += jnp.sum(d_proj.astype(F32), axis=0, keepdims=True)
-                term = mm(d_proj, w_ref[g])
-                part = term if part is None else part + term
-            ppart_ref[rows] = part.astype(BF16)
-            proj.send_block(s)
-            xhat = normalize(x_ref[rows].astype(F32))[0]
-            vd_ref[4:5] += jnp.sum(part * xhat, axis=0, keepdims=True)
-            vd_ref[5:6] += jnp.sum(part, axis=0, keepdims=True)
-            down.steps(9 + s, 10 + s)
-            return unused
-
-        lax.fori_loop(0, blocks, one, 0)
-        rows = stage_in.shape[3]
-        for g in range(3):
-            value = mm_tn(dp_ref[g], low_ref[...])
-            for t in range(2):
-                store_columns(stage_in.at[:, :, g], t, value[t * rows : (t + 1) * rows])
-
-    pl.run_scoped(
-        mix_back,
-        pltpu.VMEM((3, total_rows, channels), BF16),
-        pltpu.VMEM((HEADS + SEG, channels), F32),
-        pltpu.VMEM((HEADS + SEG, channels), F32),
-        pltpu.VMEM((2, 3, SEG, channels), F32),
-        pltpu.VMEM((3, blocks, HEADS, channels), F32),
-    )
-    late.begin()
-    for job in early:
-        job.own()
-    down.steps(13, 15)
+                for d in range(4):
+                    blend_all(dfilt_ref.at[d], [(spec_ref.at[8 + s - d], yown_ref.at[s]) for s in range(d, 4)], True)
+                dfilt_ref[4:6] = jnp.zeros((2, 2, SEG, channels), F32)
+
+            @pl.when(ctx > 0)
+            def _():
+                places = []
+                for s in range(blocks):
+                    above = lineage(par_ref, ctx * blocks + s)
+                    places.append([8 + s] + [jnp.where(a >= 0, a, 12) for a in above])
+                for d in range(DEPTH):
+                    terms = [(spec_ref.at[places[s][d]], yown_ref.at[s]) for s in range(blocks)]
+                    blend_all(dfilt_ref.at[d], terms, True)
+
+            down.steps(11, 12)
+            sign = sign_ref[...]
+            first_row = lax.broadcasted_iota(jnp.int32, (SEG, 1), 0) == 0
+            for j in range(DEPTH):
+                fix = None
+                if j + 1 < DEPTH:
+                    nr, ni = dfilt_ref[j + 1, 0], dfilt_ref[j + 1, 1]
+                    fix = jnp.sum(sign * ni, axis=0, keepdims=True)
+                    dfilt_ref[j, 0] = dfilt_ref[j, 0] + sign * ni
+                    dfilt_ref[j, 1] = dfilt_ref[j, 1] - sign * nr
+                taps = unpack_spectrum(th, tl, dfilt_ref.at[j])
+                if fix is not None:
+                    taps = jnp.where(first_row, taps - fix, taps)
+                dtaps_ref[j * SEG : (j + 1) * SEG] = taps
+
+        pl.run_scoped(conv_filters, pltpu.VMEM((DEPTH, 2, SEG, channels), F32))
+
+    pl.run_scoped(with_spectra, pltpu.VMEM((13, 2, SEG, channels), F32))
+    down.steps(12, 13)
 
     def filter_back(net_ref):
         load = pltpu.make_async_copy(net_hbm, net_ref, local.at[1])
@@ -1201,40 +1306,55 @@
             w2_ref[...] * g_two, axis=0, keepdims=True
         )
         vf_ref[...] = jnp.zeros(vf_ref.shape, F32)
-        vf_ref[0, 0 : g_one.shape[0]] = g_one * freq
-        vf_ref[1, 0 : g_two.shape[0]] = g_two * freq
-        vf_ref[2, 0:1] = g_freq
+        vf_ref[0 : g_one.shape[0], 0:units] = g_one * freq
+        vf_ref[0 : g_two.shape[0], units : 2 * units] = g_two * freq
+        vf_ref[g_two.shape[0] : g_two.shape[0] + 1, 0:units] = g_freq
         f_ctx.start(vf_ref[...])
 
     pl.run_scoped(filter_back, pltpu.VMEM(net_hbm.shape, F32))
-    a_ctx.start(va_ref[...])
-    d_ctx.start(vd_ref[...])
-    late.pair()
-    down.steps(15, 17)
-    for job in early:
-        job.cross()
-    for one, two in ((a_ctx, a_dp), (d_ctx, d_dp), (l_ctx, l_dp), (f_ctx, f_dp)):
-        two.start(one.total())
-    down.steps(17, 20)
-    late.own()
-
-    proj.steps(0, 4)
-    va_ref[...] = a_dp.total()
-    last_sum = l_dp.total()
-    for o in range(owners):
-        held = vl_ref.shape[1]
-        vl_ref[o] = last_sum[o * held : (o + 1) * held]
-    sums = d_dp.total()
-    vd_ref[...] = sums
-    d_tp.start(sums)
-    f_tp.start(f_dp.total())
-    proj.steps(4, 8)
+
+    def early_own():
+        for job in early:
+            job.own()
+
+    def early_cross():
+        for job in early:
+            job.cross()
+
+    def vectors():
+        a_dp.start(a_ctx.total())
+        d_dp.start(d_ctx.total())
+
+    def networks():
+        l_dp.start(l_ctx.total())
+        f_dp.start(f_ctx.total())
+        late.own()
+
+    def gains():
+        va_ref[...] = a_dp.total()
+        sums = d_dp.total()
+        vd_ref[...] = sums
+        d_tp.start(sums[4:6])
+
+    def last_layer():
+        f_tp.start(f_dp.total())
+        last_sum = l_dp.total()
+        for o in range(owners):
+            held = vl_ref.shape[1]
+            vl_ref[o] = last_sum[o * held : (o + 1) * held]
+
+    jobs = (early_own, late.pair, early_cross, vectors, networks, gains, last_layer)
+    for k, job in enumerate(jobs):
+        down.steps(13 + k, 14 + k)
+        proj.steps(2 * k, 2 * k + 2)
+        job()
+    proj.steps(14, 17)
     late.cross()
-    proj.steps(8, proj.pairs + 2 * LAG)
+    proj.steps(17, proj.pairs + 2 * LAG)
     for s in range(blocks):
         down.wait_block(s)
         proj.wait_block(s)
-    vd_ref[4:6] = d_tp.total()[4:6]
+    vd_ref[4:6] = d_tp.total()
     vf_ref[...] = f_tp.total()
     for job in (a_ctx, a_dp, d_ctx, d_dp, d_tp, l_ctx, l_dp, f_ctx, f_dp, f_tp):
         job.finish()
@@ -1277,11 +1397,11 @@
         skip_ref[...] = va_ref[15]
         units = f1_ref.shape[1]
         rows_one, rows_two = f1_ref.shape[0], f2_ref.shape[0]
-        f1_ref[...] = vf_ref[0, 0:rows_one]
-        f1b_ref[...] = vf_ref[0, rows_one]
-        f2_ref[...] = vf_ref[1, 0:rows_two]
-        f2b_ref[...] = vf_ref[1, rows_two]
-        freq_ref[...] = vf_ref[2, 0]
+        f1_ref[...] = vf_ref[0:rows_one, 0:units]
+        f1b_ref[...] = vf_ref[rows_one, 0:units]
+        f2_ref[...] = vf_ref[0:rows_two, units : 2 * units]
+        f2b_ref[...] = vf_ref[rows_two, units : 2 * units]
+        freq_ref[...] = vf_ref[rows_two + 8, 0:units]
         last_ref[...] = vl_ref[lax.axis_index("dp")]
 
     result_ref[...] = resid_ref[...] + dsum_ref[...].astype(F32) + bias_ref[...].reshape(1, -1)
@@ -1359,8 +1479,9 @@
             pltpu.VMEM((owners,) + filter_out.shape, BF16),
             pltpu.VMEM((owners, 3, channels, share), BF16),
             dma((owners,)), dma((owners,)), dma((owners,)), dma((owners,)),
-            dma((owners * tp_count,)), dma((tp_count, owners)),
-            dma((owners,)), dma((owners,)), dma((owners,)), dma((owners,)),
+            dma((owners, tp_count)), dma((2, tp_count, owners)),
+            dma((owners,)), dma((2, owners)), dma((owners,)), dma((2, owners)),
+            dma((tp_count,)), dma((tp_count,)), dma((3, owners, tp_count)),
             dma((4,)), dma((4,)), dma((4, 4)), dma((4, 4)), dma((4,)), dma((12,)),
         ],
         1,
@@ -1372,23 +1493,34 @@
     )
 
     piece = share // 2
-    residual, down_part, d_res, d_conv, d_zero, d_all, stage_up, stage_down, stage_out, small, grad_skip = call(
+    feed_big = [
+        sds((total_rows, width), F32),
+        sds((total_rows, width), BF16),
+        sds((total_rows, width), F32),
+        sds((total_rows, channels), F32),
+        sds((total_rows, channels), F32),
+        sds((2, owners, piece, hidden), BF16),
+        sds((2, owners, half, share), BF16),
+    ]
+    feed_in = (out_all, x, g, up_all, down_all, gate, conv, carried)
+
+    def held(v):
+        return pltpu.VMEM(v.shape, v.dtype)
+
+    residual, down_part, d_res, d_conv, d_zero, stage_up, stage_down, d_all, stage_out, small, grad_skip = call(
         feed_kernel,
-        (
-            sds((total_rows, width), F32),
-            sds((total_rows, width), BF16),
-            sds((total_rows, width), F32),
-            sds((total_rows, channels), F32),
-            sds((total_rows, channels), F32),
+        feed_big
+        + [
             sds((all_blocks, SEG, channels), BF16),
-            sds((2, owners, piece, hidden), BF16),
-            sds((2, owners, half, share), BF16),
             sds((2, owners, channels // 2, share), BF16),
             sds((8, width), F32),
             sds((1, channels), F32),
-        ),
-        [VM] * 13,
-        [
+        ],
+        [VM] * 5 + [HB] * 8,
+        [held(v) for v in feed_in]
+        + [held(v) for v in feed_big]
+        + [dma((8,)), dma((3,)), dma((4, blocks))]
+        + [
             pltpu.VMEM((total_rows, width), BF16),
             pltpu.VMEM((total_rows, hidden), BF16),
             pltpu.VMEM((total_rows, hidden), BF16),
@@ -1403,9 +1535,8 @@
         ]
         + LineSum.scratch(total_rows, width),
         2,
-    )(
-        gated, out_all, x, g, out_bias, feed_gain, feed_shift, up_all, feed_up_bias, down_all, gate, conv, carried
-    )
+        out_specs=(HB,) * 7 + (VM,) * 4,
+    )(gated, out_bias, feed_gain, feed_shift, feed_up_bias, *feed_in)
 
     shapes = [(piece, hidden), (half, share), (channels // 2, share), (3, channels // 2, share)]
     scratch = [
@@ -1416,15 +1547,19 @@
         pltpu.VMEM((total_rows, width), BF16),
         pltpu.VMEM((feat_rows, units), F32),
         pltpu.VMEM((mid_rows, units), F32),
+        held(mixed), held(low), held(in_all), held(x),
         pltpu.VMEM((all_blocks, HEADS, channels), F32),
         dma((4,)), dma((4,)), dma((8,)),
     ]
     scratch += LineSum.scratch(total_rows, width) * 2
     for shape in shapes:
         scratch += OwnerSum.scratch(owners, shape)
-    smalls = ((16, channels), (8, width), (units, channels), (3, mid_rows, units))
-    for shape, axes in zip(smalls, (2, 3, 2, 3)):
-        for count in (4, owners, tp_count)[:axes]:
+    smalls = ((16, channels), (8, width), (units, channels), (mid_rows + 8, 2 * units))
+    for counts, shape in (
+        ((4, owners), smalls[0]), ((4, owners), smalls[1]), ((tp_count,), (2, width)), ((4, owners), smalls[2]),
+        ((4, owners, tp_count), smalls[3]),
+    ):
+        for count in counts:
             scratch += SmallSum.scratch(count, shape)
     down_sum, proj_sum, own_up, own_down, own_out, own_in, va, vd, vl, vf = call(
         back_kernel,
@@ -1439,13 +1574,13 @@
             sds((owners,) + filter_out.shape, F32),
             sds(smalls[3], F32),
         ),
-        [SM] + [VM] * 24 + [HB] * 8,
+        [SM] + [VM] * 20 + [HB] * 12,
         scratch,
         3,
     )(
-        parents, d_all, d_conv, d_zero, mixed, low, in_all, x, down_part, fh, fl, th, tl, sign, short_weight,
+        parents, d_all, d_conv, d_zero, down_part, fh, fl, th, tl, sign, short_weight,
         skip_gain, ft, filter_one, filter_one_bias, filter_two, filter_two_bias, filter_freq, last, small, grad_skip,
-        proj, head, spec, filt, net, stage_up, stage_down, stage_out,
+        mixed, low, in_all, x, proj, head, spec, filt, net, stage_up, stage_down, stage_out,
     )
 
     def by_block(*shape):

time: 317 us -> 277 us (0.87)
  Pallas kernels: 314 us -> 276 us
    pallas_call x1, Pallas kernels: 66.5 us -> 49.9 us  [body(): call(front_kernel, front_out, [SM] + [VM] * 23, [pltpu.VMEM((3, channels,...]
    pallas_call x1, Pallas kernels: 129 us -> 112 us  [body(): call(back_kernel, (sds((total_rows, width), BF16), sds((total_rows, width...]
    pallas_call x1, Pallas kernels: 108 us -> 103 us  [body(): call(feed_kernel, feed_big + [sds((all_blocks, SEG, channels), BF16), sds...]
where the time goes in v4:
time: 277 us
  Pallas kernels  276 us (100%)
    pallas_call x1, Pallas kernels, body(): call(back_kernel, (sds((total_rows, width), BF16), sds((total_rows, width...  112 us
    pallas_call x1, Pallas kernels, body(): call(feed_kernel, feed_big + [sds((all_blocks, SEG, channels), BF16), sds...  103 us
    pallas_call x1, Pallas kernels, body(): call(front_kernel, front_out, [SM] + [VM] * 23, [pltpu.VMEM((3, channels,...  49.9 us
    pallas_call x1, Pallas kernels, body(): pl.pallas_call(final_kernel, grid=(blocks,), out_shape=[sds((total_rows,...  10.2 us

profile of v4, /device:TPU:0, one launch (start us, length us, event | category | flops | bytes accessed | tf_op | source)
XLA Modules:
  0.0 276.6 jit_solution(13400707838493671936)
XLA Ops:
  0.7 49.9 %shard_map.461 = (bf16[1024,768]{1,0:T(8,128)(2,1)}, f32[3,1024,192]{2,1,0:T(8,128)}, f32[3,4,8,192]{3,2,1,0:T(8,128)}, f32[2,1024,192]{2,1,0:T(8,128)}, f32[13,...) custom-call(s32[1,16]{1,0:T(1,128)} %par_ref.3, ...), custom_call_target="tpu_custom_call" | custom-call | tf_op jit(solution)/shard_map/pallas_call | solution.py:1458
  50.5 103.3 %shard_map.462 = (f32[1024,768]{1,0:T(8,128)}, bf16[1024,768]{1,0:T(8,128)(2,1)}, f32[1024,768]{1,0:T(8,128)}, f32[1024,192]{1,0:T(8,128)}, f32[1024,192]{1,0:T(...) custom-call(bf16[1024,192]{1,0:T(8,128)(2,1)} %get-tuple-element.83., ...), custom_call_target="tpu_custom_call" | custom-call | tf_op jit(solution)/shard_map/pallas_call | solution.py:1510
  153.8 112.4 %shard_map.463 = (bf16[1024,768]{1,0:T(8,128)(2,1)}, bf16[1024,768]{1,0:T(8,128)(2,1)}, f32[2,192,768]{2,1,0:T(8,128)}, f32[2,384,384]{2,1,0:T(8,128)}, f32[2,96...) custom-call(s32[1,16]{1,0:T(1,128)} %par_ref.3, ...), custom_call_target="tpu_custom_call" | custom-call | tf_op jit(solution)/shard_map/pallas_call | solution.py:1564
  266.2 10.2 %shard_map.464 = (f32[1024,768]{1,0:T(8,128)}, f32[1024,768]{1,0:T(8,128)}, f32[2,192,768]{2,1,0:T(8,128)}, f32[2,384,384]{2,1,0:T(8,128)}, f32[2,96,384]{2,1,0:...) custom-call(f32[1024,768]{1,0:T(8,128)} %get-tuple-element.90.resid_, ...), custom_call_target="tpu_custom_call" | custom-call | tf_op jit(solution)/shard_map/pallas_call | solution.py:1601

commit v5 on v4

--- a/solution.py
+++ b/solution.py
@@ -319,12 +319,12 @@
 
 
 def feed_kernel(
-    gated_ref, ob_ref, gain_ref, shift_ref, ub_ref,
-    out_hbm, x_hbm, g_hbm, up_hbm, down_hbm, mixed_hbm, conv_hbm, carried_hbm,
+    gated_ref, ob_ref, gain_ref, shift_ref, ub_ref, own_down,
+    out_hbm, x_hbm, g_hbm, up_hbm, mixed_hbm, conv_hbm, carried_hbm,
     resid_hbm, dpart_hbm, dres_hbm, dconv_hbm, dzero_hbm, gup_hbm, gdown_hbm,
     dall_ref, gout_ref, small_ref, gskip_ref,
-    out_in, x_ref, g_ref, up_ref, down_in, mixed_ref, conv_ref, carried_ref,
-    resid_ref, dpart_ref, dres_ref, dconv_ref, dzero_ref, gup_ref, gdown_ref, s_load, s_save, s_block,
+    out_in, x_ref, g_ref, up_ref, mixed_ref, conv_ref, carried_ref,
+    resid_ref, dpart_ref, dres_ref, dconv_ref, dzero_ref, gup_ref, gdown_ref, s_load, s_save, s_block, down_in, s_down, r_down,
     low_ref, hidden_ref, dpre_ref, npart_ref, nsum_ref, dmix_ref, own_ref, gall_ref, out_ref, down_ref,
     s_gate, r_gate, s_long, r_long, *line,
 ):
@@ -332,25 +332,61 @@
     width = x_ref.shape[1]
     blocks = x_ref.shape[0] // SEG
     share = width // owners
-    tp, ctx = lax.axis_index("tp"), lax.axis_index("ctx")
+    tp, ctx, dp = lax.axis_index("tp"), lax.axis_index("ctx"), lax.axis_index("dp")
     chain = LineSum(npart_ref, nsum_ref, line)
     barrier, count = signal_all(
         [spot(tp=lax.rem(tp + i, groups)) for i in range(1, groups)]
         + [spot(ctx=lax.rem(ctx + i, 4)) for i in range(1, 4)]
+        + [spot(dp=lax.rem(dp + i, owners)) for i in range(1, owners)]
     )
+
+    low_half = lax.rem(ctx, 2)
+    pair_mate = spot(ctx=ctx + 1 - 2 * low_half)
+
+    def owner(i):
+        return lax.rem(dp + i, owners)
+
+    def half_of(ref, half):
+        size = ref.shape[0] // 2
+        return ref.at[pl.ds(pl.multiple_of(half * size, 16), size)]
+
+    def send_down(i):
+        return remote(
+            half_of(own_down, low_half), half_of(down_in.at[dp], low_half), s_down.at[0, i], r_down.at[0, dp],
+            spot(dp=owner(i)),
+        )
+
+    def swap_down(i):
+        at = half_of(down_in.at[owner(i)], low_half)
+        return remote(at, at, s_down.at[1, i], r_down.at[1, owner(i)], pair_mate)
+
+    def got_down(stage, i, half):
+        at = half_of(down_in.at[owner(i)], half)
+        return remote(at, at, s_down.at[0, i], r_down.at[stage, owner(i)], pair_mate)
+
+    far = jnp.where(tp < 2, tp + 2, tp - 2)
+    beyond = jnp.where(chain.side == 0, 3, 0)
+    other = jnp.where(chain.inner, 3 - tp, far)
+    near = jnp.where(chain.inner, jnp.where(chain.side == 0, 0, 3), jnp.where(chain.side == 0, 1, 2))
 
     def gate_copy(s, i):
         rows = pl.ds(pl.multiple_of(s * SEG, SEG), SEG)
-        return remote(
-            gated_ref.at[rows], gall_ref.at[tp, rows], s_gate.at[i, s], r_gate.at[tp, s],
-            spot(tp=lax.rem(tp + i, groups)),
-        )
+        where = chain.mate if i == 0 else spot(tp=other)
+        return remote(gated_ref.at[rows], gall_ref.at[tp, rows], s_gate.at[i, s], r_gate.at[tp, s], where)
+
+    def gate_pass(s, i, source):
+        at = gall_ref.at[source, pl.ds(pl.multiple_of(s * SEG, SEG), SEG)]
+        return remote(at, at, s_gate.at[2 + i, s], r_gate.at[source, s], chain.mate)
+
+    def gate_from(s, source):
+        at = gall_ref.at[source, pl.ds(pl.multiple_of(s * SEG, SEG), SEG)]
+        return remote(at, at, s_gate.at[0, s], r_gate.at[source, s], chain.mate)
 
     loads = [
         pltpu.make_async_copy(src, dst, s_load.at[k])
         for k, (src, dst) in enumerate(
             (
-                (out_hbm, out_in), (x_hbm, x_ref), (up_hbm, up_ref), (down_hbm, down_in), (g_hbm, g_ref),
+                (out_hbm, out_in), (x_hbm, x_ref), (up_hbm, up_ref), (g_hbm, g_ref),
                 (mixed_hbm, mixed_ref), (conv_hbm, conv_ref), (carried_hbm, carried_ref),
             )
         )
@@ -370,13 +406,15 @@
     gall_ref[tp] = gated_ref[...]
     pl.semaphore_wait(barrier, count)
     for s in range(blocks):
-        for i in range(1, groups):
-            gate_copy(s, i).start()
+        for i in range(2):
+            gate_copy(s, 1 - i).start()
+    for i in range(1, owners):
+        send_down(i).start()
+    down_in[dp] = own_down[...]
     for load in loads:
         load.wait()
     for o in range(owners):
         columns = slice(o * share, (o + 1) * share)
-        down_ref[:, columns] = down_in[o]
         for z in range(groups):
             out_ref[z, :, columns] = out_in[z, o]
     ob, gain, shift = (ref[...].reshape(1, -1) for ref in (ob_ref, gain_ref, shift_ref))
@@ -386,10 +424,20 @@
 
     def core(s, unused):
         rows = pl.ds(pl.multiple_of(s * SEG, SEG), SEG)
-        for i in range(1, groups):
-            source = lax.rem(tp + i, groups)
-            at = gall_ref.at[source, rows]
-            remote(at, at, s_gate.at[i, s], r_gate.at[source, s], chain.mate).wait_recv()
+
+        @pl.when(chain.inner)
+        def _():
+            for i, source in enumerate((3 - tp, beyond)):
+                gate_from(s, source).wait_recv()
+                gate_pass(s, i, source).start()
+            gate_from(s, near).wait_recv()
+
+        @pl.when(chain.outer)
+        def _():
+            gate_from(s, near).wait_recv()
+            gate_from(s, 3 - near).wait_recv()
+            gate_from(s, 3 - tp).wait_recv()
+
         mixed = mm(gall_ref[0, rows], out_ref[0])
         for z in range(1, groups):
             mixed = mixed + mm(gall_ref[z, rows], out_ref[z])
@@ -402,6 +450,17 @@
         cdf = 0.5 * (1.0 + lax.erf(pre * math.sqrt(0.5)))
         hidden_ref[rows] = (pre * cdf).astype(BF16)
         slope = cdf + pre * (jnp.exp(-0.5 * pre * pre) * (1.0 / math.sqrt(2.0 * math.pi)))
+
+        @pl.when(s == 0)
+        def _():
+            for i in range(1, owners):
+                got_down(0, i, low_half).wait_recv()
+                swap_down(i).start()
+            for i in range(1, owners):
+                got_down(1, i, 1 - low_half).wait_recv()
+            for o in range(owners):
+                down_ref[:, o * share : (o + 1) * share] = down_in[o]
+
         grad = g_ref[rows]
         d_pre = (mm_nt(grad, down_ref[...]) * slope).astype(BF16)
         dpre_ref[rows] = d_pre
@@ -469,9 +528,19 @@
     value = mm_tn(gated_ref[...], dmix_ref[...])
     for t in range(2):
         store_columns(gout_ref, t, value[t * gout_ref.shape[2] : (t + 1) * gout_ref.shape[2]])
+    for i in range(1, owners):
+        send_down(i).wait_send()
+        swap_down(i).wait_send()
     for s in range(blocks):
-        for i in range(1, groups):
+        for i in range(2):
             gate_copy(s, i).wait_send()
+
+    @pl.when(chain.inner)
+    def _():
+        for s in range(blocks):
+            for i, source in enumerate((3 - tp, beyond)):
+                gate_pass(s, i, source).wait_send()
+
     chain.drain()
     for job in saves:
         job.wait()
@@ -491,6 +560,21 @@
                 remote(at, at, s_long.at[other, s], r_long.at[other, s], chain.mate).wait_recv()
 
 
+def sine_cosine(angle):
+    turns = jnp.floor(angle * (2.0 / math.pi) + 0.5)
+    rest = ((angle - turns * 1.5703125) - turns * 4.837512969970703125e-4) - turns * 7.54978995489188216e-8
+    square = rest * rest
+    sine = ((-1.9515295891e-4 * square + 8.3321608736e-3) * square - 1.6666654611e-1) * square * rest + rest
+    cosine = ((2.443315711809948e-5 * square - 1.388731625493765e-3) * square + 4.166664568298827e-2) * (
+        square * square
+    ) + (1.0 - 0.5 * square)
+    quarter = turns - 4.0 * jnp.floor(turns * 0.25)
+    odd = jnp.logical_or(quarter == 1.0, quarter == 3.0)
+    middle = jnp.logical_or(quarter == 1.0, quarter == 2.0)
+    sine, cosine = jnp.where(odd, cosine, sine), jnp.where(odd, sine, cosine)
+    return jnp.where(quarter >= 2.0, -sine, sine), jnp.where(middle, -cosine, cosine)
+
+
 def extend_weights(ref, weight, bias):
     rows = weight.shape[0]
     ref[...] = jnp.zeros(ref.shape, F32)
@@ -511,13 +595,13 @@
 
 
 def front_kernel(
-    par_ref, x_ref, win_ref, last_ref, out_in, up_in, down_in, ft_ref, f1_ref, f1b_ref, f2_ref, f2b_ref, freq_ref,
+    par_ref, x_ref, win_ref, last_ref, out_in, up_in, ft_ref, f1_ref, f1b_ref, f2_ref, f2b_ref, freq_ref,
     gain_ref, shift_ref, ib_ref, sw_ref, sb_ref, skip_ref, fh_ref, fl_ref, th_ref, tl_ref, sign_ref,
-    low_hbm, proj_hbm, head_hbm, mixed_hbm, spec_hbm, filt_hbm, net_hbm, in_hbm, out_hbm, up_hbm, down_hbm,
+    low_hbm, proj_hbm, head_hbm, mixed_hbm, spec_hbm, filt_hbm, net_hbm, in_hbm, out_hbm, up_hbm,
     lasts_ref, gate_ref, conv_ref, gated_ref, carried_ref,
     w_ref, low_ref, proj_ref, head_ref, mixed_ref, spec_ref, filt_ref, net_ref, taps_ref, shared_ref,
     xt_ref, tail_ref, ext_ref, w1_ref, w2_ref, acc_ref, lastb_ref, wb_ref,
-    s_in, r_in, s_last, r_last, s_out, r_out, s_up, r_up, s_down, r_down, s_line, r_line, s_swap,
+    s_in, r_in, s_last, r_last, s_out, r_out, s_up, r_up, s_line, r_line, s_swap,
     s_xt, r_xt, s_car, r_car, s_fwd, local,
 ):
     total_rows, width = x_ref.shape
@@ -548,8 +632,26 @@
     def rows_of(ref, who, size):
         return ref.at[pl.ds(pl.multiple_of(who * size, size), size)]
 
+    low_half = lax.rem(ctx, 2)
+    mate = spot(ctx=ctx + 1 - 2 * low_half)
+
+    def in_half(ref, half):
+        size = channels // 2
+        return ref.at[:, pl.ds(pl.multiple_of(half * size, 16), size)]
+
     def send_in(i):
-        return remote(win_ref, wb_ref.at[dp], s_in.at[i], r_in.at[dp], spot(dp=owner(i)))
+        return remote(
+            in_half(win_ref, low_half), in_half(wb_ref.at[dp], low_half), s_in.at[0, i], r_in.at[0, dp],
+            spot(dp=owner(i)),
+        )
+
+    def swap_in(i):
+        at = in_half(wb_ref.at[owner(i)], low_half)
+        return remote(at, at, s_in.at[1, i], r_in.at[1, owner(i)], mate)
+
+    def got_in(stage, i, half):
+        at = in_half(wb_ref.at[owner(i)], half)
+        return remote(at, at, s_in.at[0, i], r_in.at[stage, owner(i)], mate)
 
     def send_last(i):
         return remote(last_ref, lastb_ref.at[dp], s_last.at[i], r_last.at[dp], spot(dp=owner(i)))
@@ -588,13 +690,12 @@
     freq = freq_ref[...].reshape(1, -1)
     net_ref[...] = jnp.zeros(net_ref.shape, F32)
     angle = lax.dot_general(w1_ref[...] * freq, ft_ref[...], TN, **EXACT_DOT)
-    net_ref[0, 0:units] = jnp.cos(angle)
-    net_ref[1, 0:units] = jnp.sin(angle)
+    first, net_ref[0, 0:units] = sine_cosine(angle)
+    net_ref[1, 0:units] = first
     pad = net_ref.shape[1] - units
     net_ref[1, units:] = jnp.where(lax.broadcasted_iota(jnp.int32, (pad, length), 0) == 0, 1.0, 0.0)
     angle = lax.dot_general(w2_ref[...] * freq, net_ref[1], TN, **EXACT_DOT)
-    net_ref[2, 0:units] = jnp.cos(angle)
-    second = jnp.sin(angle)
+    second, net_ref[2, 0:units] = sine_cosine(angle)
     net_ref[3, 0:units] = second
     saves.append(pltpu.make_async_copy(net_ref, net_hbm, local.at[2]))
     saves[-1].start()
@@ -620,17 +721,6 @@
     saves.append(pltpu.make_async_copy(filt_ref, filt_hbm, local.at[3]))
     saves[-1].start()
 
-    for i in range(1, owners):
-        at = wb_ref.at[owner(i)]
-        remote(at, at, s_in.at[i], r_in.at[owner(i)], spot(dp=owner(i))).wait_recv()
-    for o in range(owners):
-        w_ref[:, :, o * share : (o + 1) * share] = wb_ref[o]
-    saves.append(pltpu.make_async_copy(w_ref, in_hbm, local.at[4]))
-    saves[-1].start()
-
-    low_half = lax.rem(ctx, 2)
-    mate = spot(ctx=ctx + 1 - 2 * low_half)
-
     def half_of(ref, half):
         size = ref.shape[0] // 2
         return ref.at[pl.ds(pl.multiple_of(half * size, 16), size)]
@@ -664,25 +754,23 @@
         at = up_half(rows_of(up_hbm, owner(i), up_share), low_half)
         return remote(at, at, s_swap.at[0, i, 0], r_up.at[1, owner(i)], mate)
 
-    def send_down(i):
-        return remote(
-            half_of(down_in, low_half), half_of(down_hbm.at[dp], low_half), s_down.at[i], r_down.at[0, dp],
-            spot(dp=owner(i)),
-        )
-
-    def swap_down(i):
-        at = half_of(down_hbm.at[owner(i)], low_half)
-        return remote(at, at, s_swap.at[1, i, 0], r_down.at[1, owner(i)], mate)
-
     for i in range(1, owners):
+        got_in(0, i, low_half).wait_recv()
+        swap_in(i).start()
+        send_up(i).start()
         for j in range(lines):
             send_out(i, j).start()
-        send_up(i).start()
-        send_down(i).start()
     for i in range(1, lines):
         line_out(i).start()
+    for i in range(1, owners):
+        got_in(1, i, 1 - low_half).wait_recv()
+    for o in range(owners):
+        w_ref[:, :, o * share : (o + 1) * share] = wb_ref[o]
+    saves.append(pltpu.make_async_copy(w_ref, in_hbm, local.at[4]))
+    saves[-1].start()
+
     for k, (src, dst) in enumerate(
-        ((out_in, out_hbm.at[tp, dp]), (up_in, rows_of(up_hbm, dp, up_share)), (down_in, down_hbm.at[dp]))
+        ((out_in, out_hbm.at[tp, dp]), (up_in, rows_of(up_hbm, dp, up_share)))
     ):
         saves.append(pltpu.make_async_copy(src, dst, local.at[5 + k]))
         saves[-1].start()
@@ -830,10 +918,6 @@
             remote(at, at, s_up.at[i], r_up.at[stage, who], mate).wait_recv()
             if stage == 0:
                 swap_up(i).start()
-            at = half_of(down_hbm.at[who], half)
-            remote(at, at, s_down.at[i], r_down.at[stage, who], mate).wait_recv()
-            if stage == 0:
-                swap_down(i).start()
             for line in range(lines):
                 at = half_of(out_hbm.at[line, who], half)
                 remote(at, at, s_out.at[i, line], r_out.at[stage, line, who], mate).wait_recv()
@@ -847,11 +931,10 @@
     take_halves(1, 1 - low_half)
     for i in range(1, owners):
         send_in(i).wait_send()
+        swap_in(i).wait_send()
         send_last(i).wait_send()
         send_up(i).wait_send()
-        send_down(i).wait_send()
         swap_up(i).wait_send()
-        swap_down(i).wait_send()
         for j in range(lines):
             send_out(i, j).wait_send()
             swap_out(i, j).wait_send()
@@ -906,12 +989,14 @@
             pltpu.SemaphoreType.DMA,
             pltpu.SemaphoreType.DMA,
             pltpu.SemaphoreType.DMA,
+            pltpu.SemaphoreType.DMA((2,)),
+            pltpu.VMEM((2,) + shape, F32),
         ]
 
     def __init__(self, stage, out, scratch):
-        self.stage, self.result = stage, out
+        self.stage, self.out, self.result = stage, out, scratch[-1]
         self.recv, self.keep, self.parts, self.y_own, self.y_in = scratch[:5]
-        self.sems = scratch[5:]
+        self.sems = scratch[5:-1]
         self.owners = stage.shape[1]
         self.dp, ctx = lax.axis_index("dp"), lax.axis_index("ctx")
         self.low = lax.rem(ctx, 2)
@@ -940,6 +1025,9 @@
     def to_back(self):
         at = self.result.at[self.low]
         return remote(at, at, self.sems[7], self.sems[8], self.mate)
+
+    def save(self, half):
+        return pltpu.make_async_copy(self.result.at[half], self.out.at[half], self.sems[9].at[half])
 
     def begin(self):
         self.to_mate().start()
@@ -965,6 +1053,12 @@
         self.to_across().wait_recv()
         self.result[self.low] = self.y_own[...].astype(F32) + self.y_in[...].astype(F32)
         self.to_back().start()
+        self.save(self.low).start()
+
+    def whole(self):
+        at = self.result.at[1 - self.low]
+        remote(at, at, self.sems[7], self.sems[8], self.mate).wait_recv()
+        self.save(1 - self.low).start()
 
     def finish(self):
         self.to_mate().wait_send()
@@ -972,8 +1066,8 @@
             self.to_owner(i).wait_send()
         self.to_across().wait_send()
         self.to_back().wait_send()
-        at = self.result.at[1 - self.low]
-        remote(at, at, self.sems[7], self.sems[8], self.mate).wait_recv()
+        self.save(self.low).wait()
+        self.save(1 - self.low).wait()
 
 
 class SmallSum:
@@ -1040,8 +1134,8 @@
 
     down = LineSum(dpart_ref, dsum_ref, take(11))
     proj = LineSum(ppart_ref, psum_ref, take(11))
-    early = [OwnerSum(s, o, take(14)) for s, o in ((sup_hbm, oup_ref), (sdown_hbm, odown_ref), (sout_hbm, oout_ref))]
-    late = OwnerSum(stage_in, oin_ref, take(14))
+    early = [OwnerSum(s, o, take(16)) for s, o in ((sup_hbm, oup_ref), (sdown_hbm, odown_ref), (sout_hbm, oout_ref))]
+    late = OwnerSum(stage_in, oin_ref, take(16))
     a_ctx, a_dp = SmallSum("ctx", take(3)), SmallSum("dp", take(3))
     d_ctx, d_dp, d_tp = SmallSum("ctx", take(3)), SmallSum("dp", take(3)), SmallSum("tp", take(3))
     l_ctx, l_dp = SmallSum("ctx", take(3)), SmallSum("dp", take(3))
@@ -1337,6 +1431,8 @@
         d_tp.start(sums[4:6])
 
     def last_layer():
+        for job in early:
+            job.whole()
         f_tp.start(f_dp.total())
         last_sum = l_dp.total()
         for o in range(owners):
@@ -1351,6 +1447,7 @@
     proj.steps(14, 17)
     late.cross()
     proj.steps(17, proj.pairs + 2 * LAG)
+    late.whole()
     for s in range(blocks):
         down.wait_block(s)
         proj.wait_block(s)
@@ -1448,17 +1545,16 @@
         sds((3, channels, width), BF16),
         sds((tp_count, owners, channels, share), BF16),
         sds((width, hidden), BF16),
-        sds((owners, hidden, share), BF16),
         sds((units, channels), F32),
         sds((total_rows, channels), F32),
         sds((total_rows, channels), F32),
         sds((total_rows, channels), BF16),
         sds((total_rows, channels), BF16),
     )
-    low, proj, head, mixed, spec, filt, net, in_all, out_all, up_all, down_all, last, gate, conv, gated, carried = call(
+    low, proj, head, mixed, spec, filt, net, in_all, out_all, up_all, last, gate, conv, gated, carried = call(
         front_kernel,
         front_out,
-        [SM] + [VM] * 23,
+        [SM] + [VM] * 22,
         [
             pltpu.VMEM((3, channels, width), BF16),
             pltpu.VMEM((total_rows, width), BF16),
@@ -1478,16 +1574,16 @@
             pltpu.VMEM((2, SEG, channels), F32),
             pltpu.VMEM((owners,) + filter_out.shape, BF16),
             pltpu.VMEM((owners, 3, channels, share), BF16),
-            dma((owners,)), dma((owners,)), dma((owners,)), dma((owners,)),
+            dma((2, owners)), dma((2, owners)), dma((owners,)), dma((owners,)),
             dma((owners, tp_count)), dma((2, tp_count, owners)),
-            dma((owners,)), dma((2, owners)), dma((owners,)), dma((2, owners)),
+            dma((owners,)), dma((2, owners)),
             dma((tp_count,)), dma((tp_count,)), dma((3, owners, tp_count)),
             dma((4,)), dma((4,)), dma((4, 4)), dma((4, 4)), dma((4,)), dma((12,)),
         ],
         1,
-        out_specs=(HB,) * 11 + (VM,) * 5,
+        out_specs=(HB,) * 10 + (VM,) * 5,
     )(
-        parents, x, jnp.transpose(in_proj, (1, 2, 0)), filter_out, out_proj, feed_up, feed_down, ft,
+        parents, x, jnp.transpose(in_proj, (1, 2, 0)), filter_out, out_proj, feed_up, ft,
         filter_one, filter_one_bias, filter_two, filter_two_bias, filter_freq, mixer_gain, mixer_shift,
         in_bias, short_weight, short_bias, skip_gain, fh, fl, th, tl, sign,
     )
@@ -1502,7 +1598,7 @@
         sds((2, owners, piece, hidden), BF16),
         sds((2, owners, half, share), BF16),
     ]
-    feed_in = (out_all, x, g, up_all, down_all, gate, conv, carried)
+    feed_in = (out_all, x, g, up_all, gate, conv, carried)
 
     def held(v):
         return pltpu.VMEM(v.shape, v.dtype)
@@ -1516,10 +1612,11 @@
             sds((8, width), F32),
             sds((1, channels), F32),
         ],
-        [VM] * 5 + [HB] * 8,
+        [VM] * 6 + [HB] * 7,
         [held(v) for v in feed_in]
         + [held(v) for v in feed_big]
-        + [dma((8,)), dma((3,)), dma((4, blocks))]
+        + [dma((8,)), dma((3,)), dma((4, blocks)), pltpu.VMEM((owners, hidden, share), BF16)]
+        + [dma((2, owners)), dma((2, owners))]
         + [
             pltpu.VMEM((total_rows, width), BF16),
             pltpu.VMEM((total_rows, hidden), BF16),
@@ -1536,7 +1633,7 @@
         + LineSum.scratch(total_rows, width),
         2,
         out_specs=(HB,) * 7 + (VM,) * 4,
-    )(gated, out_bias, feed_gain, feed_shift, feed_up_bias, *feed_in)
+    )(gated, out_bias, feed_gain, feed_shift, feed_up_bias, feed_down, *feed_in)
 
     shapes = [(piece, hidden), (half, share), (channels // 2, share), (3, channels // 2, share)]
     scratch = [
@@ -1577,6 +1674,7 @@
         [SM] + [VM] * 20 + [HB] * 12,
         scratch,
         3,
+        out_specs=(VM, VM, HB, HB, HB, HB, VM, VM, VM, VM),
     )(
         parents, d_all, d_conv, d_zero, down_part, fh, fl, th, tl, sign, short_weight,
         skip_gain, ft, filter_one, filter_one_bias, filter_two, filter_two_bias, filter_freq, last, small, grad_skip,

time: 277 us -> 254 us (0.917)
  Pallas kernels: 276 us -> 253 us
    pallas_call x1, Pallas kernels: 103 us -> 90 us  [body(): call(feed_kernel, feed_big + [sds((all_blocks, SEG, channels), BF16), sds...]
    pallas_call x1, Pallas kernels: 49.9 us -> 41.1 us  [body(): call(front_kernel, front_out, [SM] + [VM] * 22, [pltpu.VMEM((3, channels,...]
where the time goes in v5:
time: 254 us
  Pallas kernels  253 us (100%)
    pallas_call x1, Pallas kernels, body(): call(back_kernel, (sds((total_rows, width), BF16), sds((total_rows, width...  112 us
    pallas_call x1, Pallas kernels, body(): call(feed_kernel, feed_big + [sds((all_blocks, SEG, channels), BF16), sds...  90 us
    pallas_call x1, Pallas kernels, body(): call(front_kernel, front_out, [SM] + [VM] * 22, [pltpu.VMEM((3, channels,...  41.1 us
    pallas_call x1, Pallas kernels, body(): pl.pallas_call(final_kernel, grid=(blocks,), out_shape=[sds((total_rows,...  10.2 us

profile of v5, /device:TPU:0, one launch (start us, length us, event | category | flops | bytes accessed | tf_op | source)
XLA Modules:
  0.0 253.8 jit_solution(6315831525282844647)
XLA Ops:
  0.7 41.1 %shard_map.461 = (bf16[1024,768]{1,0:T(8,128)(2,1)}, f32[3,1024,192]{2,1,0:T(8,128)}, f32[3,4,8,192]{3,2,1,0:T(8,128)}, f32[2,1024,192]{2,1,0:T(8,128)}, f32[13,...) custom-call(s32[1,16]{1,0:T(1,128)} %par_ref.3, ...), custom_call_target="tpu_custom_call" | custom-call | tf_op jit(solution)/shard_map/pallas_call | solution.py:1554
  41.8 90.0 %shard_map.462 = (f32[1024,768]{1,0:T(8,128)}, bf16[1024,768]{1,0:T(8,128)(2,1)}, f32[1024,768]{1,0:T(8,128)}, f32[1024,192]{1,0:T(8,128)}, f32[1024,192]{1,0:T(...) custom-call(bf16[1024,192]{1,0:T(8,128)(2,1)} %get-tuple-element.82., ...), custom_call_target="tpu_custom_call" | custom-call | tf_op jit(solution)/shard_map/pallas_call | solution.py:1606
  131.8 111.5 %shard_map.463 = (bf16[1024,768]{1,0:T(8,128)(2,1)}, bf16[1024,768]{1,0:T(8,128)(2,1)}, f32[2,192,768]{2,1,0:T(8,128)}, f32[2,384,384]{2,1,0:T(8,128)}, f32[2,96...) custom-call(s32[1,16]{1,0:T(1,128)} %par_ref.3, ...), custom_call_target="tpu_custom_call" | custom-call | tf_op jit(solution)/shard_map/pallas_call | solution.py:1661
  243.4 10.2 %shard_map.464 = (f32[1024,768]{1,0:T(8,128)}, f32[1024,768]{1,0:T(8,128)}, f32[2,192,768]{2,1,0:T(8,128)}, f32[2,384,384]{2,1,0:T(8,128)}, f32[2,96,384]{2,1,0:...) custom-call(f32[1024,768]{1,0:T(8,128)} %get-tuple-element.88.resid_, ...), custom_call_target="tpu_custom_call" | custom-call | tf_op jit(solution)/shard_map/pallas_call | solution.py:1699

commit v6 on v5

--- a/solution.py
+++ b/solution.py
@@ -166,6 +166,7 @@
 
 
 CHUNK = 32
+HALF = SEG // 2
 PER = SEG // (2 * CHUNK)
 LAG = 2
 
@@ -174,7 +175,19 @@
     return pl.ds(pl.multiple_of(c * CHUNK, CHUNK), CHUNK)
 
 
-class LineSum:
+class LineRole:
+    def __init__(self):
+        tp = lax.axis_index("tp")
+        self.inner = jnp.logical_and(tp > 0, tp < 3)
+        self.outer = jnp.logical_not(self.inner)
+        self.side = jnp.where(tp < 2, 0, 1)
+        near = jnp.where(self.side == 0, 0, 3)
+        far = jnp.where(self.side == 0, 1, 2)
+        self.mate = spot(tp=jnp.where(self.inner, near, far))
+        self.cross = spot(tp=3 - tp)
+
+
+class LineSum(LineRole):
     scratch_count = 11
 
     @staticmethod
@@ -187,18 +200,11 @@
         ] + [pltpu.SemaphoreType.DMA((count,)) for _ in range(8)]
 
     def __init__(self, part, total, scratch):
+        super().__init__()
         self.part, self.total = part, total
         self.end, self.mid, self.out = scratch[:3]
         self.sems = scratch[3:]
         self.pairs = part.shape[0] // (2 * CHUNK)
-        tp = lax.axis_index("tp")
-        self.inner = jnp.logical_and(tp > 0, tp < 3)
-        self.outer = jnp.logical_not(self.inner)
-        self.side = jnp.where(tp < 2, 0, 1)
-        near = jnp.where(self.side == 0, 0, 3)
-        far = jnp.where(self.side == 0, 1, 2)
-        self.mate = spot(tp=jnp.where(self.inner, near, far))
-        self.cross = spot(tp=3 - tp)
 
     def to_mid(self, c):
         return remote(self.part.at[chunk(c)], self.end.at[chunk(c)], self.sems[0].at[c], self.sems[1].at[c], self.mate)
@@ -276,6 +282,15 @@
 
             lax.fori_loop(0, 2 * PER, one, 0)
 
+    def wait_half(self, h):
+        @pl.when(self.outer)
+        def _():
+            def one(i, unused):
+                self.final_end(h * PER + i).wait_recv()
+                return unused
+
+            lax.fori_loop(0, PER, one, 0)
+
     def drain(self):
         @pl.when(self.outer)
         def _():
@@ -320,20 +335,18 @@
 
 def feed_kernel(
     gated_ref, ob_ref, gain_ref, shift_ref, ub_ref, own_down,
-    out_hbm, x_hbm, g_hbm, up_hbm, mixed_hbm, conv_hbm, carried_hbm,
-    resid_hbm, dpart_hbm, dres_hbm, dconv_hbm, dzero_hbm, gup_hbm, gdown_hbm,
-    dall_ref, gout_ref, small_ref, gskip_ref,
-    out_in, x_ref, g_ref, up_ref, mixed_ref, conv_ref, carried_ref,
-    resid_ref, dpart_ref, dres_ref, dconv_ref, dzero_ref, gup_ref, gdown_ref, s_load, s_save, s_block, down_in, s_down, r_down,
-    low_ref, hidden_ref, dpre_ref, npart_ref, nsum_ref, dmix_ref, own_ref, gall_ref, out_ref, down_ref,
-    s_gate, r_gate, s_long, r_long, *line,
+    out_hbm, x_hbm, g_hbm, up_hbm,
+    resid_hbm, npart_hbm, dpart_hbm, gup_hbm, gdown_hbm, small_ref,
+    out_in, x_ref, g_ref, up_ref,
+    resid_ref, npart_ref, dpart_ref, gup_ref, gdown_ref, s_load, s_save, s_block, down_in, s_down, r_down,
+    up_acc, down_acc, gall_ref, out_ref, down_ref, s_gate, r_gate,
 ):
     groups, owners = out_in.shape[:2]
     width = x_ref.shape[1]
     blocks = x_ref.shape[0] // SEG
     share = width // owners
     tp, ctx, dp = lax.axis_index("tp"), lax.axis_index("ctx"), lax.axis_index("dp")
-    chain = LineSum(npart_ref, nsum_ref, line)
+    chain = LineRole()
     barrier, count = signal_all(
         [spot(tp=lax.rem(tp + i, groups)) for i in range(1, groups)]
         + [spot(ctx=lax.rem(ctx + i, 4)) for i in range(1, 4)]
@@ -387,7 +400,6 @@
         for k, (src, dst) in enumerate(
             (
                 (out_hbm, out_in), (x_hbm, x_ref), (up_hbm, up_ref), (g_hbm, g_ref),
-                (mixed_hbm, mixed_ref), (conv_hbm, conv_ref), (carried_hbm, carried_ref),
             )
         )
     ]
@@ -398,10 +410,10 @@
         rows = pl.ds(pl.multiple_of(s * SEG, SEG), SEG)
         return pltpu.make_async_copy(src.at[rows], dst.at[rows], s_block.at[k, s])
 
-    blockwise = ((resid_ref, resid_hbm), (dres_ref, dres_hbm), (dconv_ref, dconv_hbm), (dzero_ref, dzero_hbm))
+    blockwise = ((resid_ref, resid_hbm), (npart_ref, npart_hbm), (dpart_ref, dpart_hbm))
     saves = [
         pltpu.make_async_copy(src, dst, s_save.at[k])
-        for k, (src, dst) in enumerate(((dpart_ref, dpart_hbm), (gup_ref, gup_hbm), (gdown_ref, gdown_hbm)))
+        for k, (src, dst) in enumerate(((gup_ref, gup_hbm), (gdown_ref, gdown_hbm)))
     ]
     gall_ref[tp] = gated_ref[...]
     pl.semaphore_wait(barrier, count)
@@ -419,8 +431,8 @@
             out_ref[z, :, columns] = out_in[z, o]
     ob, gain, shift = (ref[...].reshape(1, -1) for ref in (ob_ref, gain_ref, shift_ref))
     ub = ub_ref[...].reshape(1, -1)
-    small_ref[...] = jnp.zeros(small_ref.shape, F32)
-    gskip_ref[...] = jnp.zeros(gskip_ref.shape, F32)
+    for ref in (small_ref, up_acc, down_acc):
+        ref[...] = jnp.zeros(ref.shape, F32)
 
     def core(s, unused):
         rows = pl.ds(pl.multiple_of(s * SEG, SEG), SEG)
@@ -445,10 +457,9 @@
         resid_ref[rows] = residual
         save(0, *blockwise[0], s).start()
         low = (normalize(residual)[0] * gain + shift).astype(BF16)
-        low_ref[rows] = low
         pre = mm(low, up_ref[...]) + ub
         cdf = 0.5 * (1.0 + lax.erf(pre * math.sqrt(0.5)))
-        hidden_ref[rows] = (pre * cdf).astype(BF16)
+        hidden = (pre * cdf).astype(BF16)
         slope = cdf + pre * (jnp.exp(-0.5 * pre * pre) * (1.0 / math.sqrt(2.0 * math.pi)))
 
         @pl.when(s == 0)
@@ -463,71 +474,24 @@
 
         grad = g_ref[rows]
         d_pre = (mm_nt(grad, down_ref[...]) * slope).astype(BF16)
-        dpre_ref[rows] = d_pre
         npart_ref[rows] = mm_nt(d_pre, up_ref[...]).astype(BF16)
+        dpart_ref[rows] = mm(hidden, down_ref[...]).astype(BF16)
+        for k in (1, 2):
+            save(k, *blockwise[k], s).start()
+        up_acc[...] += mm_tn(low, d_pre)
+        down_acc[...] += mm_tn(hidden, grad)
         small_ref[0:1] += jnp.sum(grad.astype(F32), axis=0, keepdims=True)
         small_ref[6:7] += jnp.sum(d_pre.astype(F32), axis=0, keepdims=True)
-        chain.send_block(s)
         return unused
 
     lax.fori_loop(0, blocks, core, 0)
-    chain.steps(0, PER)
-
-    def down(s, unused):
-        rows = pl.ds(pl.multiple_of(s * SEG, SEG), SEG)
-        dpart_ref[rows] = mm(hidden_ref[rows], down_ref[...]).astype(BF16)
-        return unused
-
-    lax.fori_loop(0, blocks, down, 0)
     for t in range(2):
         part = slice(t * width // 2, (t + 1) * width // 2)
-        store_rows(gup_ref, t * width // 2, mm_tn(low_ref[:, part], dpre_ref[...]))
-        units = hidden_ref.shape[1] // 2
-        store_columns(gdown_ref, t, mm_tn(hidden_ref[:, t * units : (t + 1) * units], g_ref[...]))
-
+        store_rows(gup_ref, t * width // 2, up_acc[part])
+        units = down_acc.shape[0] // 2
+        store_columns(gdown_ref, t, down_acc[t * units : (t + 1) * units])
     for job in saves:
         job.start()
-
-    def to_ctx(s, other):
-        return remote(own_ref.at[s], dall_ref.at[ctx * blocks + s], s_long.at[other, s], r_long.at[ctx, s], spot(ctx=other))
-
-    def back(s, unused):
-        chain.steps((s + 1) * PER, (s + 2) * PER)
-        chain.wait_block(s)
-        rows = pl.ds(pl.multiple_of(s * SEG, SEG), SEG)
-        xhat, scale = normalize(resid_ref[rows])
-        dn = nsum_ref[rows].astype(F32)
-        e = dn * gain
-        d_res = g_ref[rows].astype(F32) + scale * (
-            e - jnp.mean(e, axis=-1, keepdims=True) - xhat * jnp.mean(e * xhat, axis=-1, keepdims=True)
-        )
-        dres_ref[rows] = d_res
-        small_ref[2:3] += jnp.sum(dn * xhat, axis=0, keepdims=True)
-        small_ref[3:4] += jnp.sum(dn, axis=0, keepdims=True)
-        d_mix = d_res.astype(BF16)
-        dmix_ref[rows] = d_mix
-        small_ref[1:2] += jnp.sum(d_mix.astype(F32), axis=0, keepdims=True)
-        d_gated = mm_nt(d_mix, out_ref[tp])
-        d_conv = d_gated * mixed_ref[rows]
-        dconv_ref[rows] = d_conv
-        own_ref[s] = d_conv.astype(BF16)
-        for other in range(3):
-            @pl.when(other < ctx)
-            def _():
-                to_ctx(s, other).start()
-
-        dzero_ref[rows] = d_gated * conv_ref[rows]
-        gskip_ref[...] += jnp.sum(d_conv * carried_ref[rows].astype(F32), axis=0, keepdims=True)
-        for k in (1, 2, 3):
-            save(k, *blockwise[k], s).start()
-        return unused
-
-    lax.fori_loop(0, blocks, back, 0)
-    for s in range(blocks):
-        dall_ref[ctx * blocks + s] = own_ref[s]
-    value = mm_tn(gated_ref[...], dmix_ref[...])
-    for t in range(2):
-        store_columns(gout_ref, t, value[t * gout_ref.shape[2] : (t + 1) * gout_ref.shape[2]])
     for i in range(1, owners):
         send_down(i).wait_send()
         swap_down(i).wait_send()
@@ -541,23 +505,11 @@
             for i, source in enumerate((3 - tp, beyond)):
                 gate_pass(s, i, source).wait_send()
 
-    chain.drain()
     for job in saves:
         job.wait()
     for s in range(blocks):
-        for k in range(4):
+        for k in range(3):
             save(k, *blockwise[k], s).wait()
-    for other in range(4):
-        @pl.when(other < ctx)
-        def _():
-            for s in range(blocks):
-                to_ctx(s, other).wait_send()
-
-        @pl.when(other > ctx)
-        def _():
-            for s in range(blocks):
-                at = dall_ref.at[other * blocks + s]
-                remote(at, at, s_long.at[other, s], r_long.at[other, s], chain.mate).wait_recv()
 
 
 def sine_cosine(angle):
@@ -1111,17 +1063,18 @@
 
 
 def back_kernel(
-    par_ref, dall_ref, dconv_ref, dzero_ref, dpart_ref,
+    par_ref, gated_ref, dpart_ref, fgain_ref,
     fh_ref, fl_ref, th_ref, tl_ref, sign_ref, sw_ref, skip_ref,
-    ft_ref, f1_ref, f1b_ref, f2_ref, f2b_ref, freq_ref, last_ref, small_ref, gskip_ref,
-    mixed_hbm, low_hbm, w_hbm, x_hbm, proj_hbm, head_hbm, spec_hbm, filt_hbm, net_hbm, sup_hbm, sdown_hbm, sout_hbm,
-    dsum_ref, psum_ref, oup_ref, odown_ref, oout_ref, oin_ref, va_ref, vd_ref, vl_ref, vf_ref,
+    ft_ref, f1_ref, f1b_ref, f2_ref, f2b_ref, freq_ref, last_ref, small_ref,
+    npart_hbm, resid_hbm, g_hbm, gate_hbm, conv_hbm, carried_hbm, out_hbm,
+    mixed_hbm, low_hbm, w_hbm, x_hbm, proj_hbm, head_hbm, spec_hbm, filt_hbm, net_hbm, sup_hbm, sdown_hbm,
+    dres_hbm, dsum_ref, psum_ref, oup_ref, odown_ref, oout_ref, oin_ref, va_ref, vd_ref, vl_ref, vf_ref,
+    dall_ref, dconv_ref, dzero_ref, stage_out, s_long, r_long,
     yown_ref, dcar_ref, dtaps_ref, stage_in, ppart_ref, w1_ref, w2_ref,
-    mixed_ref, low_ref, w_ref, x_ref, hd_ref, s_hd, r_hd, local, *rest,
+    mixed_ref, hd_ref, s_hd, r_hd, local, *rest,
 ):
-    width = x_ref.shape[1]
+    total_rows, width = ppart_ref.shape
     channels = dconv_ref.shape[1]
-    total_rows = x_ref.shape[0]
     blocks = total_rows // SEG
     owners = sup_hbm.shape[1]
     ctx, tp, dp = lax.axis_index("ctx"), lax.axis_index("tp"), lax.axis_index("dp")
@@ -1134,7 +1087,7 @@
 
     down = LineSum(dpart_ref, dsum_ref, take(11))
     proj = LineSum(ppart_ref, psum_ref, take(11))
-    early = [OwnerSum(s, o, take(16)) for s, o in ((sup_hbm, oup_ref), (sdown_hbm, odown_ref), (sout_hbm, oout_ref))]
+    early = [OwnerSum(s, o, take(16)) for s, o in ((sup_hbm, oup_ref), (sdown_hbm, odown_ref), (stage_out, oout_ref))]
     late = OwnerSum(stage_in, oin_ref, take(16))
     a_ctx, a_dp = SmallSum("ctx", take(3)), SmallSum("dp", take(3))
     d_ctx, d_dp, d_tp = SmallSum("ctx", take(3)), SmallSum("dp", take(3)), SmallSum("tp", take(3))
@@ -1145,17 +1098,18 @@
     partners += [spot(ctx=lax.rem(ctx + i, 4)) for i in range(1, 4)]
     partners += [spot(dp=lax.rem(dp + i, owners)) for i in range(1, owners)]
     barrier, count = signal_all(partners)
+    load_part = pltpu.make_async_copy(npart_hbm, ppart_ref, local.at[10])
+    load_mixed = pltpu.make_async_copy(mixed_hbm, mixed_ref, local.at[11])
+    load_part.start()
+    load_part.wait()
     pl.semaphore_wait(barrier, count)
     for s in range(blocks):
-        down.send_block(s)
-    loads = [
-        pltpu.make_async_copy(src, dst, local.at[4 + k])
-        for k, (src, dst) in enumerate(((mixed_hbm, mixed_ref), (w_hbm, w_ref), (x_hbm, x_ref), (low_hbm, low_ref)))
-    ]
-    for load in loads:
-        load.start()
-    for job in early:
+        proj.send_block(s)
+    load_mixed.start()
+    for job in early[:2]:
         job.begin()
+    va_ref[...] = jnp.zeros(va_ref.shape, F32)
+    vd_ref[...] = small_ref[...]
     fh, fl, th, tl = fh_ref[...], fl_ref[...], th_ref, tl_ref
     skip = skip_ref[...].reshape(1, -1)
     scale = 1.0 / SEG
@@ -1164,17 +1118,148 @@
         dst[0] = value[:SEG] * scale
         dst[1] = value[SEG:] * scale
 
+    def half_rows(h):
+        return pl.ds(pl.multiple_of(h * HALF, HALF), HALF)
+
+    def half_of(who, h):
+        return dall_ref.at[who * blocks + h // 2, half_rows(lax.rem(h, 2))]
+
+    def long_to(h, other):
+        at = half_of(ctx, h)
+        return remote(at, at, s_long.at[other, h], r_long.at[ctx, h], spot(ctx=other))
+
+    def long_from(other):
+        def one(h, unused):
+            at = half_of(other, h)
+            remote(at, at, s_long.at[other, h], r_long.at[other, h], spot(ctx=lax.rem(ctx + 1, 4))).wait_recv()
+            return unused
+
+        lax.fori_loop(0, 2 * blocks, one, 0)
+
+    def feed_back(in_ref, g_ref, dres_ref, gate_ref, conv_ref, carried_ref, parts_ref, out_ref, gout_ref):
+        once = [
+            pltpu.make_async_copy(src, dst, local.at[k])
+            for k, (src, dst) in enumerate(
+                ((gate_hbm, gate_ref), (conv_hbm, conv_ref), (carried_hbm, carried_ref), (out_hbm.at[tp], parts_ref))
+            )
+        ]
+        for load in once:
+            load.start()
+
+        def fetch(h):
+            slot = lax.rem(h, 2)
+            return (
+                pltpu.make_async_copy(resid_hbm.at[half_rows(h)], in_ref.at[slot], local.at[4 + slot]),
+                pltpu.make_async_copy(g_hbm.at[half_rows(h)], g_ref.at[slot], local.at[6 + slot]),
+            )
+
+        def save(h):
+            slot = lax.rem(h, 2)
+            return pltpu.make_async_copy(dres_ref.at[slot], dres_hbm.at[half_rows(h)], local.at[8 + slot])
+
+        for load in fetch(0):
+            load.start()
+        for load in once:
+            load.wait()
+        share = width // owners
+        for o in range(owners):
+            out_ref[:, o * share : (o + 1) * share] = parts_ref[o]
+        gout_ref[...] = jnp.zeros(gout_ref.shape, F32)
+        gain = fgain_ref[...].reshape(1, -1)
+        proj.steps(0, PER)
+
+        def one(h, unused):
+            rows = half_rows(h)
+            slot = lax.rem(h, 2)
+            for load in fetch(h):
+                load.wait()
+
+            @pl.when(h + 1 < 2 * blocks)
+            def _():
+                for load in fetch(h + 1):
+                    load.start()
+
+            xhat, spread = normalize(in_ref[slot])
+            proj.steps(PER + h * PER // 2, PER + (h + 1) * PER // 2)
+            proj.wait_half(h)
+
+            @pl.when(h == 1)
+            def _():
+                for job in early[:2]:
+                    job.pair()
+
+            @pl.when(h == 2 * blocks - 3)
+            def _():
+                for b in range(blocks):
+                    down.send_block(b)
+
+            dn = psum_ref[rows].astype(F32)
+            e = dn * gain
+            d_res = g_ref[slot].astype(F32) + spread * (
+                e - jnp.mean(e, axis=-1, keepdims=True) - xhat * jnp.mean(e * xhat, axis=-1, keepdims=True)
+            )
+            d_mix = d_res.astype(BF16)
+            d_gated = mm_nt(d_mix, out_ref[...])
+            d_conv = d_gated * gate_ref[rows]
+            dall_ref[ctx * blocks + h // 2, half_rows(lax.rem(h, 2))] = d_conv.astype(BF16)
+            for other in range(2):
+                @pl.when(other < ctx)
+                def _():
+                    long_to(h, other).start()
+
+            @pl.when(h >= 2)
+            def _():
+                save(h - 2).wait()
+
+            dres_ref[slot] = d_res
+            save(h).start()
+            dconv_ref[rows] = d_conv
+            dzero_ref[rows] = d_gated * conv_ref[rows]
+
+            @pl.when(lax.rem(h, 2) == 1)
+            def _():
+                part = dall_ref[ctx * blocks + h // 2]
+                put(yown_ref.at[h // 2], mm(fh, part) + mm(fl, part))
+
+            vd_ref[2:3] += jnp.sum(dn * xhat, axis=0, keepdims=True)
+            vd_ref[3:4] += jnp.sum(dn, axis=0, keepdims=True)
+            vd_ref[1:2] += jnp.sum(d_mix.astype(F32), axis=0, keepdims=True)
+            va_ref[15:16] += jnp.sum(d_conv * carried_ref[rows].astype(F32), axis=0, keepdims=True)
+            gout_ref[...] += mm_tn(gated_ref[rows], d_mix)
+            return unused
+
+        lax.fori_loop(0, 2 * blocks, one, 0)
+        half = stage_out.shape[2]
+        for t in range(2):
+            store_columns(stage_out, t, gout_ref[t * half : (t + 1) * half])
+        save(2 * blocks - 2).wait()
+        save(2 * blocks - 1).wait()
+
+    pl.run_scoped(
+        feed_back,
+        pltpu.VMEM((2, HALF, width), F32),
+        pltpu.VMEM((2, HALF, width), BF16),
+        pltpu.VMEM((2, HALF, width), F32),
+        pltpu.VMEM((total_rows, channels), F32),
+        pltpu.VMEM((total_rows, channels), F32),
+        pltpu.VMEM((total_rows, channels), BF16),
+        pltpu.VMEM((owners, channels, width // owners), BF16),
+        pltpu.VMEM((channels, width), BF16),
+        pltpu.VMEM((channels, width), F32),
+    )
+    early[2].begin()
+    down.steps(0, 3)
+
+    def to_ctx(i):
+        at = hd_ref.at[pl.ds(ctx * blocks, blocks)]
+        return remote(at, at, s_hd.at[i], r_hd.at[ctx], spot(ctx=lax.rem(ctx + i, 4)))
+
     def conv_inputs(filt_ref, more_ref, acc_ref):
         load = pltpu.make_async_copy(filt_hbm, filt_ref, local.at[0])
         load.start()
 
-        def transform(s, unused):
-            part = dall_ref[ctx * blocks + s]
-            put(yown_ref.at[s], mm(fh, part) + mm(fl, part))
-            return unused
-
-        lax.fori_loop(0, blocks, transform, 0)
         load.wait()
+        load_mixed.wait()
 
         def leaf_sum(match):
             total = None
@@ -1187,12 +1272,13 @@
             return lambda leaf: par_ref[0, leaf] == b
 
         def finish(s, terms):
-            blend_all(acc_ref, terms, True)
-            place = pl.ds(pl.multiple_of(s * SEG, SEG), SEG)
-            dcar_ref[place] = unpack_spectrum(th, tl, acc_ref) + skip * dconv_ref[place]
+            blend_all(acc_ref.at[s], terms, True)
 
         @pl.when(ctx == 0)
         def _():
+            for other in (1, 2, 3):
+                long_from(other)
+
             def gather(k, unused):
                 p = k + 1
                 total = None
@@ -1214,6 +1300,9 @@
 
         @pl.when(ctx == 1)
         def _():
+            for other in (2, 3):
+                long_from(other)
+
             def one(b, unused):
                 put(more_ref.at[0], mm_split(fh, fl, leaf_sum(from_leaf(b + 4))))
                 finish(b, [(filt_ref.at[0], yown_ref.at[b]), (filt_ref.at[1], more_ref.at[0])])
@@ -1229,43 +1318,44 @@
 
             lax.fori_loop(0, 4, one, 0)
 
-    pl.run_scoped(
-        conv_inputs,
-        pltpu.VMEM((DEPTH, 2, SEG, channels), F32),
-        pltpu.VMEM((6, 2, SEG, channels), F32),
-        pltpu.VMEM((2, SEG, channels), F32),
-    )
-
-    for load in loads:
-        load.wait()
-
-    def to_ctx(i):
-        at = hd_ref.at[pl.ds(ctx * blocks, blocks)]
-        return remote(at, at, s_hd.at[i], r_hd.at[ctx], spot(ctx=lax.rem(ctx + i, 4)))
-
-    for s in range(blocks):
-        top = slice(s * SEG, s * SEG + HEADS)
-        d_car = dcar_ref[top]
-        rows = [dzero_ref[top], d_car * mixed_ref[1, top], d_car * mixed_ref[0, top]]
-        for g in range(3):
-            hd_ref[ctx * blocks + s, 2 * g : 2 * g + 2] = rows[g][0:2]
-        hd_ref[ctx * blocks + s, 6:8] = jnp.zeros((2, channels), F32)
-    for i in range(1, 4):
-        to_ctx(i).start()
-    down.steps(0, 4)
-    for job in early:
-        job.pair()
-
-    va_ref[...] = jnp.zeros(va_ref.shape, F32)
-    vd_ref[...] = small_ref[...]
-    va_ref[15:16] = gskip_ref[...]
-    for i in range(1, 4):
-        other = lax.rem(ctx + i, 4)
-        at = hd_ref.at[pl.ds(other * blocks, blocks)]
-        remote(at, at, s_hd.at[i], r_hd.at[other], spot(ctx=other)).wait_recv()
-
-    def with_spectra(spec_ref):
-        pltpu.make_async_copy(spec_hbm, spec_ref, local.at[0]).start()
+        down.steps(3, 5)
+        for s in range(blocks):
+            top = slice(s * SEG, s * SEG + HEADS)
+            d_car = unpack_spectrum(th.at[0:16], tl.at[0:16], acc_ref.at[s])[0:HEADS] + skip * dconv_ref[top]
+            rows = [dzero_ref[top], d_car * mixed_ref[1, top], d_car * mixed_ref[0, top]]
+            for g in range(3):
+                hd_ref[ctx * blocks + s, 2 * g : 2 * g + 2] = rows[g][0:2]
+            hd_ref[ctx * blocks + s, 6:8] = jnp.zeros((2, channels), F32)
+        for i in range(1, 4):
+            to_ctx(i).start()
+
+        def whole(s, unused):
+            place = pl.ds(pl.multiple_of(s * SEG, SEG), SEG)
+            dcar_ref[place] = unpack_spectrum(th, tl, acc_ref.at[s]) + skip * dconv_ref[place]
+            return unused
+
+        lax.fori_loop(0, blocks, whole, 0)
+
+    def mix_stage(low_ref, w_ref, x_ref):
+        loads = [
+            pltpu.make_async_copy(src, dst, local.at[4 + k])
+            for k, (src, dst) in enumerate(((w_hbm, w_ref), (x_hbm, x_ref), (low_hbm, low_ref)))
+        ]
+        for load in loads:
+            load.start()
+        pl.run_scoped(
+            conv_inputs,
+            pltpu.VMEM((DEPTH, 2, SEG, channels), F32),
+            pltpu.VMEM((6, 2, SEG, channels), F32),
+            pltpu.VMEM((blocks, 2, SEG, channels), F32),
+        )
+
+        down.steps(5, 7)
+        proj.drain()
+        for i in range(1, 4):
+            other = lax.rem(ctx + i, 4)
+            at = hd_ref.at[pl.ds(other * blocks, blocks)]
+            remote(at, at, s_hd.at[i], r_hd.at[other], spot(ctx=other)).wait_recv()
 
         def mix_back(dp_ref, ext_ref, dm_ref, pin_ref, hin_ref):
             load_heads = pltpu.make_async_copy(head_hbm, hin_ref, local.at[1])
@@ -1277,6 +1367,8 @@
 
             fetch(0).start()
             load_heads.wait()
+            for load in loads:
+                load.wait()
 
             def one(s, unused):
                 rows = pl.ds(pl.multiple_of(s * SEG, SEG), SEG)
@@ -1320,7 +1412,7 @@
                 xhat = normalize(x_ref[rows].astype(F32))[0]
                 vd_ref[4:5] += jnp.sum(part * xhat, axis=0, keepdims=True)
                 vd_ref[5:6] += jnp.sum(part, axis=0, keepdims=True)
-                down.steps(4 + s, 5 + s)
+                down.steps(7 + s, 8 + s)
                 return unused
 
             lax.fori_loop(0, blocks, one, 0)
@@ -1338,13 +1430,26 @@
             pltpu.VMEM((2, 3, SEG, channels), F32),
             pltpu.VMEM((3, blocks, HEADS, channels), F32),
         )
-        a_ctx.start(va_ref[...])
-        d_ctx.start(vd_ref[...])
-        late.begin()
-        down.steps(8, 11)
+    pl.run_scoped(
+        mix_stage,
+        pltpu.VMEM((total_rows, width), BF16),
+        pltpu.VMEM((3, channels, width), BF16),
+        pltpu.VMEM((total_rows, width), BF16),
+    )
+    a_ctx.start(va_ref[...])
+    d_ctx.start(vd_ref[...])
+    late.begin()
+    early[2].pair()
+    for job in early[:2]:
+        job.own()
+
+    def with_spectra(spec_ref):
+        load_spectra = pltpu.make_async_copy(spec_hbm, spec_ref, local.at[0])
+        load_spectra.start()
+        down.steps(11, 13)
 
         def conv_filters(dfilt_ref):
-            pltpu.make_async_copy(spec_hbm, spec_ref, local.at[0]).wait()
+            load_spectra.wait()
 
             @pl.when(ctx == 0)
             def _():
@@ -1362,7 +1467,7 @@
                     terms = [(spec_ref.at[places[s][d]], yown_ref.at[s]) for s in range(blocks)]
                     blend_all(dfilt_ref.at[d], terms, True)
 
-            down.steps(11, 12)
+            down.steps(13, 14)
             sign = sign_ref[...]
             first_row = lax.broadcasted_iota(jnp.int32, (SEG, 1), 0) == 0
             for j in range(DEPTH):
@@ -1380,7 +1485,7 @@
         pl.run_scoped(conv_filters, pltpu.VMEM((DEPTH, 2, SEG, channels), F32))
 
     pl.run_scoped(with_spectra, pltpu.VMEM((13, 2, SEG, channels), F32))
-    down.steps(12, 13)
+    down.steps(14, 16)
 
     def filter_back(net_ref):
         load = pltpu.make_async_copy(net_hbm, net_ref, local.at[1])
@@ -1407,13 +1512,17 @@
 
     pl.run_scoped(filter_back, pltpu.VMEM(net_hbm.shape, F32))
 
-    def early_own():
-        for job in early:
-            job.own()
-
-    def early_cross():
-        for job in early:
+    def first_cross():
+        for job in early[:2]:
             job.cross()
+
+    def second_own():
+        early[2].own()
+        late.pair()
+
+    def second_cross():
+        early[2].cross()
+        late.own()
 
     def vectors():
         a_dp.start(a_ctx.total())
@@ -1422,7 +1531,6 @@
     def networks():
         l_dp.start(l_ctx.total())
         f_dp.start(f_ctx.total())
-        late.own()
 
     def gains():
         va_ref[...] = a_dp.total()
@@ -1431,7 +1539,7 @@
         d_tp.start(sums[4:6])
 
     def last_layer():
-        for job in early:
+        for job in early[:2]:
             job.whole()
         f_tp.start(f_dp.total())
         last_sum = l_dp.total()
@@ -1439,13 +1547,14 @@
             held = vl_ref.shape[1]
             vl_ref[o] = last_sum[o * held : (o + 1) * held]
 
-    jobs = (early_own, late.pair, early_cross, vectors, networks, gains, last_layer)
+    jobs = (second_own, vectors, networks, first_cross, second_cross, gains, last_layer)
     for k, job in enumerate(jobs):
-        down.steps(13 + k, 14 + k)
+        down.steps(min(16 + k, 20), min(17 + k, 20))
         proj.steps(2 * k, 2 * k + 2)
         job()
     proj.steps(14, 17)
     late.cross()
+    early[2].whole()
     proj.steps(17, proj.pairs + 2 * LAG)
     late.whole()
     for s in range(blocks):
@@ -1459,6 +1568,12 @@
         job.finish()
     for i in range(1, 4):
         to_ctx(i).wait_send()
+    for other in range(2):
+        @pl.when(other < ctx)
+        def _():
+            for h in range(2 * blocks):
+                long_to(h, other).wait_send()
+
     down.drain()
     proj.drain()
 
@@ -1592,51 +1707,42 @@
     feed_big = [
         sds((total_rows, width), F32),
         sds((total_rows, width), BF16),
-        sds((total_rows, width), F32),
-        sds((total_rows, channels), F32),
-        sds((total_rows, channels), F32),
+        sds((total_rows, width), BF16),
         sds((2, owners, piece, hidden), BF16),
         sds((2, owners, half, share), BF16),
     ]
-    feed_in = (out_all, x, g, up_all, gate, conv, carried)
+    feed_in = (out_all, x, g, up_all)
 
     def held(v):
         return pltpu.VMEM(v.shape, v.dtype)
 
-    residual, down_part, d_res, d_conv, d_zero, stage_up, stage_down, d_all, stage_out, small, grad_skip = call(
+    residual, norm_part, down_part, stage_up, stage_down, small = call(
         feed_kernel,
-        feed_big
-        + [
-            sds((all_blocks, SEG, channels), BF16),
-            sds((2, owners, channels // 2, share), BF16),
-            sds((8, width), F32),
-            sds((1, channels), F32),
-        ],
-        [VM] * 6 + [HB] * 7,
+        feed_big + [sds((8, width), F32)],
+        [VM] * 6 + [HB] * 4,
         [held(v) for v in feed_in]
         + [held(v) for v in feed_big]
-        + [dma((8,)), dma((3,)), dma((4, blocks)), pltpu.VMEM((owners, hidden, share), BF16)]
+        + [dma((4,)), dma((2,)), dma((3, blocks)), pltpu.VMEM((owners, hidden, share), BF16)]
         + [dma((2, owners)), dma((2, owners))]
         + [
-            pltpu.VMEM((total_rows, width), BF16),
-            pltpu.VMEM((total_rows, hidden), BF16),
-            pltpu.VMEM((total_rows, hidden), BF16),
-            pltpu.VMEM((total_rows, width), BF16),
-            pltpu.VMEM((total_rows, width), BF16),
-            pltpu.VMEM((total_rows, width), BF16),
-            pltpu.VMEM((blocks, SEG, channels), BF16),
+            pltpu.VMEM((width, hidden), F32),
+            pltpu.VMEM((hidden, width), F32),
             pltpu.VMEM((tp_count, total_rows, channels), BF16),
             pltpu.VMEM((tp_count, channels, width), BF16),
             pltpu.VMEM((hidden, width), BF16),
-            dma((tp_count, blocks)), dma((tp_count, blocks)), dma((4, blocks)), dma((4, blocks)),
-        ]
-        + LineSum.scratch(total_rows, width),
+            dma((tp_count, blocks)), dma((tp_count, blocks)),
+        ],
         2,
-        out_specs=(HB,) * 7 + (VM,) * 4,
+        out_specs=(HB,) * 5 + (VM,),
     )(gated, out_bias, feed_gain, feed_shift, feed_up_bias, feed_down, *feed_in)
 
     shapes = [(piece, hidden), (half, share), (channels // 2, share), (3, channels // 2, share)]
     scratch = [
+        pltpu.VMEM((all_blocks, SEG, channels), BF16),
+        pltpu.VMEM((total_rows, channels), F32),
+        pltpu.VMEM((total_rows, channels), F32),
+        pltpu.VMEM((2, owners) + shapes[2], BF16),
+        dma((4, 2 * blocks)), dma((4, 2 * blocks)),
         pltpu.VMEM((blocks, 2, SEG, channels), F32),
         pltpu.VMEM((total_rows, channels), F32),
         pltpu.VMEM((length, channels), F32),
@@ -1644,9 +1750,9 @@
         pltpu.VMEM((total_rows, width), BF16),
         pltpu.VMEM((feat_rows, units), F32),
         pltpu.VMEM((mid_rows, units), F32),
-        held(mixed), held(low), held(in_all), held(x),
+        held(mixed),
         pltpu.VMEM((all_blocks, HEADS, channels), F32),
-        dma((4,)), dma((4,)), dma((8,)),
+        dma((4,)), dma((4,)), dma((12,)),
     ]
     scratch += LineSum.scratch(total_rows, width) * 2
     for shape in shapes:
@@ -1658,9 +1764,10 @@
     ):
         for count in counts:
             scratch += SmallSum.scratch(count, shape)
-    down_sum, proj_sum, own_up, own_down, own_out, own_in, va, vd, vl, vf = call(
+    d_res, down_sum, proj_sum, own_up, own_down, own_out, own_in, va, vd, vl, vf = call(
         back_kernel,
         (
+            sds((total_rows, width), F32),
             sds((total_rows, width), BF16),
             sds((total_rows, width), BF16),
         )
@@ -1671,14 +1778,14 @@
             sds((owners,) + filter_out.shape, F32),
             sds(smalls[3], F32),
         ),
-        [SM] + [VM] * 20 + [HB] * 12,
+        [SM] + [VM] * 18 + [HB] * 18,
         scratch,
         3,
-        out_specs=(VM, VM, HB, HB, HB, HB, VM, VM, VM, VM),
+        out_specs=(HB, VM, VM, HB, HB, HB, HB, VM, VM, VM, VM),
     )(
-        parents, d_all, d_conv, d_zero, down_part, fh, fl, th, tl, sign, short_weight,
-        skip_gain, ft, filter_one, filter_one_bias, filter_two, filter_two_bias, filter_freq, last, small, grad_skip,
-        mixed, low, in_all, x, proj, head, spec, filt, net, stage_up, stage_down, stage_out,
+        parents, gated, down_part, feed_gain, fh, fl, th, tl, sign, short_weight,
+        skip_gain, ft, filter_one, filter_one_bias, filter_two, filter_two_bias, filter_freq, last, small,
+        norm_part, residual, g, gate, conv, carried, out_all, mixed, low, in_all, x, proj, head, spec, filt, net, stage_up, stage_down,
     )
 
     def by_block(*shape):

time: 254 us -> 247 us (0.972)
  Pallas kernels: 253 us -> 246 us
    pallas_call x2, Pallas kernels: 202 us -> 195 us  [the longest x1 146 us: body(): call(back_kernel, (sds((total_rows, width), F32), sds((total_rows, width)...]
where the time goes in v6:
time: 247 us
  Pallas kernels  246 us (100%)
    pallas_call x1, Pallas kernels, body(): call(back_kernel, (sds((total_rows, width), F32), sds((total_rows, width)...  146 us
    pallas_call x1, Pallas kernels, body(): call(feed_kernel, feed_big + [sds((8, width), F32)], [VM] * 6 + [HB] * 4,...  48.4 us
    pallas_call x1, Pallas kernels, body(): call(front_kernel, front_out, [SM] + [VM] * 22, [pltpu.VMEM((3, channels,...  41.1 us
    pallas_call x1, Pallas kernels, body(): pl.pallas_call(final_kernel, grid=(blocks,), out_shape=[sds((total_rows,...  10.2 us

profile of v6, /device:TPU:0, one launch (start us, length us, event | category | flops | bytes accessed | tf_op | source)
XLA Modules:
  0.0 246.8 jit_solution(7324052668179659952)
XLA Ops:
  0.7 41.1 %shard_map.461 = (bf16[1024,768]{1,0:T(8,128)(2,1)}, f32[3,1024,192]{2,1,0:T(8,128)}, f32[3,4,8,192]{3,2,1,0:T(8,128)}, f32[2,1024,192]{2,1,0:T(8,128)}, f32[13,...) custom-call(s32[1,16]{1,0:T(1,128)} %par_ref.3, ...), custom_call_target="tpu_custom_call" | custom-call | tf_op jit(solution)/shard_map/pallas_call | solution.py:1669
  41.8 48.4 %shard_map.462 = (f32[1024,768]{1,0:T(8,128)}, bf16[1024,768]{1,0:T(8,128)(2,1)}, bf16[1024,768]{1,0:T(8,128)(2,1)}, bf16[2,2,192,768]{3,2,1,0:T(8,128)(2,1)}, b...) custom-call(bf16[1024,192]{1,0:T(8,128)(2,1)} %get-tuple-element.78.gated_ref, f32[768]{0:T(1024)} %ob_ref.1, ...), custom_call_target="tpu_custom_call" | custom-call | tf_op jit(solution)/shard_map/pallas_call | solution.py:1719
  90.2 146.2 %shard_map.463 = (f32[1024,768]{1,0:T(8,128)}, bf16[1024,768]{1,0:T(8,128)(2,1)}, bf16[1024,768]{1,0:T(8,128)(2,1)}, f32[2,192,768]{2,1,0:T(8,128)}, f32[2,384,3...) custom-call(s32[1,16]{1,0:T(1,128)} %par_ref.3, ...), custom_call_target="tpu_custom_call" | custom-call | tf_op jit(solution)/shard_map/pallas_call | solution.py:1767
  236.4 10.2 %shard_map.464 = (f32[1024,768]{1,0:T(8,128)}, f32[1024,768]{1,0:T(8,128)}, f32[2,192,768]{2,1,0:T(8,128)}, f32[2,384,384]{2,1,0:T(8,128)}, f32[2,96,384]{2,1,0:...) custom-call(f32[1024,768]{1,0:T(8,128)} %get-tuple-element.81.resid_, ...), custom_call_target="tpu_custom_call" | custom-call | tf_op jit(solution)/shard_map/pallas_call | solution.py:1806

commit v7 on v6

--- a/solution.py
+++ b/solution.py
@@ -1789,7 +1789,7 @@
     )
 
     def by_block(*shape):
-        return pl.BlockSpec((SEG,) + shape, lambda i: (i,) + (0,) * len(shape))
+        return pl.BlockSpec((2 * SEG,) + shape, lambda i: (i,) + (0,) * len(shape))
 
     def whole(v):
         return pl.BlockSpec(v.shape, lambda i: (0,) * len(v.shape))
@@ -1805,7 +1805,7 @@
     ]
     out = pl.pallas_call(
         final_kernel,
-        grid=(blocks,),
+        grid=(blocks // 2,),
         out_shape=[
             sds((total_rows, width), F32), sds((total_rows, width), F32), own_up, own_down, own_out,
             sds((3, channels, share), F32),

time: 247 us -> 246 us (level)
  no operation moved by 1% of the time
where the time goes in v7:
time: 246 us
  Pallas kernels  245 us (100%)
    pallas_call x1, Pallas kernels, body(): call(back_kernel, (sds((total_rows, width), F32), sds((total_rows, width)...  146 us
    pallas_call x1, Pallas kernels, body(): call(feed_kernel, feed_big + [sds((8, width), F32)], [VM] * 6 + [HB] * 4,...  48.4 us
    pallas_call x1, Pallas kernels, body(): call(front_kernel, front_out, [SM] + [VM] * 22, [pltpu.VMEM((3, channels,...  41.1 us
    pallas_call x1, Pallas kernels, body(): pl.pallas_call(final_kernel, grid=(blocks // 2,), out_shape=[sds((total_r...  9.38 us

profile of v7, /device:TPU:0, one launch (start us, length us, event | category | flops | bytes accessed | tf_op | source)
XLA Modules:
  0.0 246.0 jit_solution(1320285126259420641)
XLA Ops:
  0.7 41.1 %shard_map.461 = (bf16[1024,768]{1,0:T(8,128)(2,1)}, f32[3,1024,192]{2,1,0:T(8,128)}, f32[3,4,8,192]{3,2,1,0:T(8,128)}, f32[2,1024,192]{2,1,0:T(8,128)}, f32[13,...) custom-call(s32[1,16]{1,0:T(1,128)} %par_ref.3, ...), custom_call_target="tpu_custom_call" | custom-call | tf_op jit(solution)/shard_map/pallas_call | solution.py:1669
  41.8 48.4 %shard_map.462 = (f32[1024,768]{1,0:T(8,128)}, bf16[1024,768]{1,0:T(8,128)(2,1)}, bf16[1024,768]{1,0:T(8,128)(2,1)}, bf16[2,2,192,768]{3,2,1,0:T(8,128)(2,1)}, b...) custom-call(bf16[1024,192]{1,0:T(8,128)(2,1)} %get-tuple-element.78.gated_ref, f32[768]{0:T(1024)} %ob_ref.1, ...), custom_call_target="tpu_custom_call" | custom-call | tf_op jit(solution)/shard_map/pallas_call | solution.py:1719
  90.2 146.2 %shard_map.463 = (f32[1024,768]{1,0:T(8,128)}, bf16[1024,768]{1,0:T(8,128)(2,1)}, bf16[1024,768]{1,0:T(8,128)(2,1)}, f32[2,192,768]{2,1,0:T(8,128)}, f32[2,384,3...) custom-call(s32[1,16]{1,0:T(1,128)} %par_ref.3, ...), custom_call_target="tpu_custom_call" | custom-call | tf_op jit(solution)/shard_map/pallas_call | solution.py:1767
  236.4 9.4 %shard_map.464 = (f32[1024,768]{1,0:T(8,128)}, f32[1024,768]{1,0:T(8,128)}, f32[2,192,768]{2,1,0:T(8,128)}, f32[2,384,384]{2,1,0:T(8,128)}, f32[2,96,384]{2,1,0:...) custom-call(f32[1024,768]{1,0:T(8,128)} %get-tuple-element.81.resid_, ...), custom_call_target="tpu_custom_call" | custom-call | tf_op jit(solution)/shard_map/pallas_call | solution.py:1806

commit v8 on v7

--- a/solution.py
+++ b/solution.py
@@ -235,8 +235,7 @@
         @pl.when(k < pairs)
         def _():
             other = 2 * k + 1 - side
-            self.to_mid(2 * k).wait_recv()
-            self.to_mid(2 * k + 1).wait_recv()
+            self.to_mid(other).wait_recv()
             self.out[chunk(k)] = (
                 self.part[chunk(other)].astype(F32) + self.end[chunk(other)].astype(F32)
             ).astype(BF16)
@@ -247,6 +246,7 @@
         @pl.when(jnp.logical_and(j >= 0, j < pairs))
         def _():
             mine = 2 * j + side
+            self.to_mid(mine).wait_recv()
             self.to_cross(j).wait_recv()
             self.total[chunk(mine)] = (
                 self.part[chunk(mine)].astype(F32)

time: 246 us -> 246 us (level)
  no operation moved by 1% of the time
where the time goes in v8:
time: 246 us
  Pallas kernels  245 us (100%)
    pallas_call x1, Pallas kernels, body(): call(back_kernel, (sds((total_rows, width), F32), sds((total_rows, width)...  146 us
    pallas_call x1, Pallas kernels, body(): call(feed_kernel, feed_big + [sds((8, width), F32)], [VM] * 6 + [HB] * 4,...  48.4 us
    pallas_call x1, Pallas kernels, body(): call(front_kernel, front_out, [SM] + [VM] * 22, [pltpu.VMEM((3, channels,...  41.1 us
    pallas_call x1, Pallas kernels, body(): pl.pallas_call(final_kernel, grid=(blocks // 2,), out_shape=[sds((total_r...  9.38 us

profile of v8, /device:TPU:0, one launch (start us, length us, event | category | flops | bytes accessed | tf_op | source)
XLA Modules:
  0.0 245.7 jit_solution(7074347467318708619)
XLA Ops:
  0.7 41.1 %shard_map.461 = (bf16[1024,768]{1,0:T(8,128)(2,1)}, f32[3,1024,192]{2,1,0:T(8,128)}, f32[3,4,8,192]{3,2,1,0:T(8,128)}, f32[2,1024,192]{2,1,0:T(8,128)}, f32[13,...) custom-call(s32[1,16]{1,0:T(1,128)} %par_ref.3, ...), custom_call_target="tpu_custom_call" | custom-call | tf_op jit(solution)/shard_map/pallas_call | solution.py:1669
  41.8 48.4 %shard_map.462 = (f32[1024,768]{1,0:T(8,128)}, bf16[1024,768]{1,0:T(8,128)(2,1)}, bf16[1024,768]{1,0:T(8,128)(2,1)}, bf16[2,2,192,768]{3,2,1,0:T(8,128)(2,1)}, b...) custom-call(bf16[1024,192]{1,0:T(8,128)(2,1)} %get-tuple-element.78.gated_ref, f32[768]{0:T(1024)} %ob_ref.1, ...), custom_call_target="tpu_custom_call" | custom-call | tf_op jit(solution)/shard_map/pallas_call | solution.py:1719
  90.2 146.0 %shard_map.463 = (f32[1024,768]{1,0:T(8,128)}, bf16[1024,768]{1,0:T(8,128)(2,1)}, bf16[1024,768]{1,0:T(8,128)(2,1)}, f32[2,192,768]{2,1,0:T(8,128)}, f32[2,384,3...) custom-call(s32[1,16]{1,0:T(1,128)} %par_ref.3, ...), custom_call_target="tpu_custom_call" | custom-call | tf_op jit(solution)/shard_map/pallas_call | solution.py:1767
  236.1 9.4 %shard_map.464 = (f32[1024,768]{1,0:T(8,128)}, f32[1024,768]{1,0:T(8,128)}, f32[2,192,768]{2,1,0:T(8,128)}, f32[2,384,384]{2,1,0:T(8,128)}, f32[2,96,384]{2,1,0:...) custom-call(f32[1024,768]{1,0:T(8,128)} %get-tuple-element.81.resid_, ...), custom_call_target="tpu_custom_call" | custom-call | tf_op jit(solution)/shard_map/pallas_call | solution.py:1806
